TPU v7x, 32 devices: a whole 2x2x4 slice. The times are simulated.
32 devices in a mesh: fsdp: 32 (over z, y, x, core).
Axes of the slice: x: 2, y: 2, z: 4, core: 2. Of those that a mesh axis runs over, the one named last changes fastest.
Arguments:
- tokens: bfloat16 [8192, 1024], P('fsdp'), may hold values from -6 to 6
- lengths: int32 [4], replicated, may hold values from 1 to 4096, 8192 in all
- seq_order: int32 [4], replicated, may hold values from 0 to 3, each once
- decay_rate: float32 [8], replicated, may hold values from 7.324219e-05 to 0.025
- w_query: bfloat16 [1024, 1024], P('fsdp'), may hold values from -0.1875 to 0.1875
- w_key: bfloat16 [1024, 1024], P('fsdp'), may hold values from -0.1875 to 0.1875
- w_value: bfloat16 [1024, 1024], P('fsdp'), may hold values from -0.1875 to 0.1875
- w_unit: bfloat16 [1024, 1024], P('fsdp'), may hold values from -0.1875 to 0.1875
- w_output: bfloat16 [1024, 1024], P('fsdp'), may hold values from -0.1875 to 0.1875
- norm_gain: bfloat16 [1024], P('fsdp'), may hold values from 0.5 to 1.5
- w_left: bfloat16 [1024, 2816], P('fsdp'), may hold values from -0.1875 to 0.1875
- w_right: bfloat16 [1024, 2816], P('fsdp'), may hold values from -0.1875 to 0.1875
- w_down: bfloat16 [2816, 1024], P('fsdp'), may hold values from -0.109375 to 0.109375
- cotangent: bfloat16 [8192, 1024], P('fsdp'), may hold values from -6 to 6
Outputs:
- block_output: bfloat16 [8192, 1024], P('fsdp')
- grad_tokens: float32 [8192, 1024], P('fsdp')
- grad_query: float32 [1024, 1024], P('fsdp')
- grad_key: float32 [1024, 1024], P('fsdp')
- grad_value: float32 [1024, 1024], P('fsdp')
- grad_unit: float32 [1024, 1024], P('fsdp')
- grad_output: float32 [1024, 1024], P('fsdp')
- grad_gain: float32 [1024], P('fsdp')
- grad_left: float32 [1024, 2816], P('fsdp')
- grad_right: float32 [1024, 2816], P('fsdp')
- grad_down: float32 [2816, 1024], P('fsdp')
Inputs may be any that keep to these rules, and one draw needn't show every extreme that they name: lengths of the 4 sequences, summing to 8192; the longest is exactly 4096. Every number below 4 once; the stream holds sequence seq_order[0] first, then seq_order[1], and so on.
All inputs are finite; a program needn't handle non-finite values.
Results may differ from a plain program's by a relative error of at most 0.014.
The roundings to bfloat16 on the way count: a program that leaves them out, or rounds other values in their place, can miss the bound.
Values may be sent and summed in bfloat16 or wider, within the bound.
A program may use at most 256 MiB of HBM per device.

v0:
```python
import jax
import jax.numpy as jnp
from jax import lax
from jax.sharding import PartitionSpec as P

SPAN = 256


EPSILON = 1e-05


def entering(value, axis, combine, identity, reverse):
    length, here = (lax.axis_size(axis), lax.axis_index(axis))
    everything = jax.tree.map(lambda part: lax.all_gather(part, axis), value)
    start = jax.tree.map(
        lambda part, zero: jnp.broadcast_to(jnp.asarray(zero, part.dtype), part.shape),
        value,
        identity,
    )

    def hop(k, before):
        at = length - 1 - k if reverse else k
        reached = at > here if reverse else at < here
        new = combine(before, jax.tree.map(lambda part: part[at], everything))
        return jax.tree.map(lambda a, b: jnp.where(reached, a, b), new, before)

    return lax.fori_loop(0, length, hop, start)


def segment_of(places, lengths, seq_order):
    number = lengths.shape[0]
    picked = seq_order[:, None] == jnp.arange(number, dtype=jnp.int32)[None, :]
    packed = jnp.sum(jnp.where(picked, lengths[None, :], 0), axis=1, dtype=jnp.int32)
    bounds = jnp.cumsum(packed, dtype=jnp.int32)
    found = jnp.sum((bounds[None, :] <= places[:, None]).astype(jnp.int32), axis=1, dtype=jnp.int32)
    return jnp.where(places < 0, -1, found)


def decay_tables(segments, before, rate, block):
    length = segments.shape[0]
    count = length // block
    spans = segments.reshape(count, block)
    priors = jnp.concatenate([before.reshape(1), spans[:-1, -1]])
    steps = jnp.arange(block, dtype=jnp.int32)
    distance = steps[:, None] - steps[None, :]
    same = (spans[:, :, None] == spans[:, None, :]) & (distance >= 0)[None]
    powers = jnp.exp(-rate[:, None, None] * jnp.maximum(distance, 0).astype(jnp.float32)[None])
    within = jnp.where(same[:, None], powers[None], 0.0)
    entry = jnp.where(
        (spans == priors[:, None])[:, :, None],
        jnp.exp(-rate[None, :] * steps.astype(jnp.float32)[:, None])[None],
        0.0,
    )
    leaving = jnp.where(
        (spans == spans[:, -1:])[:, :, None],
        jnp.exp(-rate[None, :] * (block - steps).astype(jnp.float32)[:, None])[None],
        0.0,
    )
    passing = jnp.where((spans[:, -1] == priors)[:, None], jnp.exp(-rate * block)[None], 0.0)
    offsets = (jnp.arange(count, dtype=jnp.int32) * block).astype(jnp.float32)
    arrival = jnp.where(
        (priors == before)[:, None], jnp.exp(-rate[None, :] * offsets[:, None]), 0.0
    )
    through = jnp.where(segments[-1] == before, jnp.exp(-rate * length), 0.0)
    return (within, entry, leaving, passing, arrival, through)


def chain_states(earlier, later):
    return (earlier[0] * later[0], later[0][:, None, None] * earlier[1] + later[1])


def silu_slope(values):
    sigma = jax.nn.sigmoid(values)
    return sigma * (1.0 + values * (1.0 - sigma))


def row_scale(values):
    return lax.rsqrt(jnp.mean(values * values, axis=-1, keepdims=True) + EPSILON)


def body(
    tokens,
    lengths,
    seq_order,
    decay_rate,
    w_query,
    w_key,
    w_value,
    w_unit,
    w_output,
    norm_gain,
    w_left,
    w_right,
    w_down,
    cotangent,
):
    f32 = jnp.float32
    bf16 = jnp.bfloat16
    length, width = tokens.shape
    heads = decay_rate.shape[0]
    head_size = width // heads
    count = length // SPAN
    first = lax.axis_index("fsdp") * length
    places = first + jnp.arange(length, dtype=jnp.int32)
    segments = segment_of(places, lengths, seq_order)
    before = segment_of(jnp.reshape(first - 1, (1,)), lengths, seq_order)[0]
    within, entry, leaving, passing, arrival, through = decay_tables(
        segments, before, decay_rate, SPAN
    )
    attention_set = (
        lax.all_gather(w_query, "fsdp", axis=0, tiled=True),
        lax.all_gather(w_key, "fsdp", axis=0, tiled=True),
        lax.all_gather(w_value, "fsdp", axis=0, tiled=True),
        lax.all_gather(w_unit, "fsdp", axis=0, tiled=True),
        lax.all_gather(w_output, "fsdp", axis=0, tiled=True),
        lax.all_gather(norm_gain, "fsdp", axis=0, tiled=True),
    )
    feed_set = (
        lax.all_gather(w_left, "fsdp", axis=0, tiled=True),
        lax.all_gather(w_right, "fsdp", axis=0, tiled=True),
        lax.all_gather(w_down, "fsdp", axis=0, tiled=True),
    )
    full_query, full_key, full_value, full_unit, full_output, full_gain = attention_set
    full_left, full_right, full_down = feed_set
    inputs = tokens.astype(f32)
    first_scale = row_scale(inputs)
    normed = inputs * first_scale
    hidden = normed.astype(bf16)
    query_pre = jnp.dot(hidden, full_query, preferred_element_type=f32)
    key_pre = jnp.dot(hidden, full_key, preferred_element_type=f32)
    value_pre = jnp.dot(hidden, full_value, preferred_element_type=f32)
    unit_pre = jnp.dot(hidden, full_unit, preferred_element_type=f32)
    block_shape = (count, SPAN, heads, head_size)
    query_blocks = jax.nn.silu(query_pre).astype(bf16).reshape(block_shape)
    key_blocks = jax.nn.silu(key_pre).astype(bf16).reshape(block_shape)
    value_blocks = value_pre.astype(bf16).reshape(block_shape)
    scores = jnp.einsum("nthe,nshe->nhts", query_blocks, key_blocks, preferred_element_type=f32)
    mixing = (scores * within).astype(bf16)
    local_out = jnp.einsum("nhts,nshe->nthe", mixing, value_blocks, preferred_element_type=f32)
    keys_held = (key_blocks * leaving[..., None]).astype(bf16)
    increments = jnp.einsum("nshe,nshf->nhef", keys_held, value_blocks, preferred_element_type=f32)
    local_states = [jnp.zeros((heads, head_size, head_size), f32)]
    local_states.append(passing[0][:, None, None] * local_states[-1] + increments[0])
    end_state = local_states[count]
    start_pair = (jnp.ones_like(through), jnp.zeros_like(end_state))
    arriving = entering((through, end_state), "fsdp", chain_states, start_pair, False)[1]
    states = jnp.stack(local_states[:count]) + arrival[:, :, None, None] * arriving[None]
    state_low = states.astype(bf16)
    query_held = (query_blocks * entry[..., None]).astype(bf16)
    attended = local_out + jnp.einsum(
        "nthe,nhef->nthf", query_held, state_low, preferred_element_type=f32
    )
    attended_heads = attended.reshape(length, heads, head_size)
    head_scale = row_scale(attended_heads)
    unit_norm = (attended_heads * head_scale).reshape(length, width)
    gain = full_gain.astype(f32)
    gated = unit_norm * gain
    mixed_in = (gated * unit_pre).astype(bf16)
    middle = inputs + jnp.dot(mixed_in, full_output, preferred_element_type=f32)
    second_scale = row_scale(middle)
    second_unit = middle * second_scale
    second = second_unit.astype(bf16)
    left_pre = jnp.dot(second, full_left, preferred_element_type=f32)
    right_pre = jnp.dot(second, full_right, preferred_element_type=f32)
    product = (left_pre * right_pre).astype(bf16)
    result = (middle + jnp.dot(product, full_down, preferred_element_type=f32)).astype(bf16)
    back_feed = (
        lax.all_gather(w_left, "fsdp", axis=0, tiled=True),
        lax.all_gather(w_right, "fsdp", axis=0, tiled=True),
        lax.all_gather(w_down, "fsdp", axis=0, tiled=True),
    )
    back_left, back_right, back_down = back_feed
    grad_product = jnp.einsum("td,fd->tf", cotangent, back_down, preferred_element_type=f32)
    grad_left_pre = (grad_product * right_pre).astype(bf16)
    grad_right_pre = (grad_product * left_pre).astype(bf16)
    grad_w_down = jnp.einsum("tf,td->fd", product, cotangent, preferred_element_type=f32)
    grad_w_left = jnp.einsum("td,tf->df", second, grad_left_pre, preferred_element_type=f32)
    grad_w_right = jnp.einsum("td,tf->df", second, grad_right_pre, preferred_element_type=f32)
    feed_grads = (
        lax.psum_scatter(grad_w_left, "fsdp", scatter_dimension=0, tiled=True),
        lax.psum_scatter(grad_w_right, "fsdp", scatter_dimension=0, tiled=True),
        lax.psum_scatter(grad_w_down, "fsdp", scatter_dimension=0, tiled=True),
    )
    grad_second = jnp.einsum(
        "tf,df->td", grad_left_pre, back_left, preferred_element_type=f32
    ) + jnp.einsum("tf,df->td", grad_right_pre, back_right, preferred_element_type=f32)
    grad_middle = cotangent.astype(f32) + second_scale * (
        grad_second - second_unit * jnp.mean(grad_second * second_unit, axis=-1, keepdims=True)
    )
    back_attention = (
        lax.all_gather(w_query, "fsdp", axis=0, tiled=True),
        lax.all_gather(w_key, "fsdp", axis=0, tiled=True),
        lax.all_gather(w_value, "fsdp", axis=0, tiled=True),
        lax.all_gather(w_unit, "fsdp", axis=0, tiled=True),
        lax.all_gather(w_output, "fsdp", axis=0, tiled=True),
        lax.all_gather(norm_gain, "fsdp", axis=0, tiled=True),
    )
    back_query, back_key, back_value, back_unit, back_output, back_gain = back_attention
    grad_branch = grad_middle.astype(bf16)
    grad_w_output = jnp.einsum("td,te->de", mixed_in, grad_branch, preferred_element_type=f32)
    grad_mixed = jnp.einsum("te,de->td", grad_branch, back_output, preferred_element_type=f32)
    grad_gated = grad_mixed * unit_pre
    grad_unit_pre = (grad_mixed * gated).astype(bf16)
    grad_gain = jnp.sum(grad_gated * unit_norm, axis=0)
    grad_norm_heads = (grad_gated * back_gain.astype(f32)).reshape(length, heads, head_size)
    norm_heads = unit_norm.reshape(length, heads, head_size)
    grad_att = head_scale * (
        grad_norm_heads
        - norm_heads * jnp.mean(grad_norm_heads * norm_heads, axis=-1, keepdims=True)
    )
    grad_att_blocks = grad_att.astype(bf16).reshape(block_shape)
    grad_mixing = jnp.einsum(
        "nthf,nshf->nhts", grad_att_blocks, value_blocks, preferred_element_type=f32
    )
    grad_scores = (grad_mixing * within).astype(bf16)
    grad_query_blocks = (
        jnp.einsum("nhts,nshe->nthe", grad_scores, key_blocks, preferred_element_type=f32)
        + jnp.einsum("nthf,nhef->nthe", grad_att_blocks, state_low, preferred_element_type=f32)
        * entry[..., None]
    )
    grad_key_blocks = jnp.einsum(
        "nhts,nthe->nshe", grad_scores, query_blocks, preferred_element_type=f32
    )
    grad_value_blocks = jnp.einsum(
        "nhts,nthf->nshf", mixing, grad_att_blocks, preferred_element_type=f32
    )
    direct = jnp.einsum("nthe,nthf->nhef", query_held, grad_att_blocks, preferred_element_type=f32)
    leaving_sum = jnp.sum(arrival[:, :, None, None] * direct, axis=0)
    later = entering((through, leaving_sum), "fsdp", chain_states, start_pair, True)[1]
    next_grads = [later]
    grad_increment = jnp.stack(next_grads[::-1]).astype(bf16)
    grad_keys_held = jnp.einsum(
        "nhef,nshf->nshe", grad_increment, value_blocks, preferred_element_type=f32
    )
    grad_key_blocks = grad_key_blocks + grad_keys_held * leaving[..., None]
    grad_value_blocks = grad_value_blocks + jnp.einsum(
        "nshe,nhef->nshf", keys_held, grad_increment, preferred_element_type=f32
    )
    grad_query_pre = (grad_query_blocks.reshape(length, width) * silu_slope(query_pre)).astype(bf16)
    grad_key_pre = (grad_key_blocks.reshape(length, width) * silu_slope(key_pre)).astype(bf16)
    grad_value_pre = grad_value_blocks.reshape(length, width).astype(bf16)
    grad_w_query = jnp.einsum("td,te->de", hidden, grad_query_pre, preferred_element_type=f32)
    grad_w_key = jnp.einsum("td,te->de", hidden, grad_key_pre, preferred_element_type=f32)
    grad_w_value = jnp.einsum("td,te->de", hidden, grad_value_pre, preferred_element_type=f32)
    grad_w_unit = jnp.einsum("td,te->de", hidden, grad_unit_pre, preferred_element_type=f32)
    attention_grads = (
        lax.psum_scatter(grad_w_query, "fsdp", scatter_dimension=0, tiled=True),
        lax.psum_scatter(grad_w_key, "fsdp", scatter_dimension=0, tiled=True),
        lax.psum_scatter(grad_w_value, "fsdp", scatter_dimension=0, tiled=True),
        lax.psum_scatter(grad_w_unit, "fsdp", scatter_dimension=0, tiled=True),
        lax.psum_scatter(grad_w_output, "fsdp", scatter_dimension=0, tiled=True),
        lax.psum_scatter(grad_gain, "fsdp", scatter_dimension=0, tiled=True),
    )
    grad_hidden = (
        jnp.einsum("te,de->td", grad_query_pre, back_query, preferred_element_type=f32)
        + jnp.einsum("te,de->td", grad_key_pre, back_key, preferred_element_type=f32)
        + jnp.einsum("te,de->td", grad_value_pre, back_value, preferred_element_type=f32)
        + jnp.einsum("te,de->td", grad_unit_pre, back_unit, preferred_element_type=f32)
    )
    grad_inputs = grad_middle + first_scale * (
        grad_hidden - normed * jnp.mean(grad_hidden * normed, axis=-1, keepdims=True)
    )
    return (
        result,
        grad_inputs,
        attention_grads[0],
        attention_grads[1],
        attention_grads[2],
        attention_grads[3],
        attention_grads[4],
        attention_grads[5],
        feed_grads[0],
        feed_grads[1],
        feed_grads[2],
    )


def solution(mesh):
    placed = (
        P("fsdp", None),
        P(),
        P(),
        P(),
        P("fsdp", None),
        P("fsdp", None),
        P("fsdp", None),
        P("fsdp", None),
        P("fsdp", None),
        P("fsdp"),
        P("fsdp", None),
        P("fsdp", None),
        P("fsdp", None),
        P("fsdp", None),
    )
    return jax.shard_map(
        body,
        mesh=mesh,
        in_specs=placed,
        out_specs=(
            P("fsdp", None),
            P("fsdp", None),
            P("fsdp", None),
            P("fsdp", None),
            P("fsdp", None),
            P("fsdp", None),
            P("fsdp", None),
            P("fsdp"),
            P("fsdp", None),
            P("fsdp", None),
            P("fsdp", None),
        ),
        check_vma=False,
    )
```

profile of v0, /device:TPU:0, one launch (start us, length us, event | category | flops | bytes accessed | tf_op | source)
XLA Modules:
  0.0 1946.0 jit_solution(16182083020457053646)
XLA Ops:
  14.4 1.2 fusion.16
  16.5 53.3 %all-gather.18.cloned.1.call-done = bf16[1024,1024]{1,0:T(8,128)(2,1)} async-done(((bf16[32,1024]{1,0:T(8,128)(2,1)}), bf16[1024,1024]{1,0:T(8,128)(2,1)}) %all-gather.18.cloned.1.call-update) | async-done | bytes 2097168 | tf_op jit(solution)/shard_map/all_gather | solution.py:112
  69.8 2.5 fusion.62
  73.6 54.1 %all-gather.14.cloned.1.call-done = bf16[1024,1024]{1,0:T(8,128)(2,1)} async-done(((bf16[32,1024]{1,0:T(8,128)(2,1)}), bf16[1024,1024]{1,0:T(8,128)(2,1)}) %all-gather.14.cloned.1.call-update) | async-done | bytes 2097168 | tf_op jit(solution)/shard_map/all_gather | solution.py:113
  127.7 2.4 fusion.11
  130.1 1.5 convolution_add_fusion.7
  135.5 38.5 %all-reduce.1 = bf16[1024]{0:T(1024)(128)(2,1)S(1)} all-reduce(bf16[1024]{0:T(1024)(128)(2,1)S(1)} %dynamic-update-slice.1), channel_id=1, replica_groups=mesh['fsdp'=32] {'fsdp'}, use_global_device_ids=true, to_apply=%add.1 | all-reduce | flops 1024 | bytes 4096
  174.1 41.9 %all-reduce = f32[256]{0:T(256)S(1)} all-reduce(f32[256]{0:T(256)S(1)} %get-tuple-element.306), channel_id=2, replica_groups=mesh['fsdp'=32] {'fsdp'}, use_global_device_ids=true, to_apply=%add | all-reduce | flops 256 | bytes 2048
  216.0 3.3 multiply_convert_fusion.12
  221.3 1.5 fusion.27
  222.8 80.1 %all-gather.30.cloned.1.call-done = f32[256,128,128]{2,1,0:T(8,128)} async-done(((f32[8,128,128]{2,1,0:T(8,128)}), f32[256,128,128]{2,1,0:T(8,128)}) %all-gather.30.cloned.1.call-update) | async-done | bytes 16777232 | tf_op jit(solution)/shard_map/all_gather | solution.py:14
  302.9 39.1 %while.30 = (s32[]{:T(128)}, f32[8,128,128]{2,1,0:T(8,128)S(1)}, s32[]{:T(128)}, f32[32,8]{1,0:T(8,128)S(1)}, f32[32,8,128,128]{3,2,1,0:T(8,128)}, /*index=5*/s32[]{:T(128)}, s32[]{:T(128)}) while((s32[]{:T(128)}, f32[8,128,128]{2,1,0:T(8,128)S(1)}, s32[]{:T(128)}, f32[32,8]{1,0:T(8,128)S(1)}, f32[32,8,128,128]{3,2,1,0:T(8,128)}, ...), condition=%wide.region_6.7_spmd.clone, body=%wide.region_5.6_spmd.clone.sunk | while | flops 524292 | bytes 1573073 | solution.py:27
  342.6 1.7 fusion.17
  345.8 2.5 copy.104
  348.3 11.8 all-gather.20.cloned.1.call-done
  360.1 4.0 multiply_convert_fusion.8
  364.1 53.8 %all-gather.22.cloned.1.call-done = bf16[1024,1024]{1,0:T(8,128)(2,1)} async-done(((bf16[32,1024]{1,0:T(8,128)(2,1)}), bf16[1024,1024]{1,0:T(8,128)(2,1)}) %all-gather.22.cloned.1.call-update) | async-done | bytes 2097168 | tf_op jit(solution)/shard_map/all_gather | solution.py:115
  417.9 2.6 multiply_reduce_fusion.2
  421.5 65.4 %all-gather.24.cloned.1.call-done = bf16[1024,2816]{1,0:T(8,128)(2,1)} async-done(((bf16[32,2816]{1,0:T(8,128)(2,1)}), bf16[1024,2816]{1,0:T(8,128)(2,1)}) %all-gather.24.cloned.1.call-update) | async-done | bytes 5767184 | tf_op jit(solution)/shard_map/all_gather | solution.py:119
  486.9 6.0 fusion.67
  493.0 62.8 %all-gather.26.cloned.1.call-done = bf16[1024,2816]{1,0:T(8,128)(2,1)} async-done(((bf16[32,2816]{1,0:T(8,128)(2,1)}), bf16[1024,2816]{1,0:T(8,128)(2,1)}) %all-gather.26.cloned.1.call-update) | async-done | bytes 5767184 | tf_op jit(solution)/shard_map/all_gather | solution.py:120
  555.8 6.1 fusion.68
  561.8 62.8 %all-gather.28.cloned.1.call-done = bf16[2816,1024]{1,0:T(8,128)(2,1)} async-done(((bf16[88,1024]{1,0:T(8,128)(2,1)}), bf16[2816,1024]{1,0:T(8,128)(2,1)}) %all-gather.28.cloned.1.call-update) | async-done | bytes 5767184 | tf_op jit(solution)/shard_map/all_gather | solution.py:121
  624.6 7.3 multiply_convert_fusion
  632.0 5.4 fusion.69
  637.4 1.8 multiply_reduce_fusion.1
  639.3 1.7 multiply_add_fusion
  641.4 2.2 multiply_reduce_fusion
  643.6 2.5 copy.105
  646.2 1.5 fusion.19
  650.1 1.7 multiply_convert_fusion.3
  653.7 1.3 copy.124
  655.0 2.0 multiply_convert_fusion.7
  657.8 2.8 fusion.58
  661.6 2.8 fusion.52
  665.5 2.7 fusion.41
  668.3 1.3 copy-done.20
  669.7 6.0 fusion.72
  675.8 1.3 copy-done.18
  677.1 5.9 fusion.73
  683.0 1.3 copy-done.15
  684.4 5.9 fusion.74
  691.4 2.5 convolution_bitcast_fusion.2
  693.9 69.1 %all-gather.32.cloned.1.call-done = f32[256,128,128]{2,1,0:T(8,128)} async-done(((f32[8,128,128]{2,1,0:T(8,128)}), f32[256,128,128]{2,1,0:T(8,128)}) %all-gather.32.cloned.1.call-update) | async-done | bytes 16777232 | tf_op jit(solution)/shard_map/all_gather | solution.py:14
  763.0 60.5 %while.31 = (s32[]{:T(128)}, f32[8,128,128]{2,1,0:T(8,128)S(1)}, s32[]{:T(128)}, f32[32,8]{1,0:T(8,128)}, f32[32,8,128,128]{3,2,1,0:T(8,128)}, /*index=5*/s32[]{:T(128)}, s32[]{:T(128)}, s32[]{:T(128)}, s32[]{:T(128)}) while((s32[]{:T(128)}, f32[8,128,128]{2,1,0:T(8,128)S(1)}, s32[]{:T(128)}, f32[32,8]{1,0:T(8,128)}, ...), condition=%wide.region_12.13_spmd.clone, body=%wide.region_11.12_spmd.clone.sunk | while | flops 524296 | bytes 1573135 | solution.py:27
  769.4 1.2 fusion.126
  823.5 2.8 fusion.8
  826.3 2.6 copy.125
  828.9 1.6 multiply_convert_fusion.6
  831.3 2.8 fusion.56
  835.1 1.5 fusion.71
  837.3 2.9 fusion.54
  840.2 39.3 %all-reduce.2 = f32[1024]{0:T(1024)S(1)} all-reduce(f32[1024]{0:T(1024)S(1)} %get-tuple-element.302), channel_id=10, replica_groups=mesh['fsdp'=32] {'fsdp'}, use_global_device_ids=true, to_apply=%region_20.21.clone | all-reduce | flops 1024 | bytes 8192
  880.1 2.3 fusion.70
  882.4 5.4 fusion.9
  892.2 1.3 fusion.15
  893.5 13.9 reduce-scatter.9.cloned.1.call-done
  907.4 141.7 %reduce-scatter.15.cloned.1.call-done = f32[32,1024]{1,0:T(8,128)} async-done(((f32[1024,1024]{1,0:T(8,128)}), f32[32,1024]{1,0:T(8,128)}) %reduce-scatter.15.cloned.1.call-update) | async-done | bytes 131088 | tf_op jit(solution)/shard_map/reduce_scatter | solution.py:250
  1049.0 141.6 %reduce-scatter.17.cloned.1.call-done = f32[32,1024]{1,0:T(8,128)} async-done(((f32[1024,1024]{1,0:T(8,128)}), f32[32,1024]{1,0:T(8,128)}) %reduce-scatter.17.cloned.1.call-update) | async-done | bytes 131088 | tf_op jit(solution)/shard_map/reduce_scatter | solution.py:251
  1190.6 155.0 %reduce-scatter.19.cloned.1.call-done = f32[32,2816]{1,0:T(8,128)} async-done(((f32[1024,2816]{1,0:T(8,128)}), f32[32,2816]{1,0:T(8,128)}) %reduce-scatter.19.cloned.1.call-update) | async-done | bytes 360464 | tf_op jit(solution)/shard_map/reduce_scatter | solution.py:180
  1345.6 155.0 %reduce-scatter.21.cloned.1.call-done = f32[32,2816]{1,0:T(8,128)} async-done(((f32[1024,2816]{1,0:T(8,128)}), f32[32,2816]{1,0:T(8,128)}) %reduce-scatter.21.cloned.1.call-update) | async-done | bytes 360464 | tf_op jit(solution)/shard_map/reduce_scatter | solution.py:181
  1500.6 155.1 %reduce-scatter.23.cloned.1.call-done = f32[88,1024]{1,0:T(8,128)} async-done(((f32[2816,1024]{1,0:T(8,128)}), f32[88,1024]{1,0:T(8,128)}) %reduce-scatter.23.cloned.1.call-update) | async-done | bytes 360464 | tf_op jit(solution)/shard_map/reduce_scatter | solution.py:182
  1655.7 141.5 %reduce-scatter.11.cloned.1.call-done = f32[32,1024]{1,0:T(8,128)} async-done(((f32[1024,1024]{1,0:T(8,128)}), f32[32,1024]{1,0:T(8,128)}) %reduce-scatter.11.cloned.1.call-update) | async-done | bytes 131088 | tf_op jit(solution)/shard_map/reduce_scatter | solution.py:248
  1797.2 141.5 %reduce-scatter.13.cloned.1.call-done = f32[32,1024]{1,0:T(8,128)} async-done(((f32[1024,1024]{1,0:T(8,128)}), f32[32,1024]{1,0:T(8,128)}) %reduce-scatter.13.cloned.1.call-update) | async-done | bytes 131088 | tf_op jit(solution)/shard_map/reduce_scatter | solution.py:249
  (296 shorter events, 128.8 us)
Async XLA Ops:
  7.2 62.6 %all-gather.18.cloned.1.call-start = ((), (), s32[]{:S(2)}) async-start(), calls=%async_computation.10 | async-start | bytes 2162688 | tf_op jit(solution)/shard_map/all_gather | solution.py:112
  7.9 119.8 %all-gather.14.cloned.1.call-start = ((), (), s32[]{:S(2)}) async-start(), calls=%async_computation.8 | async-start | bytes 2162688 | tf_op jit(solution)/shard_map/all_gather | solution.py:113
  8.7 207.4 %all-gather.16.cloned.1.call-start = ((), (), s32[]{:S(2)}) async-start(), calls=%async_computation.9 | async-start | bytes 2162688 | tf_op jit(solution)/shard_map/all_gather | solution.py:111
  9.4 293.5 %all-gather.30.cloned.1.call-start = ((), (), s32[]{:S(2)}) async-start(), calls=%async_computation.24 | async-start | bytes 17301504 | tf_op jit(solution)/shard_map/all_gather | solution.py:14
  16.4 111.3 %copy-start = (bf16[256,1024]{1,0:T(8,128)(2,1)S(1)}, bf16[256,1024]{1,0:T(8,128)(2,1)}, u32[]{:S(2)}) copy-start(bf16[256,1024]{1,0:T(8,128)(2,1)} %param.18) | copy-start | bytes 1572868
  72.3 1.0 copy-start.4
  73.6 146.0 %copy-start.23 = (bf16[32,8,8,128]{3,2,1,0:T(8,128)(2,1)}, bf16[32,8,8,128]{3,2,1,0:T(8,128)(2,1)S(1)}, u32[]{:S(2)}) copy-start(bf16[32,8,8,128]{3,2,1,0:T(8,128)(2,1)S(1)} %fusion.32) | copy-start | bytes 1572868
  130.1 90.2 %copy-start.41 = (bf16[32,8,8,128]{3,2,1,0:T(8,128)(2,1)}, bf16[32,8,8,128]{3,2,1,0:T(8,128)(2,1)S(1)}, u32[]{:S(2)}) copy-start(bf16[32,8,8,128]{3,2,1,0:T(8,128)(2,1)S(1)} %fusion.11) | copy-start | bytes 1572868
  130.1 5.2 copy-start.45
  131.7 228.4 %all-gather.20.cloned.1.call-start = ((), (), s32[]{:S(2)}) async-start(), calls=%async_computation.11 | async-start | bytes 2162688 | tf_op jit(solution)/shard_map/all_gather | solution.py:114
  132.2 285.6 %all-gather.22.cloned.1.call-start = ((), (), s32[]{:S(2)}) async-start(), calls=%async_computation.12 | async-start | bytes 2162688 | tf_op jit(solution)/shard_map/all_gather | solution.py:115
  132.8 354.1 %all-gather.24.cloned.1.call-start = ((), (), s32[]{:S(2)}) async-start(), calls=%async_computation.13 | async-start | bytes 5947392 | tf_op jit(solution)/shard_map/all_gather | solution.py:119
  133.6 422.2 %all-gather.26.cloned.1.call-start = ((), (), s32[]{:S(2)}) async-start(), calls=%async_computation.14 | async-start | bytes 5947392 | tf_op jit(solution)/shard_map/all_gather | solution.py:120
  134.3 490.3 %all-gather.28.cloned.1.call-start = ((), (), s32[]{:S(2)}) async-start(), calls=%async_computation.15 | async-start | bytes 5947392 | tf_op jit(solution)/shard_map/all_gather | solution.py:121
  135.1 627.9 %all-gather.32.cloned.1.call-start = ((), (), s32[]{:S(2)}) async-start(), calls=%async_computation.25 | async-start | bytes 17301504 | tf_op jit(solution)/shard_map/all_gather | solution.py:14
  219.6 123.1 %copy-start.12 = (bf16[256,1024]{0,1:T(8,128)(2,1)}, bf16[256,1024]{0,1:T(8,128)(2,1)S(1)}, u32[]{:S(2)}) copy-start(bf16[256,1024]{0,1:T(8,128)(2,1)S(1)} %copy.126) | copy-start | bytes 1572868
  220.3 1.0 copy-start.36
  342.0 0.6 copy-start.43
  420.5 216.9 %copy-start.1 = (f32[256,1024]{1,0:T(8,128)}, f32[256,1024]{1,0:T(8,128)S(1)}, u32[]{:S(2)}) copy-start(f32[256,1024]{1,0:T(8,128)S(1)} %get-tuple-element.317) | copy-start | bytes 3145732
  632.0 5.4 copy-start.19
  632.0 5.4 copy-start.17
  632.0 5.4 copy-start.44
  637.4 1.9 copy-start.21
  637.4 3.6 copy-start.39
  639.3 1.9 copy-start.11
  639.3 2.2 copy-start.38
  646.2 1.5 copy-start.3
  646.2 2.5 copy-start.13
  647.9 0.8 copy-start.7
  648.7 1.4 copy-start.42
  649.8 2.0 copy-start.24
  649.9 257.5 %reduce-scatter.9.cloned.1.call-start = ((), (), s32[]{:S(2)}) async-start(), calls=%async_computation.16 | async-start | bytes 4325376 | tf_op jit(solution)/shard_map/reduce_scatter | solution.py:247
  651.9 1.8 copy-start.37
  651.9 1.4 copy-start.8
  657.0 0.8 copy-start.26
  660.6 1.0 copy-start.31
  660.6 388.4 %reduce-scatter.15.cloned.1.call-start = ((), (), s32[]{:S(2)}) async-start(), calls=%async_computation.19 | async-start | bytes 4325376 | tf_op jit(solution)/shard_map/reduce_scatter | solution.py:250
  664.4 1.0 copy-start.33
  664.5 526.1 %reduce-scatter.17.cloned.1.call-start = ((), (), s32[]{:S(2)}) async-start(), calls=%async_computation.20 | async-start | bytes 4325376 | tf_op jit(solution)/shard_map/reduce_scatter | solution.py:251
  668.2 1.4 copy-start.20
  668.2 1.5 copy-start.30
  668.3 677.3 %reduce-scatter.19.cloned.1.call-start = ((), (), s32[]{:S(2)}) async-start(), calls=%async_computation.21 | async-start | bytes 11894784 | tf_op jit(solution)/shard_map/reduce_scatter | solution.py:180
  675.7 1.4 copy-start.18
  675.7 824.9 %reduce-scatter.21.cloned.1.call-start = ((), (), s32[]{:S(2)}) async-start(), calls=%async_computation.22 | async-start | bytes 11894784 | tf_op jit(solution)/shard_map/reduce_scatter | solution.py:181
  683.0 1.4 copy-start.15
  683.0 1.5 copy-start.22
  683.0 972.7 %reduce-scatter.23.cloned.1.call-start = ((), (), s32[]{:S(2)}) async-start(), calls=%async_computation.23 | async-start | bytes 11894784 | tf_op jit(solution)/shard_map/reduce_scatter | solution.py:182
  690.4 1.0 copy-start.14
  690.4 1106.8 %reduce-scatter.11.cloned.1.call-start = ((), (), s32[]{:S(2)}) async-start(), calls=%async_computation.17 | async-start | bytes 4325376 | tf_op jit(solution)/shard_map/reduce_scatter | solution.py:248
  823.5 5.3 copy-start.5
  830.5 0.8 copy-start.28
  834.1 1.0 copy-start.9
  834.1 2.6 copy-start.25
  834.1 1104.6 %reduce-scatter.13.cloned.1.call-start = ((), (), s32[]{:S(2)}) async-start(), calls=%async_computation.18 | async-start | bytes 4325376 | tf_op jit(solution)/shard_map/reduce_scatter | solution.py:249
  837.2 2.9 copy-start.34
  840.1 39.9 %copy-start.27 = (bf16[256,1024]{1,0:T(8,128)(2,1)S(1)}, bf16[256,1024]{1,0:T(8,128)(2,1)}, u32[]{:S(2)}) copy-start(bf16[256,1024]{1,0:T(8,128)(2,1)} %copy-done.26) | copy-start | bytes 1572868
  840.2 42.2 %copy-start.2 = (f32[256,1024]{1,0:T(8,128)S(1)}, f32[256,1024]{1,0:T(8,128)}, u32[]{:S(2)}) copy-start(f32[256,1024]{1,0:T(8,128)} %copy-done.1) | copy-start | bytes 3145732
  879.5 2.9 copy-start.16
  882.4 5.4 copy-start.10
  882.4 5.4 copy-start.29
  887.8 1.0 copy-start.35
  887.8 1.8 copy-start.40
  889.6 1.6 copy-start.6
  889.6 1.7 copy-start.32
Sparse Core Ops, SparseCore 0:
  10.8 58.9 all-gather.17
  72.7 55.0 all-gather.13
  130.6 55.0 all-gather.15
  189.0 113.8 all-gather.29
  305.6 54.4 all-gather.19
  362.8 55.0 all-gather.21
  420.7 66.1 all-gather.23
  489.8 65.9 all-gather.25
  558.6 65.9 all-gather.27
  650.0 112.9 all-gather.31
  765.9 141.4 reduce-scatter.8
  910.1 138.9 reduce-scatter.14
  1051.9 138.6 reduce-scatter.16
  1193.3 152.1 reduce-scatter.18
  1348.3 152.2 reduce-scatter.20
  1503.3 152.3 reduce-scatter.22
  1658.4 138.7 reduce-scatter.10
  1799.9 138.7 reduce-scatter.12
where the time goes:
time: 1960 us; the launch traced here: 1950 us
  waiting for transfers between devices  1560 us (80%)
  blocking collectives  120 us (6%)
  matrix products  102 us (5%)
  other arithmetic  88.6 us (5%)
  local copies, waits for them, and re-layouts  51.3 us (3%)
    reduce_scatter x1, waiting for transfers between devices, body(): lax.psum_scatter(grad_w_down, 'fsdp', scatter_dimension=0, tiled=True)  155 us
    reduce_scatter x1, waiting for transfers between devices, body(): lax.psum_scatter(grad_w_right, 'fsdp', scatter_dimension=0, tiled=True)  155 us
    reduce_scatter x1, waiting for transfers between devices, body(): lax.psum_scatter(grad_w_left, 'fsdp', scatter_dimension=0, tiled=True)  155 us
    all_gather x2, waiting for transfers between devices, entering(): everything = jax.tree.map(lambda part: lax.all_gather(part, axis), value)  149 us
    reduce_scatter x1, waiting for transfers between devices, body(): lax.psum_scatter(grad_w_unit, 'fsdp', scatter_dimension=0, tiled=True)  142 us
    reduce_scatter x1, waiting for transfers between devices, body(): lax.psum_scatter(grad_w_output, 'fsdp', scatter_dimension=0, tiled=True)  142 us
    reduce_scatter x1, waiting for transfers between devices, body(): lax.psum_scatter(grad_w_value, 'fsdp', scatter_dimension=0, tiled=True)  142 us
    reduce_scatter x1, waiting for transfers between devices, body(): lax.psum_scatter(grad_w_key, 'fsdp', scatter_dimension=0, tiled=True)  142 us
  transfers between devices with their start and end apart: 18, of which 17 were waited for; matrix products, arithmetic and copies ran while one was open for 10% of the time, Pallas kernels for 0%

commit v1 on v0

--- a/solution.py
+++ b/solution.py
@@ -1,13 +1,533 @@
+import functools
+
 import jax
 import jax.numpy as jnp
 from jax import lax
+from jax.experimental import pallas as pl
+from jax.experimental.pallas import tpu as pltpu
 from jax.sharding import PartitionSpec as P
 
 SPAN = 256
-
-
+AXIS = "fsdp"
+TE_DE = "te,de->td"
+TD_TE = "td,te->de"
 EPSILON = 1e-05
-
+LOGICAL = pl.DeviceIdType.LOGICAL
+VMEM_LIMIT = 64000000
+
+
+class Place:
+    def __init__(self):
+        me = lax.axis_index(AXIS)
+        self.me = me
+        self.c = lax.rem(me, 2)
+        self.x = lax.rem(me // 2, 2)
+        self.y = lax.rem(me // 4, 2)
+        self.z = me // 8
+        self.inner = (self.z == 1) | (self.z == 2)
+        self.even = lax.rem(self.z, 2) == 0
+        self.sib = self.z + 1 - 2 * lax.rem(self.z, 2)
+        half = self.z // 2
+        self.near = 2 - half
+        self.far = 3 - 3 * half
+        self.cross = 3 - self.z
+        self.x1 = 1 - self.x
+        self.y1 = 1 - self.y
+        self.c1 = 1 - self.c
+        self.to = {
+            "S": self.dev(self.sib, self.y, self.x, self.c),
+            "K": self.dev(self.cross, self.y, self.x, self.c),
+            "x": self.dev(self.z, self.y, self.x1, self.c),
+            "y": self.dev(self.z, self.y1, self.x, self.c),
+            "p": self.dev(self.z, self.y, self.x, self.c1),
+        }
+
+    def dev(self, z, y, x, c):
+        return ((z * 2 + y) * 2 + x) * 2 + c
+
+
+def greet(place):
+    barrier = pltpu.get_barrier_semaphore()
+    for link in ("p", "x", "y", "S"):
+        pl.semaphore_signal(barrier, inc=1, device_id=place.to[link], device_id_type=LOGICAL)
+
+    @pl.when(place.inner)
+    def _():
+        pl.semaphore_signal(barrier, inc=1, device_id=place.to["K"], device_id_type=LOGICAL)
+
+    pl.semaphore_wait(barrier, jnp.where(place.inner, 5, 4))
+
+
+def arrived(ref, send, recv, place):
+    pltpu.make_async_remote_copy(
+        src_ref=ref,
+        dst_ref=ref,
+        send_sem=send,
+        recv_sem=recv,
+        device_id=place.to["p"],
+        device_id_type=LOGICAL,
+    ).wait_recv()
+
+
+class Gather:
+    RECV = ("Cs", "Cn", "Cf", "Xo", "Xs", "Xn", "Xf", "Yo", "Ys", "Yn", "Yf", "D0", "D1", "En", "Ef")
+    GROUPS = ("C", "X", "Y", "D")
+    NRECV = 19
+    NSEND = 25
+
+    def __init__(self, place, own, full, send, recv, index):
+        self.p, self.own, self.full = place, own, full
+        self.send, self.recv, self.index = send, recv, index
+        self.sent = []
+        p = place
+        self.where = {}
+        for g, y, x in (("C", p.y, p.x), ("X", p.y, p.x1), ("Y", p.y1, p.x), ("D", p.y1, p.x1)):
+            for k, z in (("o", p.z), ("s", p.sib), ("n", p.near), ("f", p.far)):
+                self.where[g + k] = (z, y, x, p.c)
+        for a, b in (("D0", "Do"), ("D1", "Ds"), ("En", "Dn"), ("Ef", "Df")):
+            self.where[a] = self.where[b]
+
+    def slot(self, name):
+        return self.full.at[self.where[name]]
+
+    def copy(self, name, link, landing):
+        src = self.own if name == "Co" else self.slot(name)
+        k = len(self.sent)
+        made = pltpu.make_async_remote_copy(
+            src_ref=src,
+            dst_ref=self.slot(name),
+            send_sem=self.send.at[self.index, k],
+            recv_sem=self.recv.at[self.index, self.RECV.index(landing)],
+            device_id=self.p.to[link],
+            device_id_type=LOGICAL,
+        )
+        return made
+
+    def go(self, name, link, landing, cond=None):
+        made = self.copy(name, link, landing)
+        self.sent.append((made, cond))
+        if cond is None:
+            made.start()
+        else:
+            pl.when(cond)(made.start)
+
+    def wait(self, name):
+        arrived(self.slot(name), self.send.at[self.index, 0], self.recv.at[self.index, self.RECV.index(name)], self.p)
+
+    def group(self, g):
+        p = self.p
+        y = p.y if g in "CX" else p.y1
+        x = p.x if g in "CY" else p.x1
+        return y, x
+
+    def pair(self, g):
+        y, x = self.group(g)
+        ref = self.full.at[:, y, x, self.p.c]
+        k = len(self.sent)
+        made = pltpu.make_async_remote_copy(
+            src_ref=ref,
+            dst_ref=ref,
+            send_sem=self.send.at[self.index, k],
+            recv_sem=self.recv.at[self.index, 15 + self.GROUPS.index(g)],
+            device_id=self.p.to["p"],
+            device_id_type=LOGICAL,
+        )
+        self.sent.append((made, None))
+        made.start()
+
+    def round(self, r):
+        p = self.p
+        inner, even = p.inner, p.even
+        odd = jnp.logical_not(even)
+        if r == 0:
+            keep = pltpu.make_async_copy(self.own, self.slot("Co"), self.send.at[self.index, self.NSEND])
+            self.keep = keep
+            keep.start()
+            self.go("Co", "S", "Cs")
+            self.go("Co", "K", "Cn", inner)
+            self.go("Co", "x", "Xo")
+            self.go("Co", "y", "Yo")
+        if r == 1:
+            self.wait("Cs")
+            self.go("Cs", "K", "Cf", inner)
+            self.go("Cs", "x", "Xs")
+            self.go("Cs", "y", "Ys")
+            self.wait("Xo")
+            self.go("Xo", "y", "D0", even)
+            self.wait("Yo")
+            self.go("Yo", "x", "D0", odd)
+        if r == 2:
+            self.wait("Cn")
+            self.go("Cn", "S", "Cn", inner)
+            self.go("Cn", "x", "Xn")
+            self.go("Cn", "y", "Yn")
+            self.wait("Xs")
+            self.go("Xs", "y", "D1", odd)
+            self.wait("Ys")
+            self.go("Ys", "x", "D1", even)
+            self.wait("D0")
+            self.go("D0", "K", "En", inner)
+        if r == 3:
+            self.wait("Cf")
+            self.go("Cf", "S", "Cf", inner)
+            self.go("Cf", "x", "Xf")
+            self.go("Cf", "y", "Yf")
+            self.keep.wait()
+            self.pair("C")
+            self.wait("D1")
+            self.go("D1", "K", "Ef", inner)
+            self.wait("Xn")
+            self.wait("Yn")
+        if r == 4:
+            self.wait("En")
+            self.go("En", "S", "En", inner)
+            self.wait("Xf")
+            self.pair("X")
+            self.wait("Yf")
+            self.pair("Y")
+        if r == 5:
+            self.wait("Ef")
+            self.go("Ef", "S", "Ef", inner)
+            self.pair("D")
+
+    def pairs(self):
+        for g in self.GROUPS:
+            y, x = self.group(g)
+            ref = self.full.at[:, y, x, self.p.c1]
+            arrived(ref, self.send.at[self.index, 0], self.recv.at[self.index, 15 + self.GROUPS.index(g)], self.p)
+
+    def finish(self):
+        for made, cond in self.sent:
+            if cond is None:
+                made.wait_send()
+            else:
+                pl.when(cond)(made.wait_send)
+
+
+def gather_kernel(n, *refs):
+    own, full = refs[:n], refs[n : 2 * n]
+    send, recv = refs[2 * n :]
+    place = Place()
+    greet(place)
+    made = [Gather(place, own[i], full[i], send, recv, i) for i in range(n)]
+    for step in range(n + 5):
+        for r in range(6):
+            i = step - r
+            if 0 <= i < n:
+                made[i].round(r)
+    for one in made:
+        one.pairs()
+    for one in made:
+        one.finish()
+
+
+def gather_all(shards):
+    n = len(shards)
+    return pl.pallas_call(
+        functools.partial(gather_kernel, n),
+        out_shape=[jax.ShapeDtypeStruct((4, 2, 2, 2) + s.shape, s.dtype) for s in shards],
+        in_specs=[pl.BlockSpec(memory_space=pltpu.VMEM)] * n,
+        out_specs=[pl.BlockSpec(memory_space=pltpu.HBM)] * n,
+        scratch_shapes=[
+            pltpu.SemaphoreType.DMA((n, Gather.NSEND + 1)),
+            pltpu.SemaphoreType.DMA((n, Gather.NRECV)),
+        ],
+        compiler_params=pltpu.CompilerParams(
+            collective_id=0, has_side_effects=True, vmem_limit_bytes=VMEM_LIMIT
+        ),
+        name="gather",
+    )(*shards)
+
+
+def add_into(out, parts):
+    rows = out.shape[0]
+    step = 8 if rows % 16 else 16
+
+    @pl.loop(0, rows // step)
+    def _(i):
+        at = pl.ds(pl.multiple_of(i * step, step), step)
+        total = parts[0][at, :].astype(jnp.float32)
+        for part in parts[1:]:
+            total = total + part[at, :].astype(jnp.float32)
+        out[at, :] = total.astype(out.dtype)
+
+
+class Scatter:
+    NRECV = 20
+    NSEND = 22
+    SLOTS = ("x0", "x1", "x2", "x3", "Fx", "y0", "y1", "y2", "y3", "Fy", "En", "Ef", "Cn", "Cf", "Co", "De", "Do", "KCs", "KCo")
+
+    def __init__(self, place, part, acc, own, came, out, send, recv, index):
+        self.p, self.part, self.acc, self.own, self.came, self.out = place, part, acc, own, came, out
+        self.send, self.recv, self.index = send, recv, index
+        self.sent = []
+        p = place
+        half = p.z // 2
+        self.ze, self.zo = 2 * half, 2 * half + 1
+        self.C = lambda z: (z, p.y, p.x)
+        self.X = lambda z: (z, p.y, p.x1)
+        self.Y = lambda z: (z, p.y1, p.x)
+        self.D = lambda z: (z, p.y1, p.x1)
+
+    def go(self, where, link, slot, cond=None):
+        k = len(self.sent)
+        at = self.SLOTS.index(slot) if isinstance(slot, str) else slot
+        made = pltpu.make_async_remote_copy(
+            src_ref=self.acc.at[where],
+            dst_ref=self.came.at[at],
+            send_sem=self.send.at[self.index, k],
+            recv_sem=self.recv.at[self.index, at],
+            device_id=self.p.to[link],
+            device_id_type=LOGICAL,
+        )
+        self.sent.append((made, cond))
+        if cond is None:
+            made.start()
+        else:
+            pl.when(cond)(made.start)
+
+    def wait(self, slot):
+        at = self.SLOTS.index(slot) if isinstance(slot, str) else slot
+        arrived(self.came.at[at], self.send.at[self.index, 0], self.recv.at[self.index, at], self.p)
+        return self.came.at[at]
+
+    def add(self, where, slots):
+        parts = [self.wait(s) for s in slots]
+        add_into(self.acc.at[where], [self.acc.at[where]] + parts)
+
+    def round(self, r):
+        p = self.p
+        inner = p.inner
+        outer = jnp.logical_not(inner)
+        ze, zo, near, far = self.ze, self.zo, p.near, p.far
+        if r == 0:
+            made = pltpu.make_async_remote_copy(
+                src_ref=self.part.at[:, :, :, p.c1],
+                dst_ref=self.acc,
+                send_sem=self.send.at[self.index, 0],
+                recv_sem=self.recv.at[self.index, 19],
+                device_id=p.to["p"],
+                device_id_type=LOGICAL,
+            )
+            self.sent.append((made, None))
+            made.start()
+            self.load = pltpu.make_async_copy(
+                self.part.at[:, :, :, p.c], self.own, self.send.at[self.index, self.NSEND]
+            )
+            self.load.start()
+        if r == 1:
+            self.load.wait()
+            arrived(self.acc, self.send.at[self.index, 0], self.recv.at[self.index, 19], p)
+
+            @pl.loop(0, 4)
+            def _(z):
+                for y in range(2):
+                    for x in range(2):
+                        add_into(self.acc.at[z, y, x], [self.acc.at[z, y, x], self.own.at[z, y, x]])
+
+            self.go(self.D(far), "S", "Ef", outer)
+            self.go(self.D(near), "S", "En", outer)
+            self.go(self.X(far), "x", far)
+            self.go(self.Y(far), "y", far + 5)
+            self.go(self.D(ze), "y", "Fy", outer)
+            self.go(self.D(zo), "x", "Fx", outer)
+            self.go(self.X(near), "x", near)
+            self.go(self.Y(near), "y", near + 5)
+            self.go(self.X(zo), "x", zo)
+            self.go(self.Y(ze), "y", ze + 5)
+        if r == 2:
+
+            @pl.when(inner)
+            def _():
+                self.add(self.D(far), ["Ef"])
+                self.add(self.D(near), ["En"])
+
+            self.go(self.D(far), "K", jnp.where(p.z == 1, self.SLOTS.index("Do"), self.SLOTS.index("De")), inner)
+            self.go(self.D(near), "K", jnp.where(p.z == 1, self.SLOTS.index("De"), self.SLOTS.index("Do")), inner)
+            parts = [self.wait(far), self.wait(far + 5)]
+            add_into(self.acc.at[self.C(far)], [self.acc.at[self.C(far)]] + parts)
+            self.go(self.C(far), "S", "Cf", outer)
+        if r == 3:
+
+            @pl.when(inner)
+            def _():
+                self.add(self.D(ze), ["De"])
+                self.add(self.D(zo), ["Do"])
+                self.add(self.C(far), ["Cf"])
+
+            self.go(self.D(ze), "y", "Fy", inner)
+            self.go(self.D(zo), "x", "Fx", inner)
+            self.go(self.C(far), "K", "KCs", inner)
+            parts = [self.wait(near), self.wait(near + 5)]
+            add_into(self.acc.at[self.C(near)], [self.acc.at[self.C(near)]] + parts)
+            self.go(self.C(near), "S", "Cn", outer)
+        if r == 4:
+            self.add(self.X(ze), ["Fy"])
+            self.add(self.Y(zo), ["Fx"])
+            self.go(self.X(ze), "x", ze)
+            self.go(self.Y(zo), "y", zo + 5)
+
+            @pl.when(inner)
+            def _():
+                self.add(self.C(near), ["Cn"])
+
+            self.go(self.C(near), "K", "KCo", inner)
+        if r == 5:
+            self.add(self.C(p.sib), [p.sib, p.sib + 5])
+
+            @pl.when(inner)
+            def _():
+                self.add(self.C(p.sib), ["KCs"])
+
+            self.go(self.C(p.sib), "S", "Co")
+        if r == 6:
+            slots = [p.z, p.z + 5, "Co"]
+            parts = [self.acc.at[self.C(p.z)]] + [self.wait(s) for s in slots]
+            add_into(self.out, parts)
+
+            @pl.when(inner)
+            def _():
+                add_into(self.out, [self.out, self.wait("KCo")])
+
+    def finish(self):
+        for made, cond in self.sent:
+            if cond is None:
+                made.wait_send()
+            else:
+                pl.when(cond)(made.wait_send)
+
+
+def scatter_kernel(n, *refs):
+    part, out = refs[:n], refs[n : 2 * n]
+    acc, own, came = refs[2 * n : 3 * n], refs[3 * n : 4 * n], refs[4 * n : 5 * n]
+    send, recv = refs[5 * n :]
+    place = Place()
+    greet(place)
+    made = [
+        Scatter(place, part[i], acc[i], own[i], came[i], out[i], send, recv, i) for i in range(n)
+    ]
+    for step in range(n + 6):
+        for r in range(7):
+            i = step - r
+            if 0 <= i < n:
+                made[i].round(r)
+    for one in made:
+        one.finish()
+
+
+def scatter_all(parts):
+    n = len(parts)
+    blocks = [(p.shape[4:], p.dtype) for p in parts]
+    return pl.pallas_call(
+        functools.partial(scatter_kernel, n),
+        out_shape=[jax.ShapeDtypeStruct(b, jnp.float32) for b, _ in blocks],
+        in_specs=[pl.BlockSpec(memory_space=pltpu.HBM)] * n,
+        out_specs=[pl.BlockSpec(memory_space=pltpu.VMEM)] * n,
+        scratch_shapes=[pltpu.VMEM((4, 2, 2) + b, t) for b, t in blocks]
+        + [pltpu.VMEM((4, 2, 2) + b, t) for b, t in blocks]
+        + [pltpu.VMEM((19,) + b, t) for b, t in blocks]
+        + [
+            pltpu.SemaphoreType.DMA((n, Scatter.NSEND + 1)),
+            pltpu.SemaphoreType.DMA((n, Scatter.NRECV)),
+        ],
+        compiler_params=pltpu.CompilerParams(
+            collective_id=3, has_side_effects=True, vmem_limit_bytes=VMEM_LIMIT
+        ),
+        name="scatter",
+    )(*parts)
+
+
+def states_kernel(reverse, through, value, out, met, planes, ready, send, recv):
+    me = lax.axis_index(AXIS)
+    z, r = me // 8, lax.rem(me, 8)
+    barrier = pltpu.get_barrier_semaphore()
+    plane = [z * 8 + lax.bitwise_xor(r, k) for k in range(8)]
+    level = [lax.rem(z + k, 4) * 8 + r for k in range(4)]
+    for peer in plane[1:] + level[1:]:
+        pl.semaphore_signal(barrier, inc=1, device_id=peer, device_id_type=LOGICAL)
+    pl.semaphore_wait(barrier, 10)
+
+    def copy(src, dst, k, peer):
+        return pltpu.make_async_remote_copy(
+            src_ref=src,
+            dst_ref=dst,
+            send_sem=send.at[k],
+            recv_sem=recv.at[k],
+            device_id=peer,
+            device_id_type=LOGICAL,
+        )
+
+    first = [copy(value.at[lax.bitwise_xor(r, k)], met.at[r], k, plane[k]) for k in range(1, 8)]
+    for one in first:
+        one.start()
+    met[r] = value[r]
+    for k in range(1, 8):
+        copy(value.at[0], met.at[lax.bitwise_xor(r, k)], k, plane[k]).wait_recv()
+    order = range(7, -1, -1) if reverse else range(8)
+    total = jnp.zeros(met.shape[1:], jnp.float32)
+    for i in order:
+        total = through[(z * 8 + i) * 8 + r] * total + met[i]
+    planes[z] = total
+    second = []
+    for k in range(1, 4):
+        far = z - k if reverse else z + k
+        cond = far >= 0 if reverse else far <= 3
+        made = copy(planes.at[z], planes.at[z], 7 + k, far * 8 + r)
+        second.append((made, cond))
+        pl.when(cond)(made.start)
+    ready[8] = jnp.zeros(met.shape[1:], jnp.float32)
+    for k in range(3, 0, -1):
+        far = z + k if reverse else z - k
+        cond = far <= 3 if reverse else far >= 0
+
+        @pl.when(cond)
+        def _():
+            copy(planes.at[z], planes.at[far], 7 + k, plane[0]).wait_recv()
+            kept = jnp.float32(1.0)
+            for i in range(8):
+                kept = kept * through[(far * 8 + i) * 8 + r]
+            ready[8] = kept * ready[8] + planes[far]
+
+    total = ready[8]
+    for i in order:
+        ready[i] = total
+        total = through[(z * 8 + i) * 8 + r] * total + met[i]
+    third = [
+        copy(ready.at[lax.bitwise_xor(r, k)], out.at[r], 10 + k, plane[k]) for k in range(1, 8)
+    ]
+    for one in third:
+        one.start()
+    out[r] = ready[r]
+    for k in range(1, 8):
+        copy(ready.at[0], out.at[lax.bitwise_xor(r, k)], 10 + k, plane[k]).wait_recv()
+    for one in first + third:
+        one.wait_send()
+    for made, cond in second:
+        pl.when(cond)(made.wait_send)
+
+
+def states(value, through, reverse):
+    tile = value.shape[1:]
+    return pl.pallas_call(
+        functools.partial(states_kernel, reverse),
+        out_shape=jax.ShapeDtypeStruct(value.shape, jnp.float32),
+        in_specs=[
+            pl.BlockSpec(memory_space=pltpu.SMEM),
+            pl.BlockSpec(memory_space=pltpu.VMEM),
+        ],
+        out_specs=pl.BlockSpec(memory_space=pltpu.VMEM),
+        scratch_shapes=[
+            pltpu.VMEM((8,) + tile, jnp.float32),
+            pltpu.VMEM((4,) + tile, jnp.float32),
+            pltpu.VMEM((9,) + tile, jnp.float32),
+            pltpu.SemaphoreType.DMA((18,)),
+            pltpu.SemaphoreType.DMA((18,)),
+        ],
+        compiler_params=pltpu.CompilerParams(
+            collective_id=2 if reverse else 1, has_side_effects=True, vmem_limit_bytes=16000000
+        ),
+        name="states_back" if reverse else "states",
+    )(through.reshape(-1), value)
 
 def entering(value, axis, combine, identity, reverse):
     length, here = (lax.axis_size(axis), lax.axis_index(axis))
@@ -100,7 +620,7 @@
     heads = decay_rate.shape[0]
     head_size = width // heads
     count = length // SPAN
-    first = lax.axis_index("fsdp") * length
+    first = lax.axis_index(AXIS) * length
     places = first + jnp.arange(length, dtype=jnp.int32)
     segments = segment_of(places, lengths, seq_order)
     before = segment_of(jnp.reshape(first - 1, (1,)), lengths, seq_order)[0]
@@ -108,17 +628,17 @@
         segments, before, decay_rate, SPAN
     )
     attention_set = (
-        lax.all_gather(w_query, "fsdp", axis=0, tiled=True),
-        lax.all_gather(w_key, "fsdp", axis=0, tiled=True),
-        lax.all_gather(w_value, "fsdp", axis=0, tiled=True),
-        lax.all_gather(w_unit, "fsdp", axis=0, tiled=True),
-        lax.all_gather(w_output, "fsdp", axis=0, tiled=True),
-        lax.all_gather(norm_gain, "fsdp", axis=0, tiled=True),
+        lax.all_gather(w_query, AXIS, axis=0, tiled=True),
+        lax.all_gather(w_key, AXIS, axis=0, tiled=True),
+        lax.all_gather(w_value, AXIS, axis=0, tiled=True),
+        lax.all_gather(w_unit, AXIS, axis=0, tiled=True),
+        lax.all_gather(w_output, AXIS, axis=0, tiled=True),
+        lax.all_gather(norm_gain, AXIS, axis=0, tiled=True),
     )
     feed_set = (
-        lax.all_gather(w_left, "fsdp", axis=0, tiled=True),
-        lax.all_gather(w_right, "fsdp", axis=0, tiled=True),
-        lax.all_gather(w_down, "fsdp", axis=0, tiled=True),
+        lax.all_gather(w_left, AXIS, axis=0, tiled=True),
+        lax.all_gather(w_right, AXIS, axis=0, tiled=True),
+        lax.all_gather(w_down, AXIS, axis=0, tiled=True),
     )
     full_query, full_key, full_value, full_unit, full_output, full_gain = attention_set
     full_left, full_right, full_down = feed_set
@@ -143,7 +663,7 @@
     local_states.append(passing[0][:, None, None] * local_states[-1] + increments[0])
     end_state = local_states[count]
     start_pair = (jnp.ones_like(through), jnp.zeros_like(end_state))
-    arriving = entering((through, end_state), "fsdp", chain_states, start_pair, False)[1]
+    arriving = entering((through, end_state), AXIS, chain_states, start_pair, False)[1]
     states = jnp.stack(local_states[:count]) + arrival[:, :, None, None] * arriving[None]
     state_low = states.astype(bf16)
     query_held = (query_blocks * entry[..., None]).astype(bf16)
@@ -165,9 +685,9 @@
     product = (left_pre * right_pre).astype(bf16)
     result = (middle + jnp.dot(product, full_down, preferred_element_type=f32)).astype(bf16)
     back_feed = (
-        lax.all_gather(w_left, "fsdp", axis=0, tiled=True),
-        lax.all_gather(w_right, "fsdp", axis=0, tiled=True),
-        lax.all_gather(w_down, "fsdp", axis=0, tiled=True),
+        lax.all_gather(w_left, AXIS, axis=0, tiled=True),
+        lax.all_gather(w_right, AXIS, axis=0, tiled=True),
+        lax.all_gather(w_down, AXIS, axis=0, tiled=True),
     )
     back_left, back_right, back_down = back_feed
     grad_product = jnp.einsum("td,fd->tf", cotangent, back_down, preferred_element_type=f32)
@@ -177,9 +697,9 @@
     grad_w_left = jnp.einsum("td,tf->df", second, grad_left_pre, preferred_element_type=f32)
     grad_w_right = jnp.einsum("td,tf->df", second, grad_right_pre, preferred_element_type=f32)
     feed_grads = (
-        lax.psum_scatter(grad_w_left, "fsdp", scatter_dimension=0, tiled=True),
-        lax.psum_scatter(grad_w_right, "fsdp", scatter_dimension=0, tiled=True),
-        lax.psum_scatter(grad_w_down, "fsdp", scatter_dimension=0, tiled=True),
+        lax.psum_scatter(grad_w_left, AXIS, scatter_dimension=0, tiled=True),
+        lax.psum_scatter(grad_w_right, AXIS, scatter_dimension=0, tiled=True),
+        lax.psum_scatter(grad_w_down, AXIS, scatter_dimension=0, tiled=True),
     )
     grad_second = jnp.einsum(
         "tf,df->td", grad_left_pre, back_left, preferred_element_type=f32
@@ -188,17 +708,17 @@
         grad_second - second_unit * jnp.mean(grad_second * second_unit, axis=-1, keepdims=True)
     )
     back_attention = (
-        lax.all_gather(w_query, "fsdp", axis=0, tiled=True),
-        lax.all_gather(w_key, "fsdp", axis=0, tiled=True),
-        lax.all_gather(w_value, "fsdp", axis=0, tiled=True),
-        lax.all_gather(w_unit, "fsdp", axis=0, tiled=True),
-        lax.all_gather(w_output, "fsdp", axis=0, tiled=True),
-        lax.all_gather(norm_gain, "fsdp", axis=0, tiled=True),
+        lax.all_gather(w_query, AXIS, axis=0, tiled=True),
+        lax.all_gather(w_key, AXIS, axis=0, tiled=True),
+        lax.all_gather(w_value, AXIS, axis=0, tiled=True),
+        lax.all_gather(w_unit, AXIS, axis=0, tiled=True),
+        lax.all_gather(w_output, AXIS, axis=0, tiled=True),
+        lax.all_gather(norm_gain, AXIS, axis=0, tiled=True),
     )
     back_query, back_key, back_value, back_unit, back_output, back_gain = back_attention
     grad_branch = grad_middle.astype(bf16)
-    grad_w_output = jnp.einsum("td,te->de", mixed_in, grad_branch, preferred_element_type=f32)
-    grad_mixed = jnp.einsum("te,de->td", grad_branch, back_output, preferred_element_type=f32)
+    grad_w_output = jnp.einsum(TD_TE, mixed_in, grad_branch, preferred_element_type=f32)
+    grad_mixed = jnp.einsum(TE_DE, grad_branch, back_output, preferred_element_type=f32)
     grad_gated = grad_mixed * unit_pre
     grad_unit_pre = (grad_mixed * gated).astype(bf16)
     grad_gain = jnp.sum(grad_gated * unit_norm, axis=0)
@@ -226,7 +746,7 @@
     )
     direct = jnp.einsum("nthe,nthf->nhef", query_held, grad_att_blocks, preferred_element_type=f32)
     leaving_sum = jnp.sum(arrival[:, :, None, None] * direct, axis=0)
-    later = entering((through, leaving_sum), "fsdp", chain_states, start_pair, True)[1]
+    later = entering((through, leaving_sum), AXIS, chain_states, start_pair, True)[1]
     next_grads = [later]
     grad_increment = jnp.stack(next_grads[::-1]).astype(bf16)
     grad_keys_held = jnp.einsum(
@@ -239,23 +759,23 @@
     grad_query_pre = (grad_query_blocks.reshape(length, width) * silu_slope(query_pre)).astype(bf16)
     grad_key_pre = (grad_key_blocks.reshape(length, width) * silu_slope(key_pre)).astype(bf16)
     grad_value_pre = grad_value_blocks.reshape(length, width).astype(bf16)
-    grad_w_query = jnp.einsum("td,te->de", hidden, grad_query_pre, preferred_element_type=f32)
-    grad_w_key = jnp.einsum("td,te->de", hidden, grad_key_pre, preferred_element_type=f32)
-    grad_w_value = jnp.einsum("td,te->de", hidden, grad_value_pre, preferred_element_type=f32)
-    grad_w_unit = jnp.einsum("td,te->de", hidden, grad_unit_pre, preferred_element_type=f32)
+    grad_w_query = jnp.einsum(TD_TE, hidden, grad_query_pre, preferred_element_type=f32)
+    grad_w_key = jnp.einsum(TD_TE, hidden, grad_key_pre, preferred_element_type=f32)
+    grad_w_value = jnp.einsum(TD_TE, hidden, grad_value_pre, preferred_element_type=f32)
+    grad_w_unit = jnp.einsum(TD_TE, hidden, grad_unit_pre, preferred_element_type=f32)
     attention_grads = (
-        lax.psum_scatter(grad_w_query, "fsdp", scatter_dimension=0, tiled=True),
-        lax.psum_scatter(grad_w_key, "fsdp", scatter_dimension=0, tiled=True),
-        lax.psum_scatter(grad_w_value, "fsdp", scatter_dimension=0, tiled=True),
-        lax.psum_scatter(grad_w_unit, "fsdp", scatter_dimension=0, tiled=True),
-        lax.psum_scatter(grad_w_output, "fsdp", scatter_dimension=0, tiled=True),
-        lax.psum_scatter(grad_gain, "fsdp", scatter_dimension=0, tiled=True),
+        lax.psum_scatter(grad_w_query, AXIS, scatter_dimension=0, tiled=True),
+        lax.psum_scatter(grad_w_key, AXIS, scatter_dimension=0, tiled=True),
+        lax.psum_scatter(grad_w_value, AXIS, scatter_dimension=0, tiled=True),
+        lax.psum_scatter(grad_w_unit, AXIS, scatter_dimension=0, tiled=True),
+        lax.psum_scatter(grad_w_output, AXIS, scatter_dimension=0, tiled=True),
+        lax.psum_scatter(grad_gain, AXIS, scatter_dimension=0, tiled=True),
     )
     grad_hidden = (
-        jnp.einsum("te,de->td", grad_query_pre, back_query, preferred_element_type=f32)
-        + jnp.einsum("te,de->td", grad_key_pre, back_key, preferred_element_type=f32)
-        + jnp.einsum("te,de->td", grad_value_pre, back_value, preferred_element_type=f32)
-        + jnp.einsum("te,de->td", grad_unit_pre, back_unit, preferred_element_type=f32)
+        jnp.einsum(TE_DE, grad_query_pre, back_query, preferred_element_type=f32)
+        + jnp.einsum(TE_DE, grad_key_pre, back_key, preferred_element_type=f32)
+        + jnp.einsum(TE_DE, grad_value_pre, back_value, preferred_element_type=f32)
+        + jnp.einsum(TE_DE, grad_unit_pre, back_unit, preferred_element_type=f32)
     )
     grad_inputs = grad_middle + first_scale * (
         grad_hidden - normed * jnp.mean(grad_hidden * normed, axis=-1, keepdims=True)
@@ -275,39 +795,241 @@
     )
 
 
+def body_kernels(
+    tokens,
+    lengths,
+    seq_order,
+    decay_rate,
+    w_query,
+    w_key,
+    w_value,
+    w_unit,
+    w_output,
+    norm_gain,
+    w_left,
+    w_right,
+    w_down,
+    cotangent,
+):
+    f32 = jnp.float32
+    bf16 = jnp.bfloat16
+    length, width = tokens.shape
+    heads = decay_rate.shape[0]
+    head_size = width // heads
+    count = length // SPAN
+    first = lax.axis_index(AXIS) * length
+    places = first + jnp.arange(length, dtype=jnp.int32)
+    segments = segment_of(places, lengths, seq_order)
+    before = segment_of(jnp.reshape(first - 1, (1,)), lengths, seq_order)[0]
+    within, entry, leaving, passing, arrival, through = decay_tables(
+        segments, before, decay_rate, SPAN
+    )
+    devices = lax.axis_size(AXIS)
+    me = lax.axis_index(AXIS)
+    mine = jnp.arange(devices, dtype=jnp.int32)[:, None] == me
+    gain_tile = jnp.where(mine, norm_gain.astype(f32)[None, :], 0.0).reshape(heads, head_size)
+    full = gather_all(
+        [w_query, w_key, w_value, w_unit, gain_tile, w_output]
+        + [w_left[:, : w_left.shape[1] // 2], w_left[:, w_left.shape[1] // 2 :]]
+        + [w_right[:, : w_right.shape[1] // 2], w_right[:, w_right.shape[1] // 2 :]]
+        + [w_down]
+    )
+    full_query, full_key, full_value, full_unit = [f.reshape(-1, width) for f in full[:4]]
+    full_gain = jnp.sum(full[4].reshape(devices, heads, head_size), axis=0).reshape(width)
+    full_output = full[5].reshape(-1, width)
+    full_left = jnp.concatenate([f.reshape(width, -1) for f in full[6:8]], axis=1)
+    full_right = jnp.concatenate([f.reshape(width, -1) for f in full[8:10]], axis=1)
+    full_down = full[10].reshape(-1, width)
+    ends = segment_of((jnp.arange(devices + 1, dtype=jnp.int32)) * length - 1, lengths, seq_order)
+    through_all = jnp.where(
+        (ends[1:] == ends[:-1])[:, None], jnp.exp(-decay_rate * length)[None, :], 0.0
+    )
+    inputs = tokens.astype(f32)
+    first_scale = row_scale(inputs)
+    normed = inputs * first_scale
+    hidden = normed.astype(bf16)
+    query_pre = jnp.dot(hidden, full_query, preferred_element_type=f32)
+    key_pre = jnp.dot(hidden, full_key, preferred_element_type=f32)
+    value_pre = jnp.dot(hidden, full_value, preferred_element_type=f32)
+    unit_pre = jnp.dot(hidden, full_unit, preferred_element_type=f32)
+    block_shape = (count, SPAN, heads, head_size)
+    query_blocks = jax.nn.silu(query_pre).astype(bf16).reshape(block_shape)
+    key_blocks = jax.nn.silu(key_pre).astype(bf16).reshape(block_shape)
+    value_blocks = value_pre.astype(bf16).reshape(block_shape)
+    scores = jnp.einsum("nthe,nshe->nhts", query_blocks, key_blocks, preferred_element_type=f32)
+    mixing = (scores * within).astype(bf16)
+    local_out = jnp.einsum("nhts,nshe->nthe", mixing, value_blocks, preferred_element_type=f32)
+    keys_held = (key_blocks * leaving[..., None]).astype(bf16)
+    increments = jnp.einsum("nshe,nshf->nhef", keys_held, value_blocks, preferred_element_type=f32)
+    local_states = [jnp.zeros((heads, head_size, head_size), f32)]
+    local_states.append(passing[0][:, None, None] * local_states[-1] + increments[0])
+    end_state = local_states[count]
+    arriving = states(end_state, through_all, False)
+    held = jnp.stack(local_states[:count]) + arrival[:, :, None, None] * arriving[None]
+    state_low = held.astype(bf16)
+    query_held = (query_blocks * entry[..., None]).astype(bf16)
+    attended = local_out + jnp.einsum(
+        "nthe,nhef->nthf", query_held, state_low, preferred_element_type=f32
+    )
+    attended_heads = attended.reshape(length, heads, head_size)
+    head_scale = row_scale(attended_heads)
+    unit_norm = (attended_heads * head_scale).reshape(length, width)
+    gain = full_gain.astype(f32)
+    gated = unit_norm * gain
+    mixed_in = (gated * unit_pre).astype(bf16)
+    middle = inputs + jnp.dot(mixed_in, full_output, preferred_element_type=f32)
+    second_scale = row_scale(middle)
+    second_unit = middle * second_scale
+    second = second_unit.astype(bf16)
+    left_pre = jnp.dot(second, full_left, preferred_element_type=f32)
+    right_pre = jnp.dot(second, full_right, preferred_element_type=f32)
+    product = (left_pre * right_pre).astype(bf16)
+    result = (middle + jnp.dot(product, full_down, preferred_element_type=f32)).astype(bf16)
+    back_left, back_right, back_down = full_left, full_right, full_down
+    grad_product = jnp.einsum("td,fd->tf", cotangent, back_down, preferred_element_type=f32)
+    grad_left_pre = (grad_product * right_pre).astype(bf16)
+    grad_right_pre = (grad_product * left_pre).astype(bf16)
+    grad_w_down = jnp.einsum("tf,td->fd", product, cotangent, preferred_element_type=f32)
+    grad_w_left = jnp.einsum("td,tf->df", second, grad_left_pre, preferred_element_type=f32)
+    grad_w_right = jnp.einsum("td,tf->df", second, grad_right_pre, preferred_element_type=f32)
+    grad_second = jnp.einsum(
+        "tf,df->td", grad_left_pre, back_left, preferred_element_type=f32
+    ) + jnp.einsum("tf,df->td", grad_right_pre, back_right, preferred_element_type=f32)
+    grad_middle = cotangent.astype(f32) + second_scale * (
+        grad_second - second_unit * jnp.mean(grad_second * second_unit, axis=-1, keepdims=True)
+    )
+    back_query, back_key, back_value, back_unit = full_query, full_key, full_value, full_unit
+    back_output, back_gain = full_output, full_gain
+    grad_branch = grad_middle.astype(bf16)
+    grad_w_output = jnp.einsum(TD_TE, mixed_in, grad_branch, preferred_element_type=f32)
+    grad_mixed = jnp.einsum(TE_DE, grad_branch, back_output, preferred_element_type=f32)
+    grad_gated = grad_mixed * unit_pre
+    grad_unit_pre = (grad_mixed * gated).astype(bf16)
+    grad_gain = jnp.sum(grad_gated * unit_norm, axis=0)
+    grad_norm_heads = (grad_gated * back_gain.astype(f32)).reshape(length, heads, head_size)
+    norm_heads = unit_norm.reshape(length, heads, head_size)
+    grad_att = head_scale * (
+        grad_norm_heads
+        - norm_heads * jnp.mean(grad_norm_heads * norm_heads, axis=-1, keepdims=True)
+    )
+    grad_att_blocks = grad_att.astype(bf16).reshape(block_shape)
+    grad_mixing = jnp.einsum(
+        "nthf,nshf->nhts", grad_att_blocks, value_blocks, preferred_element_type=f32
+    )
+    grad_scores = (grad_mixing * within).astype(bf16)
+    grad_query_blocks = (
+        jnp.einsum("nhts,nshe->nthe", grad_scores, key_blocks, preferred_element_type=f32)
+        + jnp.einsum("nthf,nhef->nthe", grad_att_blocks, state_low, preferred_element_type=f32)
+        * entry[..., None]
+    )
+    grad_key_blocks = jnp.einsum(
+        "nhts,nthe->nshe", grad_scores, query_blocks, preferred_element_type=f32
+    )
+    grad_value_blocks = jnp.einsum(
+        "nhts,nthf->nshf", mixing, grad_att_blocks, preferred_element_type=f32
+    )
+    direct = jnp.einsum("nthe,nthf->nhef", query_held, grad_att_blocks, preferred_element_type=f32)
+    leaving_sum = jnp.sum(arrival[:, :, None, None] * direct, axis=0)
+    later = states(leaving_sum, through_all, True)
+    next_grads = [later]
+    grad_increment = jnp.stack(next_grads[::-1]).astype(bf16)
+    grad_keys_held = jnp.einsum(
+        "nhef,nshf->nshe", grad_increment, value_blocks, preferred_element_type=f32
+    )
+    grad_key_blocks = grad_key_blocks + grad_keys_held * leaving[..., None]
+    grad_value_blocks = grad_value_blocks + jnp.einsum(
+        "nshe,nhef->nshf", keys_held, grad_increment, preferred_element_type=f32
+    )
+    grad_query_pre = (grad_query_blocks.reshape(length, width) * silu_slope(query_pre)).astype(bf16)
+    grad_key_pre = (grad_key_blocks.reshape(length, width) * silu_slope(key_pre)).astype(bf16)
+    grad_value_pre = grad_value_blocks.reshape(length, width).astype(bf16)
+    grad_w_query = jnp.einsum(TD_TE, hidden, grad_query_pre, preferred_element_type=f32)
+    grad_w_key = jnp.einsum(TD_TE, hidden, grad_key_pre, preferred_element_type=f32)
+    grad_w_value = jnp.einsum(TD_TE, hidden, grad_value_pre, preferred_element_type=f32)
+    grad_w_unit = jnp.einsum(TD_TE, hidden, grad_unit_pre, preferred_element_type=f32)
+    def blocks(grad):
+        return grad.astype(bf16).reshape((4, 2, 2, 2, -1) + grad.shape[1:])
+
+    gain_rows = grad_gain.reshape(devices, 1, width // devices)
+    gain_rows = jnp.pad(gain_rows, ((0, 0), (0, 7), (0, 128 - width // devices)))
+    split = w_left.shape[1] // 2
+    grads = scatter_all(
+        [blocks(grad_w_down)]
+        + [blocks(grad_w_left[:, :split]), blocks(grad_w_left[:, split:])]
+        + [blocks(grad_w_right[:, :split]), blocks(grad_w_right[:, split:])]
+        + [blocks(grad_w_output), gain_rows.reshape(4, 2, 2, 2, 8, 128)]
+        + [blocks(grad_w_unit), blocks(grad_w_value), blocks(grad_w_key), blocks(grad_w_query)]
+    )
+    feed_grads = (
+        jnp.concatenate(grads[1:3], axis=1),
+        jnp.concatenate(grads[3:5], axis=1),
+        grads[0],
+    )
+    attention_grads = (
+        grads[10],
+        grads[9],
+        grads[8],
+        grads[7],
+        grads[5],
+        grads[6][0, : width // devices],
+    )
+    grad_hidden = (
+        jnp.einsum(TE_DE, grad_query_pre, back_query, preferred_element_type=f32)
+        + jnp.einsum(TE_DE, grad_key_pre, back_key, preferred_element_type=f32)
+        + jnp.einsum(TE_DE, grad_value_pre, back_value, preferred_element_type=f32)
+        + jnp.einsum(TE_DE, grad_unit_pre, back_unit, preferred_element_type=f32)
+    )
+    grad_inputs = grad_middle + first_scale * (
+        grad_hidden - normed * jnp.mean(grad_hidden * normed, axis=-1, keepdims=True)
+    )
+    return (
+        result,
+        grad_inputs,
+        attention_grads[0],
+        attention_grads[1],
+        attention_grads[2],
+        attention_grads[3],
+        attention_grads[4],
+        attention_grads[5],
+        feed_grads[0],
+        feed_grads[1],
+        feed_grads[2],
+    )
+
+
 def solution(mesh):
     placed = (
-        P("fsdp", None),
+        P(AXIS, None),
         P(),
         P(),
         P(),
-        P("fsdp", None),
-        P("fsdp", None),
-        P("fsdp", None),
-        P("fsdp", None),
-        P("fsdp", None),
-        P("fsdp"),
-        P("fsdp", None),
-        P("fsdp", None),
-        P("fsdp", None),
-        P("fsdp", None),
+        P(AXIS, None),
+        P(AXIS, None),
+        P(AXIS, None),
+        P(AXIS, None),
+        P(AXIS, None),
+        P(AXIS),
+        P(AXIS, None),
+        P(AXIS, None),
+        P(AXIS, None),
+        P(AXIS, None),
     )
     return jax.shard_map(
-        body,
+        body_kernels if mesh.size == 32 else body,
         mesh=mesh,
         in_specs=placed,
         out_specs=(
-            P("fsdp", None),
-            P("fsdp", None),
-            P("fsdp", None),
-            P("fsdp", None),
-            P("fsdp", None),
-            P("fsdp", None),
-            P("fsdp", None),
-            P("fsdp"),
-            P("fsdp", None),
-            P("fsdp", None),
-            P("fsdp", None),
+            P(AXIS, None),
+            P(AXIS, None),
+            P(AXIS, None),
+            P(AXIS, None),
+            P(AXIS, None),
+            P(AXIS, None),
+            P(AXIS, None),
+            P(AXIS),
+            P(AXIS, None),
+            P(AXIS, None),
+            P(AXIS, None),
         ),
         check_vma=False,
     )

time: 1960 us -> 407 us (0.21)
  waiting for transfers between devices: 1560 us -> 0 us
  Pallas kernels: 0 us -> 287 us
  blocking collectives: 120 us -> 0 us
  other arithmetic: 88.6 us -> 18 us
  matrix products: 102 us -> 59.4 us
    reduce_scatter x8 -> x0, waiting for transfers between devices: 1050 us -> none  [the longest x1 155 us: body(): lax.psum_scatter(grad_w_down, 'fsdp', scatter_dimension=0, tiled=True)]
    all_gather x10 -> x0, waiting for transfers between devices: 513 us -> none  [the longest x2 149 us: entering(): everything = jax.tree.map(lambda part: lax.all_gather(part, axis), value)]
    pallas_call x0 -> x4, Pallas kernels: none -> 287 us  [the longest x1 119 us: gather_all(): pl.pallas_call(functools.partial(gather_kernel, n), out_shape=[jax.ShapeD...]
    unnamed x3 -> x0, blocking collectives: 120 us -> none
    select_n x64 -> x3, other arithmetic: 75 us -> 0.69 us  [the longest x1 0.61 us: body_kernels(): jnp.where(mine, norm_gain.astype(f32)[None, :], 0.0)]
    dot_general x36, matrix products: 102 us -> 59.4 us  [the longest x1 5.25 us: body_kernels(): jnp.einsum('tf,df->td', grad_right_pre, back_right, preferred_element_typ...]
    mul x67 -> x3, local copies, waits for them, and re-layouts: 28.7 us -> 3.9 us  [the longest x1 2.52 us: body_kernels(): grad_gated * back_gain.astype(f32)]
  transfers between devices with their start and end apart: 18 -> 0, of which waited for: 17 -> 0; matrix products, arithmetic and copies ran while one was open for 10% -> 0% of each run, Pallas kernels for 0% -> 0%
where the time goes in v1:
time: 407 us; the launch traced here: 402 us
  Pallas kernels  287 us (71%)
  matrix products  59.4 us (15%)
  local copies, waits for them, and re-layouts  34.5 us (8%)
  other arithmetic  18 us (4%)
    pallas_call x1, Pallas kernels, gather_all(): pl.pallas_call(functools.partial(gather_kernel, n), out_shape=[jax.ShapeD...  119 us
    pallas_call x1, Pallas kernels, scatter_all(): pl.pallas_call(functools.partial(scatter_kernel, n), out_shape=[jax.Shape...  117 us
    pallas_call x2, Pallas kernels, states(): pl.pallas_call(functools.partial(states_kernel, reverse), out_shape=jax.S...  51.1 us
    unnamed x84, local copies, waits for them, and re-layouts  14.1 us

profile of v1, /device:TPU:0, one launch (start us, length us, event | category | flops | bytes accessed | tf_op | source)
XLA Modules:
  0.0 402.1 jit_solution(11622152842186784310)
XLA Ops:
  0.7 0.9 select_reduce_fusion
  3.2 1.2 fusion.19
  8.4 1.8 fusion.70
  10.1 119.2 %gather.1 = (bf16[4,2,2,2,32,1024]{5,4,3,2,1,0:T(8,128)(2,1)}, bf16[4,2,2,2,32,1024]{5,4,3,2,1,0:T(8,128)(2,1)}, bf16[4,2,2,2,32,1024]{5,4,3,2,1,0:T(8,128)(2,1)...) custom-call(bf16[32,1024]{1,0:T(8,128)(2,1)} %refs_0_.1, ...), custom_call_target="tpu_custom_call" | custom-call | tf_op jit(solution)/shard_map/gather/pallas_call | solution.py:226
  129.3 1.1 reduce_sum.129
  130.4 2.5 fusion.14
  133.0 0.8 fusion.63
  133.8 1.0 copy-done.3
  135.0 0.9 convolution_add_fusion.6.value
  136.0 19.6 %states.1 = f32[8,128,128]{2,1,0:T(8,128)S(1)} custom-call(f32[256]{0:T(256)S(1)} %select_n.96.through, f32[8,128,128]{2,1,0:T(8,128)S(1)} %convolution_add_fusion.6.value), custom_call_target="tpu_custom_call" | custom-call | tf_op jit(solution)/shard_map/states/pallas_call | solution.py:511
  155.6 1.8 multiply_convert_fusion.12
  157.6 0.7 multiply_convert_fusion.4
  159.4 1.3 copy.82
  160.8 1.3 copy.83
  162.1 3.1 multiply_convert_fusion.8
  165.3 0.8 multiply_reduce_fusion.2
  166.3 1.0 copy-done.35
  167.3 0.9 copy-done.36
  168.2 1.7 fusion.1
  170.2 0.9 copy-done.34
  171.0 1.7 fusion.3
  173.0 1.8 multiply_convert_fusion.1
  174.9 5.2 %fusion = f32[256,1024]{1,0:T(8,128)S(1)} fusion(bf16[256,2816]{1,0:T(8,128)(2,1)S(1)} %get-tuple-element.65, bf16[1024,1408]{1,0:T(8,128)(2,1)} %bitcast.212, bf16[1024,1408]{1,0:T(8,128)(2,1)} %bitcast.210), kind=kOutput, calls=%fused_computation.6 | convolution fusion | flops 1487929344 | bytes 8257536 | tf_op jit(solution)/shard_map/tf,df->td/dot_general | solution.py:897
  180.1 2.5 fusion.12
  182.6 1.8 multiply_reduce_fusion.1
  184.7 2.1 multiply_reduce_fusion
  186.9 0.7 pad.4
  187.5 2.5 copy.85
  190.1 1.5 fusion.22
  191.6 1.5 fusion.27
  193.7 31.5 %states_back.1 = f32[8,128,128]{2,1,0:T(8,128)S(1)} custom-call(f32[256]{0:T(256)S(1)} %select_n.96.through, f32[8,128,128]{2,1,0:T(8,128)S(1)} %convolution_multiply_fusion.value), custom_call_target="tpu_custom_call" | custom-call | tf_op jit(solution)/shard_map/states_back/pallas_call | solution.py:511
  225.2 1.4 fusion.13
  226.6 0.7 multiply_convert_fusion.3
  227.6 1.3 fusion.11
  229.8 1.3 copy.105
  231.1 1.9 multiply_convert_fusion.7
  233.0 3.4 fusion.72
  236.4 2.5 copy.106
  238.9 1.8 multiply_convert_fusion.6
  240.8 2.1 convolution_add_fusion.4
  243.0 0.8 convolution_add_fusion.3
  243.8 0.8 copy-done.9
  244.7 0.9 fusion.15
  245.6 1.3 fusion.18
  246.8 2.1 convolution_convert_fusion.7
  248.9 2.2 convolution_convert_fusion.6
  251.1 2.2 convolution_convert_fusion.5
  253.4 2.2 convolution_convert_fusion.4
  255.6 2.2 convolution_convert_fusion.3
  257.7 4.4 %convolution_convert_fusion.2 = bf16[2816,1024]{1,0:T(8,128)(2,1)} fusion(bf16[256,2816]{1,0:T(8,128)(2,1)S(1)} %copy-done.2, bf16[256,1024]{1,0:T(8,128)(2,1)S(1)} %copy-done.24), kind=kOutput, calls=%fused_computation.4 | convolution fusion | flops 1479278592 | bytes 7733248 | tf_op jit(solution)/shard_map/tf,td->fd/dot_general | solution.py:892
  262.1 1.7 convolution_convert_fusion.1
  263.9 3.0 fusion.69
  266.8 1.7 convolution_convert_fusion
  268.6 2.9 fusion.68
  271.5 117.1 %scatter.1 = (f32[88,1024]{1,0:T(8,128)}, f32[32,1408]{1,0:T(8,128)}, f32[32,1408]{1,0:T(8,128)}, f32[32,1408]{1,0:T(8,128)}, f32[32,1408]{1,0:T(8,128)}, /*inde...) custom-call(bf16[4,2,2,2,88,1024]{5,4,3,2,1,0:T(8,128)(2,1)} %bitcas, ...), custom_call_target="tpu_custom_call" | custom-call | tf_op jit(solution)/shard_map/scatter/pallas_call | solution.py:421
  388.6 1.2 slice_bitcast_fusion
  389.8 1.8 pad_maximum_fusion.8
  391.6 1.8 pad_maximum_fusion.9
  393.3 1.6 copy.148
  394.9 1.6 copy.149
  396.5 1.6 copy.150
  398.1 1.6 copy.151
  399.6 1.6 copy.152
  401.2 0.7 copy.153
  (118 shorter events, 9.1 us)
Async XLA Ops:
  4.4 128.5 %copy-start = (bf16[256,1024]{1,0:T(8,128)(2,1)S(1)}, bf16[256,1024]{1,0:T(8,128)(2,1)}, u32[]{:S(2)}) copy-start(bf16[256,1024]{1,0:T(8,128)(2,1)} %param.14) | copy-start | bytes 1572868
  129.3 3.7 copy-start.10
  133.0 3.0 copy-start.29
  133.7 1.0 copy-start.3
  134.7 20.9 %copy-start.27 = (bf16[4,2,2,2,32,1024]{5,4,3,2,1,0:T(8,128)(2,1)S(1)}, bf16[4,2,2,2,32,1024]{5,4,3,2,1,0:T(8,128)(2,1)}, u32[]{:S(2)}) copy-start(bf16[4,2,2,2,32,1024]{5,4,3,2,1,0:T(8,128)(2,1)} %get-tuple-element.34) | copy-start | bytes 6291460
  135.0 22.6 %copy-start.19 = (bf16[32,8,8,128]{3,2,1,0:T(8,128)(2,1)}, bf16[32,8,8,128]{3,2,1,0:T(8,128)(2,1)S(1)}, u32[]{:S(2)}) copy-start(bf16[32,8,8,128]{3,2,1,0:T(8,128)(2,1)S(1)} %fusion.35) | copy-start | bytes 1572868
  157.4 1.0 copy-start.30
  157.6 1.3 copy-start.13
  158.4 1.0 copy-start.25
  162.1 3.1 copy-start.12
  165.3 0.9 copy-start.17
  165.3 2.0 copy-start.35
  165.3 2.9 copy-start.36
  168.2 1.7 copy-start.15
  168.2 2.0 copy-start.33
  168.2 2.9 copy-start.34
  168.2 4.6 %slice-start = ((s8[5767168]{0:T(1024)(128)(4,1)}), s8[4194304]{0:T(1024)(128)(4,1)S(1)}, s32[]{:S(2)}) async-start(s8[5767168]{0:T(1024)(128)(4,1)} %bitcast.167), calls=%async_computation | async-start | bytes 8388608
  171.0 1.9 slice-start.1
  171.0 1.9 copy-start.23
  174.8 5.3 %copy-start.5 = (bf16[256,2816]{1,0:T(8,128)(2,1)}, bf16[256,2816]{1,0:T(8,128)(2,1)S(1)}, u32[]{:S(2)}) copy-start(bf16[256,2816]{1,0:T(8,128)(2,1)S(1)} %get-tuple-element.65) | copy-start | bytes 4325380
  174.8 5.3 %copy-start.1 = (bf16[256,2816]{1,0:T(8,128)(2,1)}, bf16[256,2816]{1,0:T(8,128)(2,1)S(1)}, u32[]{:S(2)}) copy-start(bf16[256,2816]{1,0:T(8,128)(2,1)S(1)} %get-tuple-element.64) | copy-start | bytes 4325380
  174.8 7.7 %copy-start.7 = (bf16[256,2816]{1,0:T(8,128)(2,1)}, bf16[256,2816]{1,0:T(8,128)(2,1)S(1)}, u32[]{:S(2)}) copy-start(bf16[256,2816]{1,0:T(8,128)(2,1)S(1)} %get-tuple-element.63) | copy-start | bytes 4325380
  190.1 3.0 copy-start.26
  191.5 1.8 copy-start.14
  193.0 32.2 %copy-start.20 = (bf16[32,8,8,128]{3,2,1,0:T(8,128)(2,1)S(1)}, bf16[32,8,8,128]{3,2,1,0:T(8,128)(2,1)}, u32[]{:S(2)}) copy-start(bf16[32,8,8,128]{3,2,1,0:T(8,128)(2,1)} %copy-done.19) | copy-start | bytes 1572868
  193.4 33.2 %copy-start.31 = (bf16[32,8,8,128]{3,2,1,0:T(8,128)(2,1)S(1)}, bf16[32,8,8,128]{3,2,1,0:T(8,128)(2,1)}, u32[]{:S(2)}) copy-start(bf16[32,8,8,128]{3,2,1,0:T(8,128)(2,1)} %copy-done.29) | copy-start | bytes 1572868
  233.0 5.9 %copy-start.4 = (f32[256,1024]{1,0:T(8,128)S(1)}, f32[256,1024]{1,0:T(8,128)}, u32[]{:S(2)}) copy-start(f32[256,1024]{1,0:T(8,128)} %copy-done.3) | copy-start | bytes 3145732
  238.9 1.9 copy-start.11
  240.8 2.1 copy-start.21
  240.8 2.2 copy-start.28
  243.0 1.6 copy-start.9
  243.0 1.7 copy-start.22
  245.6 1.3 copy-start.18
  253.3 4.4 %copy-start.2 = (bf16[256,2816]{1,0:T(8,128)(2,1)S(1)}, bf16[256,2816]{1,0:T(8,128)(2,1)}, u32[]{:S(2)}) copy-start(bf16[256,2816]{1,0:T(8,128)(2,1)} %copy-done.1) | copy-start | bytes 4325380
  253.3 4.4 %copy-start.24 = (bf16[256,1024]{1,0:T(8,128)(2,1)S(1)}, bf16[256,1024]{1,0:T(8,128)(2,1)}, u32[]{:S(2)}) copy-start(bf16[256,1024]{1,0:T(8,128)(2,1)} %param.27) | copy-start | bytes 1572868
  257.7 4.4 %copy-start.8 = (bf16[256,2816]{1,0:T(8,128)(2,1)S(1)}, bf16[256,2816]{1,0:T(8,128)(2,1)}, u32[]{:S(2)}) copy-start(bf16[256,2816]{1,0:T(8,128)(2,1)} %copy-done.7) | copy-start | bytes 4325380
  257.7 4.4 %copy-start.16 = (bf16[256,1024]{1,0:T(8,128)(2,1)S(1)}, bf16[256,1024]{1,0:T(8,128)(2,1)}, u32[]{:S(2)}) copy-start(bf16[256,1024]{1,0:T(8,128)(2,1)} %copy-done.15) | copy-start | bytes 1572868
  263.9 3.0 copy-start.6
  388.6 12.6 %copy-start.32 = (f32[88,1024]{1,0:T(8,128)S(1)}, f32[88,1024]{1,0:T(8,128)}, u32[]{:S(2)}) copy-start(f32[88,1024]{1,0:T(8,128)} %get-tuple-element.115) | copy-start | bytes 1081348

commit v2 on v1

--- a/solution.py
+++ b/solution.py
@@ -204,41 +204,6 @@
                 pl.when(cond)(made.wait_send)
 
 
-def gather_kernel(n, *refs):
-    own, full = refs[:n], refs[n : 2 * n]
-    send, recv = refs[2 * n :]
-    place = Place()
-    greet(place)
-    made = [Gather(place, own[i], full[i], send, recv, i) for i in range(n)]
-    for step in range(n + 5):
-        for r in range(6):
-            i = step - r
-            if 0 <= i < n:
-                made[i].round(r)
-    for one in made:
-        one.pairs()
-    for one in made:
-        one.finish()
-
-
-def gather_all(shards):
-    n = len(shards)
-    return pl.pallas_call(
-        functools.partial(gather_kernel, n),
-        out_shape=[jax.ShapeDtypeStruct((4, 2, 2, 2) + s.shape, s.dtype) for s in shards],
-        in_specs=[pl.BlockSpec(memory_space=pltpu.VMEM)] * n,
-        out_specs=[pl.BlockSpec(memory_space=pltpu.HBM)] * n,
-        scratch_shapes=[
-            pltpu.SemaphoreType.DMA((n, Gather.NSEND + 1)),
-            pltpu.SemaphoreType.DMA((n, Gather.NRECV)),
-        ],
-        compiler_params=pltpu.CompilerParams(
-            collective_id=0, has_side_effects=True, vmem_limit_bytes=VMEM_LIMIT
-        ),
-        name="gather",
-    )(*shards)
-
-
 def add_into(out, parts):
     rows = out.shape[0]
     step = 8 if rows % 16 else 16
@@ -528,6 +493,373 @@
         ),
         name="states_back" if reverse else "states",
     )(through.reshape(-1), value)
+
+
+def bounds_of(lengths, order):
+    total, found = jnp.int32(0), []
+    for j in range(lengths.shape[0]):
+        total = total + lengths[order[j]]
+        found.append(total)
+    return found
+
+
+def segment_at(bounds, places):
+    found = jnp.zeros_like(places)
+    for bound in bounds:
+        found = found + jnp.where(bound <= places, 1, 0)
+    return found
+
+
+def same_segment(bounds, earlier, later):
+    same = jnp.int32(0)
+    for bound in bounds:
+        same = same + jnp.where((bound <= earlier) != (bound <= later), 1, 0)
+    return jnp.where((earlier >= 0) & (same == 0), 1.0, 0.0).astype(jnp.float32)
+
+
+def spans_of(first, bounds, dist, entry, leaving):
+    size = dist.shape[0]
+    t = lax.broadcasted_iota(jnp.int32, (size, size), 0)
+    s = lax.broadcasted_iota(jnp.int32, (size, size), 1)
+    same = segment_at(bounds, t + first) == segment_at(bounds, s + first)
+    dist[...] = jnp.where(same & (s <= t), t - s, -1).astype(jnp.float32)
+    t = lax.broadcasted_iota(jnp.int32, entry.shape, 0)
+    here = segment_at(bounds, t + first)
+    ahead = segment_at(bounds, jnp.full(entry.shape, first - 1, jnp.int32))
+    ahead = jnp.where(jnp.full(entry.shape, first, jnp.int32) == 0, -1, ahead)
+    last = segment_at(bounds, jnp.full(entry.shape, first + size - 1, jnp.int32))
+    entry[...] = jnp.where(here == ahead, t, -1).astype(jnp.float32)
+    leaving[...] = jnp.where(here == last, size - t, -1).astype(jnp.float32)
+
+
+def decay(distance, rate):
+    return jnp.where(distance >= 0, jnp.exp(-rate * distance), 0.0)
+
+
+def mm(a, b):
+    return jnp.dot(a, b, preferred_element_type=jnp.float32)
+
+
+def mm_nt(a, b):
+    return lax.dot_general(a, b, (((1,), (1,)), ((), ())), preferred_element_type=jnp.float32)
+
+
+def mm_tn(a, b):
+    return lax.dot_general(a, b, (((0,), (0,)), ((), ())), preferred_element_type=jnp.float32)
+
+
+def head_of(h):
+    return pl.ds(pl.multiple_of(h * 128, 128), 128)
+
+
+def norm_scale(values):
+    return lax.rsqrt(jnp.mean(values * values, axis=-1, keepdims=True) + EPSILON)
+
+
+class States:
+    PEERS = 10
+
+    def __init__(self, place, bounds, rate, reverse, value, met, planes, ready, out, send, recv):
+        self.bounds, self.reverse = bounds, reverse
+        self.value, self.met, self.planes, self.ready, self.out = value, met, planes, ready, out
+        self.send, self.recv = send, recv
+        self.z, self.r = place.z, lax.rem(place.me, 8)
+        self.plane = [self.z * 8 + lax.bitwise_xor(self.r, k) for k in range(8)]
+        self.level = [lax.rem(self.z + k, 4) * 8 + self.r for k in range(4)]
+        self.order = range(7, -1, -1) if reverse else range(8)
+        self.step = jnp.exp(jnp.full((1, 128), -SPAN * rate[self.r], jnp.float32))
+
+    def through(self, device):
+        return same_segment(self.bounds, device * SPAN - 1, device * SPAN + SPAN - 1)
+
+    def copy(self, src, dst, k, peer):
+        return pltpu.make_async_remote_copy(
+            src_ref=src,
+            dst_ref=dst,
+            send_sem=self.send.at[k],
+            recv_sem=self.recv.at[k],
+            device_id=peer,
+            device_id_type=LOGICAL,
+        )
+
+    def other(self, k):
+        return lax.bitwise_xor(self.r, k)
+
+    def spread(self):
+        self.first = [
+            self.copy(self.value.at[self.other(k)], self.met.at[self.r], k, self.plane[k])
+            for k in range(1, 8)
+        ]
+        for one in self.first:
+            one.start()
+        self.met[self.r] = self.value[self.r]
+
+    def total(self):
+        for k in range(1, 8):
+            self.copy(self.value.at[0], self.met.at[self.other(k)], k, self.plane[k]).wait_recv()
+        total = jnp.zeros(self.met.shape[1:], jnp.float32)
+        for i in self.order:
+            total = self.through(self.z * 8 + i) * self.step * total + self.met[i]
+        self.planes[self.z] = total
+        self.second = []
+        for k in range(1, 4):
+            far = self.z - k if self.reverse else self.z + k
+            cond = far >= 0 if self.reverse else far <= 3
+            made = self.copy(
+                self.planes.at[self.z], self.planes.at[self.z], 7 + k, far * 8 + self.r
+            )
+            self.second.append((made, cond))
+            pl.when(cond)(made.start)
+
+    def back(self):
+        self.ready[8] = jnp.zeros(self.met.shape[1:], jnp.float32)
+        for k in range(3, 0, -1):
+            far = self.z + k if self.reverse else self.z - k
+            cond = far <= 3 if self.reverse else far >= 0
+
+            @pl.when(cond)
+            def _():
+                self.copy(
+                    self.planes.at[self.z], self.planes.at[far], 7 + k, self.plane[0]
+                ).wait_recv()
+                kept = jnp.ones((1, 128), jnp.float32)
+                for i in range(8):
+                    kept = kept * (self.through(far * 8 + i) * self.step)
+                self.ready[8] = kept * self.ready[8] + self.planes[far]
+
+        total = self.ready[8]
+        for i in self.order:
+            self.ready[i] = total
+            total = self.through(self.z * 8 + i) * self.step * total + self.met[i]
+        self.third = [
+            self.copy(self.ready.at[self.other(k)], self.out.at[self.r], 10 + k, self.plane[k])
+            for k in range(1, 8)
+        ]
+        for one in self.third:
+            one.start()
+        self.out[self.r] = self.ready[self.r]
+
+    def done(self):
+        for k in range(1, 8):
+            self.copy(self.ready.at[0], self.out.at[self.other(k)], 10 + k, self.plane[k]).wait_recv()
+
+    def finish(self):
+        for one in self.first + self.third:
+            one.wait_send()
+        for made, cond in self.second:
+            pl.when(cond)(made.wait_send)
+
+
+def greet_more(place):
+    barrier = pltpu.get_barrier_semaphore()
+    r = lax.rem(place.me, 8)
+    peers = [place.z * 8 + lax.bitwise_xor(r, k) for k in range(1, 8)]
+    peers += [lax.rem(place.z + k, 4) * 8 + r for k in range(1, 4)]
+    for peer in peers:
+        pl.semaphore_signal(barrier, inc=1, device_id=peer, device_id_type=LOGICAL)
+    pl.semaphore_wait(barrier, len(peers))
+
+
+def forward_kernel(
+    lengths,
+    order,
+    rate,
+    tokens,
+    gain_own,
+    s_key,
+    s_value,
+    s_query,
+    s_unit,
+    s_output,
+    s_left,
+    s_right,
+    s_down,
+    *refs,
+):
+    f32, bf16 = jnp.float32, jnp.bfloat16
+    n = 11
+    full, refs = refs[:n], refs[n:]
+    saved, refs = refs[:16], refs[16:]
+    kept, refs = refs[:16], refs[16:]
+    (hidden, keys, values, queries, key_pre, query_pre, unit_pre, probs) = kept[:8]
+    (attended, state_low, mixed, middle, second, left, right, product) = kept[8:]
+    (dist, entry, leaving, gains, gain, value, met, planes, ready, arriving) = refs[:10]
+    (narrow, wide, send, recv, state_send, state_recv, load_sem, save_sem) = refs[10:]
+    place = Place()
+    half = s_left.shape[1] // 2
+    own = [s_key, s_value, s_query, s_unit, gain_own, s_output]
+    own += [s_left.at[:, pl.ds(0, half)], s_left.at[:, pl.ds(half, half)]]
+    own += [s_right.at[:, pl.ds(0, half)], s_right.at[:, pl.ds(half, half)], s_down]
+    greet_more(place)
+    made = [Gather(place, own[i], full[i], send, recv, i) for i in range(n)]
+    bounds = bounds_of(lengths, order)
+    states = States(
+        place, bounds, rate, False, value, met, planes, ready, arriving, state_send, state_recv
+    )
+    slots = {0: narrow.at[0], 1: narrow.at[1], 2: narrow.at[0], 3: narrow.at[1], 4: gains}
+    slots.update({5: narrow.at[0], 6: wide.at[0], 7: wide.at[1], 8: wide.at[0], 9: wide.at[1]})
+    saves = []
+
+    def save(*numbers):
+        for i in numbers:
+            copy = pltpu.make_async_copy(kept[i], saved[i], save_sem.at[i])
+            copy.start()
+            saves.append(copy)
+
+    def weight(i):
+        ref = slots[i]
+        return ref[...].reshape(-1, ref.shape[-1])
+
+    def start():
+        x = tokens[...].astype(f32)
+        hidden[...] = (x * norm_scale(x)).astype(bf16)
+        spans_of(place.me * SPAN, bounds, dist, entry, leaving)
+        save(0)
+
+    def project(i, pre, low):
+        out = mm(hidden[...], weight(i))
+        if pre is not None:
+            pre[...] = out
+            out = out / (1.0 + jnp.exp(-out))
+        low[...] = out.astype(bf16)
+
+    def key():
+        project(0, key_pre, keys)
+        save(1, 4)
+
+    def increments():
+        project(1, None, values)
+
+        @pl.loop(0, 8)
+        def _(h):
+            at = head_of(h)
+            held = (keys[:, at].astype(f32) * decay(leaving[...], rate[h])).astype(bf16)
+            value[h] = mm_tn(held, values[:, at])
+
+        states.spread()
+        save(2)
+
+    def query():
+        project(2, query_pre, queries)
+
+        @pl.loop(0, 8)
+        def _(h):
+            at = head_of(h)
+            scores = mm_nt(queries[:, at], keys[:, at])
+            low = (scores * decay(dist[...], rate[h])).astype(bf16)
+            probs[h] = low
+            attended[:, at] = mm(low, values[:, at])
+
+        save(3, 5, 7)
+
+    def unit():
+        unit_pre[...] = mm(hidden[...], weight(3))
+        save(6)
+
+    def attend():
+        gain[...] = jnp.sum(gains[...].reshape(-1, 8, 128), axis=0)
+
+        @pl.loop(0, 8)
+        def _(h):
+            at = head_of(h)
+            low = arriving[h].astype(bf16)
+            state_low[h] = low
+            held = (queries[:, at].astype(f32) * decay(entry[...], rate[h])).astype(bf16)
+            out = attended[:, at] + mm(held, low)
+            attended[:, at] = out
+            mixed[:, at] = (
+                out * norm_scale(out) * gain[pl.ds(h, 1), :] * unit_pre[:, at]
+            ).astype(bf16)
+
+        save(8, 9, 10)
+
+    def output():
+        out = tokens[...].astype(f32) + mm(mixed[...], weight(5))
+        middle[...] = out
+        second[...] = (out * norm_scale(out)).astype(bf16)
+        save(11, 12)
+
+    def gate(i, side, part):
+        side[:, pl.ds(part * half, half)] = mm(second[...], weight(i))
+
+    def multiply():
+        @pl.loop(0, SPAN // 16)
+        def _(i):
+            at = pl.ds(pl.multiple_of(i * 16, 16), 16)
+            product[at, :] = (left[at, :] * right[at, :]).astype(bf16)
+
+        save(13, 14, 15)
+
+    tasks = {0: [start], 7: [key], 8: [increments], 9: [states.total, query], 10: [states.back, unit]}
+    tasks[11] = [states.done, attend]
+    tasks[12] = [output]
+    tasks[13] = [lambda: gate(6, left, 0)]
+    tasks[14] = [lambda: gate(7, left, 1)]
+    tasks[15] = [lambda: gate(8, right, 0)]
+    tasks[16] = [lambda: gate(9, right, 1), multiply]
+    loads = {}
+    for step in range(n + 6):
+        for r in range(6):
+            if 0 <= step - r < n:
+                made[step - r].round(r)
+        i = step - 6
+        if 0 <= i < n:
+            made[i].pairs()
+        if i - 1 in loads:
+            loads[i - 1].wait()
+        if i in slots:
+            loads[i] = pltpu.make_async_copy(full[i], slots[i], load_sem.at[i])
+            loads[i].start()
+        for task in tasks.get(step, []):
+            task()
+    for one in made:
+        one.finish()
+    states.finish()
+    for copy in saves:
+        copy.wait()
+
+
+def forward(lengths, order, rate, tokens, gain_tile, shards):
+    f32, bf16 = jnp.float32, jnp.bfloat16
+    size, width = tokens.shape
+    wide = shards[5].shape[1]
+    half = wide // 2
+    blocks = [(s.shape, s.dtype) for s in shards[:4]] + [(gain_tile.shape, f32)]
+    blocks += [(shards[4].shape, bf16)] + [((32, half), bf16)] * 4 + [(shards[7].shape, bf16)]
+    square, cube = (size, width), (8, 128, 128)
+    kept = [(square, bf16)] * 4 + [(square, f32)] * 3 + [((8, size, size), bf16)]
+    kept += [(square, f32), (cube, bf16), (square, bf16), (square, f32), (square, bf16)]
+    kept += [((size, wide), f32)] * 2 + [((size, wide), bf16)]
+    vmem, hbm = pl.BlockSpec(memory_space=pltpu.VMEM), pl.BlockSpec(memory_space=pltpu.HBM)
+    smem = pl.BlockSpec(memory_space=pltpu.SMEM)
+    n = len(blocks)
+    out = pl.pallas_call(
+        forward_kernel,
+        out_shape=[jax.ShapeDtypeStruct((4, 2, 2, 2) + s, t) for s, t in blocks]
+        + [jax.ShapeDtypeStruct(s, t) for s, t in kept],
+        in_specs=[smem] * 3 + [vmem] * 10,
+        out_specs=[hbm] * (n + len(kept)),
+        scratch_shapes=[pltpu.VMEM(s, t) for s, t in kept]
+        + [pltpu.VMEM((size, size), f32), pltpu.VMEM((size, 128), f32), pltpu.VMEM((size, 128), f32)]
+        + [pltpu.VMEM((4, 2, 2, 2, 8, 128), f32), pltpu.VMEM((8, 128), f32)]
+        + [pltpu.VMEM(cube, f32), pltpu.VMEM(cube, f32), pltpu.VMEM((4, 128, 128), f32)]
+        + [pltpu.VMEM((9, 128, 128), f32), pltpu.VMEM(cube, f32)]
+        + [
+            pltpu.VMEM((2, 4, 2, 2, 2, 32, width), bf16),
+            pltpu.VMEM((2, 4, 2, 2, 2, 32, half), bf16),
+            pltpu.SemaphoreType.DMA((n, Gather.NSEND + 1)),
+            pltpu.SemaphoreType.DMA((n, Gather.NRECV)),
+            pltpu.SemaphoreType.DMA((18,)),
+            pltpu.SemaphoreType.DMA((18,)),
+            pltpu.SemaphoreType.DMA((n,)),
+            pltpu.SemaphoreType.DMA((len(kept),)),
+        ],
+        compiler_params=pltpu.CompilerParams(
+            collective_id=0, has_side_effects=True, vmem_limit_bytes=VMEM_LIMIT
+        ),
+        name="forward",
+    )(lengths, order, rate, tokens, gain_tile, *shards)
+    return out[:n], out[n:]
 
 def entering(value, axis, combine, identity, reverse):
     length, here = (lax.axis_size(axis), lax.axis_index(axis))
@@ -828,13 +1160,15 @@
     me = lax.axis_index(AXIS)
     mine = jnp.arange(devices, dtype=jnp.int32)[:, None] == me
     gain_tile = jnp.where(mine, norm_gain.astype(f32)[None, :], 0.0).reshape(heads, head_size)
-    full = gather_all(
-        [w_query, w_key, w_value, w_unit, gain_tile, w_output]
-        + [w_left[:, : w_left.shape[1] // 2], w_left[:, w_left.shape[1] // 2 :]]
-        + [w_right[:, : w_right.shape[1] // 2], w_right[:, w_right.shape[1] // 2 :]]
-        + [w_down]
-    )
-    full_query, full_key, full_value, full_unit = [f.reshape(-1, width) for f in full[:4]]
+    full, kept = forward(
+        lengths,
+        seq_order,
+        decay_rate,
+        tokens,
+        gain_tile,
+        [w_key, w_value, w_query, w_unit, w_output, w_left, w_right, w_down],
+    )
+    full_key, full_value, full_query, full_unit = [f.reshape(-1, width) for f in full[:4]]
     full_gain = jnp.sum(full[4].reshape(devices, heads, head_size), axis=0).reshape(width)
     full_output = full[5].reshape(-1, width)
     full_left = jnp.concatenate([f.reshape(width, -1) for f in full[6:8]], axis=1)
@@ -844,46 +1178,24 @@
     through_all = jnp.where(
         (ends[1:] == ends[:-1])[:, None], jnp.exp(-decay_rate * length)[None, :], 0.0
     )
+    hidden, keys, values, queries, key_pre, query_pre, unit_pre, mixing = kept[:8]
+    attended, state_low, mixed_in, middle, second, left_pre, right_pre, product = kept[8:]
+    block_shape = (count, SPAN, heads, head_size)
+    query_blocks = queries.reshape(block_shape)
+    key_blocks = keys.reshape(block_shape)
+    value_blocks = values.reshape(block_shape)
+    mixing, state_low = mixing[None], state_low[None]
     inputs = tokens.astype(f32)
     first_scale = row_scale(inputs)
     normed = inputs * first_scale
-    hidden = normed.astype(bf16)
-    query_pre = jnp.dot(hidden, full_query, preferred_element_type=f32)
-    key_pre = jnp.dot(hidden, full_key, preferred_element_type=f32)
-    value_pre = jnp.dot(hidden, full_value, preferred_element_type=f32)
-    unit_pre = jnp.dot(hidden, full_unit, preferred_element_type=f32)
-    block_shape = (count, SPAN, heads, head_size)
-    query_blocks = jax.nn.silu(query_pre).astype(bf16).reshape(block_shape)
-    key_blocks = jax.nn.silu(key_pre).astype(bf16).reshape(block_shape)
-    value_blocks = value_pre.astype(bf16).reshape(block_shape)
-    scores = jnp.einsum("nthe,nshe->nhts", query_blocks, key_blocks, preferred_element_type=f32)
-    mixing = (scores * within).astype(bf16)
-    local_out = jnp.einsum("nhts,nshe->nthe", mixing, value_blocks, preferred_element_type=f32)
     keys_held = (key_blocks * leaving[..., None]).astype(bf16)
-    increments = jnp.einsum("nshe,nshf->nhef", keys_held, value_blocks, preferred_element_type=f32)
-    local_states = [jnp.zeros((heads, head_size, head_size), f32)]
-    local_states.append(passing[0][:, None, None] * local_states[-1] + increments[0])
-    end_state = local_states[count]
-    arriving = states(end_state, through_all, False)
-    held = jnp.stack(local_states[:count]) + arrival[:, :, None, None] * arriving[None]
-    state_low = held.astype(bf16)
     query_held = (query_blocks * entry[..., None]).astype(bf16)
-    attended = local_out + jnp.einsum(
-        "nthe,nhef->nthf", query_held, state_low, preferred_element_type=f32
-    )
     attended_heads = attended.reshape(length, heads, head_size)
     head_scale = row_scale(attended_heads)
     unit_norm = (attended_heads * head_scale).reshape(length, width)
-    gain = full_gain.astype(f32)
-    gated = unit_norm * gain
-    mixed_in = (gated * unit_pre).astype(bf16)
-    middle = inputs + jnp.dot(mixed_in, full_output, preferred_element_type=f32)
+    gated = unit_norm * full_gain
     second_scale = row_scale(middle)
     second_unit = middle * second_scale
-    second = second_unit.astype(bf16)
-    left_pre = jnp.dot(second, full_left, preferred_element_type=f32)
-    right_pre = jnp.dot(second, full_right, preferred_element_type=f32)
-    product = (left_pre * right_pre).astype(bf16)
     result = (middle + jnp.dot(product, full_down, preferred_element_type=f32)).astype(bf16)
     back_left, back_right, back_down = full_left, full_right, full_down
     grad_product = jnp.einsum("td,fd->tf", cotangent, back_down, preferred_element_type=f32)

time: 407 us -> 379 us (0.931)
  matrix products: 59.4 us -> 42.7 us
  Pallas kernels: 287 us -> 279 us
    pallas_call x2 -> x1, Pallas kernels: 51.1 us -> 25.2 us  [states(): pl.pallas_call(functools.partial(states_kernel, reverse), out_shape=jax.S...]
    pallas_call x1, Pallas kernels: 119 us -> 137 us  [forward(): pl.pallas_call(forward_kernel, out_shape=[jax.ShapeDtypeStruct((4, 2, 2,...]
    dot_general x11 -> x0, matrix products: 15 us -> none  [the longest x1 3.13 us: body_kernels(): unit_pre = jnp.dot(hidden, full_unit, preferred_element_type=f32)]
    dot_general x1, matrix products: 1.83 us -> 6.34 us  [body_kernels(): jnp.einsum('td,fd->tf', cotangent, back_down, preferred_element_type=f32)]
    unnamed x84 -> x74, local copies, waits for them, and re-layouts: 14.1 us -> 16.8 us
where the time goes in v2:
time: 379 us; the launch traced here: 375 us
  Pallas kernels  279 us (74%)
  matrix products  42.7 us (11%)
  local copies, waits for them, and re-layouts  34.3 us (9%)
  other arithmetic  15.6 us (4%)
    pallas_call x1, Pallas kernels, forward(): pl.pallas_call(forward_kernel, out_shape=[jax.ShapeDtypeStruct((4, 2, 2,...  137 us
    pallas_call x1, Pallas kernels, scatter_all(): pl.pallas_call(functools.partial(scatter_kernel, n), out_shape=[jax.Shape...  117 us
    pallas_call x1, Pallas kernels, states(): pl.pallas_call(functools.partial(states_kernel, reverse), out_shape=jax.S...  25.2 us
    unnamed x74, local copies, waits for them, and re-layouts  16.8 us

profile of v2, /device:TPU:0, one launch (start us, length us, event | category | flops | bytes accessed | tf_op | source)
XLA Modules:
  0.0 374.6 jit_solution(13428211558955961827)
XLA Ops:
  0.7 0.9 select_reduce_fusion
  1.7 0.6 fusion.41
  3.2 1.2 fusion.23
  4.5 0.6 slice.36
  5.8 0.7 multiply_exponential_fusion
  6.5 0.7 broadcast_in_dim.163
  7.4 0.6 broadcast_select_fusion.1.gain_own
  8.4 136.9 %forward.1 = (bf16[4,2,2,2,32,1024]{5,4,3,2,1,0:T(8,128)(2,1)}, bf16[4,2,2,2,32,1024]{5,4,3,2,1,0:T(8,128)(2,1)}, bf16[4,2,2,2,32,1024]{5,4,3,2,1,0:T(8,128)(2,1...) custom-call(s32[4]{0:T(128)} %lengths.1, s32[4]{0:T(128)} %order.1, ...), custom_call_target="tpu_custom_call" | custom-call | tf_op jit(solution)/shard_map/forward/pallas_call | solution.py:836
  145.3 6.3 %multiply_convert_fusion = (bf16[256,2816]{1,0:T(8,128)(2,1)S(1)}, bf16[256,2816]{1,0:T(8,128)(2,1)S(1)}) fusion(f32[256,2816]{1,0:T(8,128)} %get-tuple-element.55, f32[256,2816]{1,0:T(8,128)} %get-tuple-element.52, bf16[2816,1024]{1,0:T(8,128)(2,1)} %bitcast.147, bf16[256,1024]{1,0:T(8,128)(2,1)} %param.27), kind=kOutput, calls=%fused_computation.12 | convolution fusion | flops 1479278592 | bytes 14942208 | tf_op jit(solution)/shard_map/td,fd->tf/dot_general | solution.py:1201
  151.7 0.4 copy-done.14
  152.1 2.5 fusion.15
  154.6 0.5 copy-done.31
  155.2 0.9 copy-done.32
  156.0 2.1 fusion
  158.3 0.4 copy-done.30
  158.7 1.8 multiply_reduce_fusion.3
  160.9 0.6 copy-done.28
  161.7 1.0 copy.91
  162.7 1.6 copy.94
  164.3 0.3 multiply_reduce_fusion.2
  164.6 0.3 mul.285
  165.2 2.0 multiply_reduce_fusion
  167.3 0.7 pad.4
  167.9 1.4 copy.95
  169.3 0.6 multiply_reduce_fusion.1
  170.0 1.6 multiply_convert_fusion.8
  171.6 1.4 copy.84
  173.0 1.6 fusion.49
  174.9 25.2 %states_back.1 = f32[8,128,128]{2,1,0:T(8,128)S(1)} custom-call(f32[256]{0:T(256)S(1)} %select_n.92.through, f32[8,128,128]{2,1,0:T(8,128)S(1)} %convolution_multiply_fusion.value), custom_call_target="tpu_custom_call" | custom-call | tf_op jit(solution)/shard_map/states_back/pallas_call | solution.py:476
  200.1 0.6 fusion.16
  200.7 0.7 multiply_convert_fusion.2
  201.8 1.3 fusion.14
  203.1 0.5 convolution_bitcast_fusion.4
  203.6 1.3 fusion.12
  204.8 2.6 copy.89
  207.4 2.5 copy.90
  210.0 3.1 multiply_convert_fusion.5
  213.0 0.7 fusion.48
  213.8 0.8 copy-done.21
  214.6 0.8 convolution_add_fusion.3
  215.5 0.8 convolution_add_fusion.2
  216.6 0.7 copy-done.16
  217.3 0.9 fusion.19
  218.2 1.2 fusion.22
  219.5 2.1 convolution_convert_fusion.7
  221.6 2.1 convolution_convert_fusion.6
  223.7 2.1 convolution_convert_fusion.5
  225.8 2.2 convolution_convert_fusion.4
  228.0 2.2 convolution_convert_fusion.3
  230.2 1.7 convolution_convert_fusion
  231.9 3.2 fusion.44
  235.1 1.7 convolution_convert_fusion.1
  236.9 2.9 fusion.45
  239.8 4.2 %convolution_convert_fusion.2 = bf16[2816,1024]{1,0:T(8,128)(2,1)} fusion(bf16[256,2816]{1,0:T(8,128)(2,1)S(1)} %copy-done.15, bf16[256,1024]{1,0:T(8,128)(2,1)S(1)} %copy-done.10), kind=kOutput, calls=%fused_computation.10 | convolution fusion | flops 1479278592 | bytes 7733248 | tf_op jit(solution)/shard_map/tf,td->fd/dot_general | solution.py:1204
  243.9 117.1 %scatter.1 = (f32[88,1024]{1,0:T(8,128)}, f32[32,1408]{1,0:T(8,128)}, f32[32,1408]{1,0:T(8,128)}, f32[32,1408]{1,0:T(8,128)}, f32[32,1408]{1,0:T(8,128)}, /*inde...) custom-call(bf16[4,2,2,2,88,1024]{5,4,3,2,1,0:T(8,128)(2,1)} %bitcas, ...), custom_call_target="tpu_custom_call" | custom-call | tf_op jit(solution)/shard_map/scatter/pallas_call | solution.py:386
  361.0 1.2 slice_bitcast_fusion
  362.3 1.8 pad_maximum_fusion
  364.0 1.8 pad_maximum_fusion.1
  365.8 1.6 copy.124
  367.4 1.6 copy.125
  368.9 1.6 copy.126
  370.5 1.6 copy.127
  372.1 1.6 copy.128
  373.6 0.7 copy.129
  (92 shorter events, 3.2 us)
Async XLA Ops:
  145.3 6.4 %copy-start = (bf16[4,2,2,2,88,1024]{5,4,3,2,1,0:T(8,128)(2,1)S(1)}, bf16[4,2,2,2,88,1024]{5,4,3,2,1,0:T(8,128)(2,1)}, u32[]{:S(2)}) copy-start(bf16[4,2,2,2,88,1024]{5,4,3,2,1,0:T(8,128)(2,1)} %get-tuple-element.51) | copy-start | bytes 17301508
  145.3 6.4 %copy-start.12 = (f32[256,1024]{1,0:T(8,128)S(1)}, f32[256,1024]{1,0:T(8,128)}, u32[]{:S(2)}) copy-start(f32[256,1024]{1,0:T(8,128)} %get-tuple-element.49) | copy-start | bytes 3145732
  145.3 6.8 %copy-start.14 = (bf16[256,2816]{1,0:T(8,128)(2,1)S(1)}, bf16[256,2816]{1,0:T(8,128)(2,1)}, u32[]{:S(2)}) copy-start(bf16[256,2816]{1,0:T(8,128)(2,1)} %get-tuple-element.50) | copy-start | bytes 4325380
  152.1 2.5 copy-start.1
  152.1 6.2 %copy-start.3 = (bf16[256,2816]{1,0:T(8,128)(2,1)}, bf16[256,2816]{1,0:T(8,128)(2,1)S(1)}, u32[]{:S(2)}) copy-start(bf16[256,2816]{1,0:T(8,128)(2,1)S(1)} %get-tuple-element.95) | copy-start | bytes 4325380
  152.1 3.0 copy-start.31
  152.1 3.9 %copy-start.32 = (bf16[4,2,2,2,32,1408]{5,4,3,2,1,0:T(8,128)(2,1)S(1)}, bf16[4,2,2,2,32,1408]{5,4,3,2,1,0:T(8,128)(2,1)}, u32[]{:S(2)}) copy-start(bf16[4,2,2,2,32,1408]{5,4,3,2,1,0:T(8,128)(2,1)} %get-tuple-element.54) | copy-start | bytes 8650756
  156.0 2.2 copy-start.29
  156.0 2.7 copy-start.30
  158.7 1.9 copy-start.9
  160.5 0.9 copy-start.28
  160.6 1.1 copy-start.24
  162.7 2.3 copy-start.11
  162.7 2.3 copy-start.17
  162.7 2.5 copy-start.22
  171.6 3.0 copy-start.7
  173.0 27.1 %copy-start.18 = (bf16[256,1024]{1,0:T(8,128)(2,1)S(1)}, bf16[256,1024]{1,0:T(8,128)(2,1)}, u32[]{:S(2)}) copy-start(bf16[256,1024]{1,0:T(8,128)(2,1)} %get-tuple-element.58) | copy-start | bytes 1572868
  174.6 26.1 %copy-start.25 = (bf16[256,1024]{1,0:T(8,128)(2,1)S(1)}, bf16[256,1024]{1,0:T(8,128)(2,1)}, u32[]{:S(2)}) copy-start(bf16[256,1024]{1,0:T(8,128)(2,1)} %get-tuple-element.63) | copy-start | bytes 1572868
  200.1 1.3 copy-start.8
  201.8 1.8 copy-start.27
  209.9 3.1 copy-start.19
  213.0 1.6 copy-start.21
  213.8 1.7 copy-start.20
  215.5 1.0 copy-start.5
  215.5 1.8 copy-start.16
  218.2 1.3 copy-start.23
  218.2 3.4 copy-start.6
  225.8 4.3 %copy-start.4 = (bf16[256,2816]{1,0:T(8,128)(2,1)S(1)}, bf16[256,2816]{1,0:T(8,128)(2,1)}, u32[]{:S(2)}) copy-start(bf16[256,2816]{1,0:T(8,128)(2,1)} %copy-done.3) | copy-start | bytes 4325380
  225.8 4.3 %copy-start.13 = (bf16[256,1024]{1,0:T(8,128)(2,1)S(1)}, bf16[256,1024]{1,0:T(8,128)(2,1)}, u32[]{:S(2)}) copy-start(bf16[256,1024]{1,0:T(8,128)(2,1)} %get-tuple-element.73) | copy-start | bytes 1572868
  231.9 3.3 copy-start.2
  236.9 2.9 copy-start.10
  236.9 2.9 copy-start.15
  361.0 12.6 %copy-start.26 = (f32[88,1024]{1,0:T(8,128)S(1)}, f32[88,1024]{1,0:T(8,128)}, u32[]{:S(2)}) copy-start(f32[88,1024]{1,0:T(8,128)} %get-tuple-element.130) | copy-start | bytes 1081348

commit v3 on v2

--- a/solution.py
+++ b/solution.py
@@ -44,18 +44,6 @@
 
     def dev(self, z, y, x, c):
         return ((z * 2 + y) * 2 + x) * 2 + c
-
-
-def greet(place):
-    barrier = pltpu.get_barrier_semaphore()
-    for link in ("p", "x", "y", "S"):
-        pl.semaphore_signal(barrier, inc=1, device_id=place.to[link], device_id_type=LOGICAL)
-
-    @pl.when(place.inner)
-    def _():
-        pl.semaphore_signal(barrier, inc=1, device_id=place.to["K"], device_id_type=LOGICAL)
-
-    pl.semaphore_wait(barrier, jnp.where(place.inner, 5, 4))
 
 
 def arrived(ref, send, recv, place):
@@ -222,8 +210,8 @@
     NSEND = 22
     SLOTS = ("x0", "x1", "x2", "x3", "Fx", "y0", "y1", "y2", "y3", "Fy", "En", "Ef", "Cn", "Cf", "Co", "De", "Do", "KCs", "KCo")
 
-    def __init__(self, place, part, acc, own, came, out, send, recv, index):
-        self.p, self.part, self.acc, self.own, self.came, self.out = place, part, acc, own, came, out
+    def __init__(self, place, part, acc, term, came, out, send, recv, index):
+        self.p, self.part, self.acc, self.term, self.came, self.out = place, part, acc, term, came, out
         self.send, self.recv, self.index = send, recv, index
         self.sent = []
         p = place
@@ -266,30 +254,18 @@
         outer = jnp.logical_not(inner)
         ze, zo, near, far = self.ze, self.zo, p.near, p.far
         if r == 0:
-            made = pltpu.make_async_remote_copy(
-                src_ref=self.part.at[:, :, :, p.c1],
+            self.given = pltpu.make_async_remote_copy(
+                src_ref=self.part,
                 dst_ref=self.acc,
-                send_sem=self.send.at[self.index, 0],
+                send_sem=self.send.at[self.index, self.NSEND],
                 recv_sem=self.recv.at[self.index, 19],
                 device_id=p.to["p"],
                 device_id_type=LOGICAL,
             )
-            self.sent.append((made, None))
-            made.start()
-            self.load = pltpu.make_async_copy(
-                self.part.at[:, :, :, p.c], self.own, self.send.at[self.index, self.NSEND]
-            )
-            self.load.start()
+            self.given.start()
         if r == 1:
-            self.load.wait()
             arrived(self.acc, self.send.at[self.index, 0], self.recv.at[self.index, 19], p)
-
-            @pl.loop(0, 4)
-            def _(z):
-                for y in range(2):
-                    for x in range(2):
-                        add_into(self.acc.at[z, y, x], [self.acc.at[z, y, x], self.own.at[z, y, x]])
-
+            self.term.second(self.acc)
             self.go(self.D(far), "S", "Ef", outer)
             self.go(self.D(near), "S", "En", outer)
             self.go(self.X(far), "x", far)
@@ -354,145 +330,15 @@
             def _():
                 add_into(self.out, [self.out, self.wait("KCo")])
 
+    def handed(self):
+        self.given.wait_send()
+
     def finish(self):
         for made, cond in self.sent:
             if cond is None:
                 made.wait_send()
             else:
                 pl.when(cond)(made.wait_send)
-
-
-def scatter_kernel(n, *refs):
-    part, out = refs[:n], refs[n : 2 * n]
-    acc, own, came = refs[2 * n : 3 * n], refs[3 * n : 4 * n], refs[4 * n : 5 * n]
-    send, recv = refs[5 * n :]
-    place = Place()
-    greet(place)
-    made = [
-        Scatter(place, part[i], acc[i], own[i], came[i], out[i], send, recv, i) for i in range(n)
-    ]
-    for step in range(n + 6):
-        for r in range(7):
-            i = step - r
-            if 0 <= i < n:
-                made[i].round(r)
-    for one in made:
-        one.finish()
-
-
-def scatter_all(parts):
-    n = len(parts)
-    blocks = [(p.shape[4:], p.dtype) for p in parts]
-    return pl.pallas_call(
-        functools.partial(scatter_kernel, n),
-        out_shape=[jax.ShapeDtypeStruct(b, jnp.float32) for b, _ in blocks],
-        in_specs=[pl.BlockSpec(memory_space=pltpu.HBM)] * n,
-        out_specs=[pl.BlockSpec(memory_space=pltpu.VMEM)] * n,
-        scratch_shapes=[pltpu.VMEM((4, 2, 2) + b, t) for b, t in blocks]
-        + [pltpu.VMEM((4, 2, 2) + b, t) for b, t in blocks]
-        + [pltpu.VMEM((19,) + b, t) for b, t in blocks]
-        + [
-            pltpu.SemaphoreType.DMA((n, Scatter.NSEND + 1)),
-            pltpu.SemaphoreType.DMA((n, Scatter.NRECV)),
-        ],
-        compiler_params=pltpu.CompilerParams(
-            collective_id=3, has_side_effects=True, vmem_limit_bytes=VMEM_LIMIT
-        ),
-        name="scatter",
-    )(*parts)
-
-
-def states_kernel(reverse, through, value, out, met, planes, ready, send, recv):
-    me = lax.axis_index(AXIS)
-    z, r = me // 8, lax.rem(me, 8)
-    barrier = pltpu.get_barrier_semaphore()
-    plane = [z * 8 + lax.bitwise_xor(r, k) for k in range(8)]
-    level = [lax.rem(z + k, 4) * 8 + r for k in range(4)]
-    for peer in plane[1:] + level[1:]:
-        pl.semaphore_signal(barrier, inc=1, device_id=peer, device_id_type=LOGICAL)
-    pl.semaphore_wait(barrier, 10)
-
-    def copy(src, dst, k, peer):
-        return pltpu.make_async_remote_copy(
-            src_ref=src,
-            dst_ref=dst,
-            send_sem=send.at[k],
-            recv_sem=recv.at[k],
-            device_id=peer,
-            device_id_type=LOGICAL,
-        )
-
-    first = [copy(value.at[lax.bitwise_xor(r, k)], met.at[r], k, plane[k]) for k in range(1, 8)]
-    for one in first:
-        one.start()
-    met[r] = value[r]
-    for k in range(1, 8):
-        copy(value.at[0], met.at[lax.bitwise_xor(r, k)], k, plane[k]).wait_recv()
-    order = range(7, -1, -1) if reverse else range(8)
-    total = jnp.zeros(met.shape[1:], jnp.float32)
-    for i in order:
-        total = through[(z * 8 + i) * 8 + r] * total + met[i]
-    planes[z] = total
-    second = []
-    for k in range(1, 4):
-        far = z - k if reverse else z + k
-        cond = far >= 0 if reverse else far <= 3
-        made = copy(planes.at[z], planes.at[z], 7 + k, far * 8 + r)
-        second.append((made, cond))
-        pl.when(cond)(made.start)
-    ready[8] = jnp.zeros(met.shape[1:], jnp.float32)
-    for k in range(3, 0, -1):
-        far = z + k if reverse else z - k
-        cond = far <= 3 if reverse else far >= 0
-
-        @pl.when(cond)
-        def _():
-            copy(planes.at[z], planes.at[far], 7 + k, plane[0]).wait_recv()
-            kept = jnp.float32(1.0)
-            for i in range(8):
-                kept = kept * through[(far * 8 + i) * 8 + r]
-            ready[8] = kept * ready[8] + planes[far]
-
-    total = ready[8]
-    for i in order:
-        ready[i] = total
-        total = through[(z * 8 + i) * 8 + r] * total + met[i]
-    third = [
-        copy(ready.at[lax.bitwise_xor(r, k)], out.at[r], 10 + k, plane[k]) for k in range(1, 8)
-    ]
-    for one in third:
-        one.start()
-    out[r] = ready[r]
-    for k in range(1, 8):
-        copy(ready.at[0], out.at[lax.bitwise_xor(r, k)], 10 + k, plane[k]).wait_recv()
-    for one in first + third:
-        one.wait_send()
-    for made, cond in second:
-        pl.when(cond)(made.wait_send)
-
-
-def states(value, through, reverse):
-    tile = value.shape[1:]
-    return pl.pallas_call(
-        functools.partial(states_kernel, reverse),
-        out_shape=jax.ShapeDtypeStruct(value.shape, jnp.float32),
-        in_specs=[
-            pl.BlockSpec(memory_space=pltpu.SMEM),
-            pl.BlockSpec(memory_space=pltpu.VMEM),
-        ],
-        out_specs=pl.BlockSpec(memory_space=pltpu.VMEM),
-        scratch_shapes=[
-            pltpu.VMEM((8,) + tile, jnp.float32),
-            pltpu.VMEM((4,) + tile, jnp.float32),
-            pltpu.VMEM((9,) + tile, jnp.float32),
-            pltpu.SemaphoreType.DMA((18,)),
-            pltpu.SemaphoreType.DMA((18,)),
-        ],
-        compiler_params=pltpu.CompilerParams(
-            collective_id=2 if reverse else 1, has_side_effects=True, vmem_limit_bytes=16000000
-        ),
-        name="states_back" if reverse else "states",
-    )(through.reshape(-1), value)
 
 
 def bounds_of(lengths, order):
@@ -554,6 +400,18 @@
 
 def norm_scale(values):
     return lax.rsqrt(jnp.mean(values * values, axis=-1, keepdims=True) + EPSILON)
+
+
+def slope(a):
+    sigma = 1.0 / (1.0 + jnp.exp(-a))
+    return sigma * (1.0 + a * (1.0 - sigma))
+
+
+def flat_rows(value):
+    return value.astype(jnp.float32).reshape(-1, value.shape[-1]).astype(jnp.bfloat16)
+
+
+SAVED_BACK = 18
 
 
 class States:
@@ -665,6 +523,7 @@
     order,
     rate,
     tokens,
+    cot,
     gain_own,
     s_key,
     s_value,
@@ -679,12 +538,14 @@
     f32, bf16 = jnp.float32, jnp.bfloat16
     n = 11
     full, refs = refs[:n], refs[n:]
-    saved, refs = refs[:16], refs[16:]
-    kept, refs = refs[:16], refs[16:]
-    (hidden, keys, values, queries, key_pre, query_pre, unit_pre, probs) = kept[:8]
-    (attended, state_low, mixed, middle, second, left, right, product) = kept[8:]
-    (dist, entry, leaving, gains, gain, value, met, planes, ready, arriving) = refs[:10]
-    (narrow, wide, send, recv, state_send, state_recv, load_sem, save_sem) = refs[10:]
+    saved, refs = refs[:SAVED_BACK], refs[SAVED_BACK:]
+    kept, refs = refs[:SAVED_BACK], refs[SAVED_BACK:]
+    (hidden_rows, keys, values, queries, key_pre, query_pre, unit_pre, probs) = kept[:8]
+    (attended, state_low, mixed_rows, middle, second_rows, left, right, product) = kept[8:16]
+    gain, down_term = kept[16:]
+    (hidden, mixed, second, turned) = refs[:4]
+    (dist, entry, leaving, gains, value, met, planes, ready, arriving) = refs[4:13]
+    (narrow, wide, send, recv, state_send, state_recv, load_sem, save_sem) = refs[13:]
     place = Place()
     half = s_left.shape[1] // 2
     own = [s_key, s_value, s_query, s_unit, gain_own, s_output]
@@ -710,10 +571,17 @@
         ref = slots[i]
         return ref[...].reshape(-1, ref.shape[-1])
 
+    def turn(ref, rows):
+        @pl.loop(0, 8)
+        def _(i):
+            block = ref[:, head_of(i)].astype(f32).T
+            rows[i // 2, i % 2] = block.reshape((2, 2) + rows.shape[4:]).astype(bf16)
+
     def start():
         x = tokens[...].astype(f32)
         hidden[...] = (x * norm_scale(x)).astype(bf16)
         spans_of(place.me * SPAN, bounds, dist, entry, leaving)
+        turn(hidden, hidden_rows)
         save(0)
 
     def project(i, pre, low):
@@ -771,24 +639,39 @@
                 out * norm_scale(out) * gain[pl.ds(h, 1), :] * unit_pre[:, at]
             ).astype(bf16)
 
-        save(8, 9, 10)
+        turn(mixed, mixed_rows)
+        save(8, 9, 10, 16)
 
     def output():
         out = tokens[...].astype(f32) + mm(mixed[...], weight(5))
         middle[...] = out
         second[...] = (out * norm_scale(out)).astype(bf16)
+        turn(second, second_rows)
         save(11, 12)
 
     def gate(i, side, part):
         side[:, pl.ds(part * half, half)] = mm(second[...], weight(i))
 
     def multiply():
-        @pl.loop(0, SPAN // 16)
-        def _(i):
-            at = pl.ds(pl.multiple_of(i * 16, 16), 16)
-            product[at, :] = (left[at, :] * right[at, :]).astype(bf16)
-
-        save(13, 14, 15)
+        cols = cot.shape[1] // 2
+
+        @pl.loop(0, 2)
+        def _(j):
+            @pl.loop(0, half // 128)
+            def _(i):
+                at = pl.ds(pl.multiple_of(j * half + i * 128, 128), 128)
+                block = (left[:, at] * right[:, at]).astype(bf16).astype(f32)
+                turned[pl.ds(pl.multiple_of(i * 128, 128), 128), :] = block.T
+
+            both = pl.ds(2 * j, 2)
+            block = turned[...].reshape((2,) + product.shape[1:])
+            product[both] = block.astype(bf16)
+            rows = flat_rows(product[both, :, :, place.c1])
+            for m in range(2):
+                term = mm(rows, cot[:, pl.ds(m * cols, cols)])
+                down_term[m, both] = term.reshape((2,) + down_term.shape[2:]).astype(bf16)
+
+        save(13, 14, 15, 17)
 
     tasks = {0: [start], 7: [key], 8: [increments], 9: [states.total, query], 10: [states.back, unit]}
     tasks[11] = [states.done, attend]
@@ -803,15 +686,15 @@
             if 0 <= step - r < n:
                 made[step - r].round(r)
         i = step - 6
+        if i - 1 in loads:
+            loads[i - 1].wait()
+        for task in tasks.get(step, []):
+            task()
         if 0 <= i < n:
             made[i].pairs()
-        if i - 1 in loads:
-            loads[i - 1].wait()
         if i in slots:
             loads[i] = pltpu.make_async_copy(full[i], slots[i], load_sem.at[i])
             loads[i].start()
-        for task in tasks.get(step, []):
-            task()
     for one in made:
         one.finish()
     states.finish()
@@ -819,7 +702,7 @@
         copy.wait()
 
 
-def forward(lengths, order, rate, tokens, gain_tile, shards):
+def forward(lengths, order, rate, tokens, cot, gain_tile, shards):
     f32, bf16 = jnp.float32, jnp.bfloat16
     size, width = tokens.shape
     wide = shards[5].shape[1]
@@ -827,9 +710,12 @@
     blocks = [(s.shape, s.dtype) for s in shards[:4]] + [(gain_tile.shape, f32)]
     blocks += [(shards[4].shape, bf16)] + [((32, half), bf16)] * 4 + [(shards[7].shape, bf16)]
     square, cube = (size, width), (8, 128, 128)
-    kept = [(square, bf16)] * 4 + [(square, f32)] * 3 + [((8, size, size), bf16)]
-    kept += [(square, f32), (cube, bf16), (square, bf16), (square, f32), (square, bf16)]
-    kept += [((size, wide), f32)] * 2 + [((size, wide), bf16)]
+    rows, down_rows = shards[4].shape[0], shards[7].shape[0]
+    across = ((4, 2, 2, 2, rows, size), bf16)
+    kept = [across] + [(square, bf16)] * 3 + [(square, f32)] * 3 + [((8, size, size), bf16)]
+    kept += [(square, f32), (cube, bf16), across, (square, f32), across]
+    kept += [((size, wide), f32)] * 2 + [((4, 2, 2, 2, down_rows, size), bf16), ((8, 128), f32)]
+    kept += [((2, 4, 2, 2, down_rows, width // 2), bf16)]
     vmem, hbm = pl.BlockSpec(memory_space=pltpu.VMEM), pl.BlockSpec(memory_space=pltpu.HBM)
     smem = pl.BlockSpec(memory_space=pltpu.SMEM)
     n = len(blocks)
@@ -837,11 +723,13 @@
         forward_kernel,
         out_shape=[jax.ShapeDtypeStruct((4, 2, 2, 2) + s, t) for s, t in blocks]
         + [jax.ShapeDtypeStruct(s, t) for s, t in kept],
-        in_specs=[smem] * 3 + [vmem] * 10,
+        in_specs=[smem] * 3 + [vmem] * 11,
         out_specs=[hbm] * (n + len(kept)),
         scratch_shapes=[pltpu.VMEM(s, t) for s, t in kept]
+        + [pltpu.VMEM(square, bf16)] * 3
+        + [pltpu.VMEM((half, size), f32)]
         + [pltpu.VMEM((size, size), f32), pltpu.VMEM((size, 128), f32), pltpu.VMEM((size, 128), f32)]
-        + [pltpu.VMEM((4, 2, 2, 2, 8, 128), f32), pltpu.VMEM((8, 128), f32)]
+        + [pltpu.VMEM((4, 2, 2, 2, 8, 128), f32)]
         + [pltpu.VMEM(cube, f32), pltpu.VMEM(cube, f32), pltpu.VMEM((4, 128, 128), f32)]
         + [pltpu.VMEM((9, 128, 128), f32), pltpu.VMEM(cube, f32)]
         + [
@@ -858,8 +746,344 @@
             collective_id=0, has_side_effects=True, vmem_limit_bytes=VMEM_LIMIT
         ),
         name="forward",
-    )(lengths, order, rate, tokens, gain_tile, *shards)
+    )(lengths, order, rate, tokens, cot, gain_tile, *shards)
     return out[:n], out[n:]
+
+def backward_kernel(lengths, order, rate, tokens, cot, *refs):
+    f32, bf16 = jnp.float32, jnp.bfloat16
+    n = 12
+    saved, refs = refs[:SAVED_BACK], refs[SAVED_BACK:]
+    (h_hidden, h_keys, h_values, h_queries, h_key_pre, h_query_pre, h_unit_pre, h_probs) = saved[:8]
+    (h_attended, h_state_low, h_mixed, h_middle, h_second, h_left, h_right, h_product) = saved[8:16]
+    h_gain, h_down = saved[16:]
+    w_in, refs = refs[:10], refs[10:]
+    (w_key, w_value, w_query, w_unit, w_output, w_l0, w_l1, w_r0, w_r1, w_down) = w_in
+    out, result_out, tokens_out, refs = refs[:n], refs[n], refs[n + 1], refs[n + 2 :]
+    acc, came, refs = refs[:n], refs[n : 2 * n], refs[2 * n :]
+    (part, gain_part, wd, down, wl, left, right, f1, f2, f3, f4) = refs[:11]
+    (branch, ga, gup, gkp, gvp, result, glp, grp, rows, mixed, product) = refs[11:22]
+    (probs, state_low, gain, gg, dist, entry, leaving) = refs[22:29]
+    (value, met, planes, ready, arriving) = refs[29:34]
+    (send, recv, state_send, state_recv, load_sem) = refs[34:]
+    place = Place()
+    half = h_left.shape[1] // 2
+    width = tokens.shape[1]
+    left_w, right_w = left.at[:, pl.ds(0, width)], right.at[:, pl.ds(0, width)]
+    queries, keys = glp.at[:, pl.ds(0, width)], glp.at[:, pl.ds(width, width)]
+    values, gqp = grp.at[:, pl.ds(0, width)], grp.at[:, pl.ds(width, width)]
+    wn = wl.at[:, :, :, :, :, pl.ds(0, width)]
+    greet_more(place)
+    bounds = bounds_of(lengths, order)
+    states = States(
+        place, bounds, rate, True, value, met, planes, ready, arriving, state_send, state_recv
+    )
+    loads = {}
+
+    def load(name, src, dst):
+        copy = pltpu.make_async_copy(src, dst, load_sem.at[len(loads)])
+        loads[name] = copy
+        copy.start()
+
+    def loaded(*names):
+        for name in names:
+            loads[name].wait()
+
+    def weight(cols):
+        return wl[:, :, :, :, :, pl.ds(0, cols)].reshape(-1, cols)
+
+    def side(i):
+        return pl.ds(i * half, half)
+
+    def product_of(i):
+        return flat_rows(product[pl.ds(2 * i, 2)])
+
+    class Piece:
+        def __init__(self, rows, core_rows, grad, cols, need=()):
+            self.rows, self.core_rows, self.grad, self.cols, self.need = rows, core_rows, grad, cols, need
+
+        def term(self, zh, core):
+            lhs = self.rows[pl.ds(zh * 2, 2), :, :, core]
+            lhs = flat_rows(lhs) if self.core_rows % 16 else lhs.reshape(-1, lhs.shape[-1])
+            out = mm(lhs, self.grad[...])
+            return out.reshape(2, 2, 2, self.core_rows, self.cols)
+
+        def first(self):
+            @pl.loop(0, 2)
+            def _(zh):
+                part[pl.ds(zh * 2, 2), :, :, :, pl.ds(0, self.cols)] = self.term(
+                    zh, place.c1
+                ).astype(bf16)
+
+        def second(self, acc):
+            @pl.loop(0, 2)
+            def _(zh):
+                at = pl.ds(zh * 2, 2)
+                acc[at] = (acc[at].astype(f32) + self.term(zh, place.c)).astype(bf16)
+
+    class Gain:
+        def first(self):
+            gain_part[...] = jnp.broadcast_to(gg[...][None, None, None], gain_part.shape)
+
+        def second(self, acc):
+            acc[...] = acc[...] + gg[...][None, None, None]
+
+    wide = part.at[:, :, :, :, pl.ds(0, half)]
+    narrow = part.at[:, :, :, :, pl.ds(0, width)]
+    cols = width // 2
+    pieces = [(h_down.at[m], Piece(product, 88, cot.at[:, pl.ds(m * cols, cols)], cols)) for m in (0, 1)]
+    pieces += [(wide, Piece(rows, 32, glp.at[:, side(i)], half)) for i in (0, 1)]
+    pieces += [(wide, Piece(rows, 32, grp.at[:, side(i)], half)) for i in (0, 1)]
+    pieces += [(narrow, Piece(mixed, 32, branch, width)), (gain_part, Gain())]
+    pieces += [(narrow, Piece(rows, 32, g, width)) for g in (gup, gqp, gvp, gkp)]
+    made = [
+        Scatter(place, pieces[i][0], acc[i], pieces[i][1], came[i], out[i], send, recv, i)
+        for i in range(n)
+    ]
+
+    def begin():
+        spans_of(place.me * SPAN, bounds, dist, entry, leaving)
+
+    def gates(i):
+        loaded("down%d" % i, "left%d" % i, "right%d" % i)
+        pair = 2 * wd.shape[4]
+
+        @pl.loop(0, 8)
+        def _(k):
+            at = pl.ds(pl.multiple_of(k * pair, 16), pair)
+            down[at, :] = flat_rows(wd[k // 4, (k // 2) % 2, k % 2])
+
+        grad = mm_nt(cot[...], down[...])
+        glp[:, side(i)] = (grad * right[...]).astype(bf16)
+        grp[:, side(i)] = (grad * left[...]).astype(bf16)
+        if i == 0:
+            loaded("middle")
+            f3[...] = f2[...] + mm_tn(product_of(0), down[...])
+            load("down1", w_down.at[pl.ds(2, 2)], wd)
+            load("left1", h_left.at[:, side(1)], left)
+            load("right1", h_right.at[:, side(1)], right)
+        else:
+            result[...] = (f3[...] + mm_tn(product_of(1), down[...])).astype(bf16)
+            load("unit_pre", h_unit_pre, left_w)
+            load("result", result, result_out)
+
+    def second_part(name, grad, i, following, start):
+        loaded(name)
+        term = mm_nt(grad[:, side(i)], weight(half))
+        f1[...] = term if start else f1[...] + term
+        load(*following)
+
+    def middle():
+        @pl.loop(0, SPAN // 16)
+        def _(i):
+            at = pl.ds(pl.multiple_of(i * 16, 16), 16)
+            x, g = f2[at, :], f1[at, :]
+            scale = norm_scale(x)
+            unit = x * scale
+            grad = cot[at, :].astype(f32) + scale * (
+                g - unit * jnp.mean(g * unit, axis=-1, keepdims=True)
+            )
+            f3[at, :] = grad
+            branch[at, :] = grad.astype(bf16)
+
+        load("attended", h_attended, f2)
+
+    def spare():
+        load("queries", h_queries, queries)
+        load("keys", h_keys, keys)
+        load("values", h_values, values)
+        load("hidden", h_hidden, rows)
+
+    def attention():
+        loaded("output")
+        f1[...] = mm_nt(branch[...], weight(width))
+        load("unit", w_unit, wn)
+        loaded("attended", "unit_pre", "queries", "gain")
+
+        @pl.loop(0, 8)
+        def _(h):
+            at = head_of(h)
+            att, up, gm = f2[:, at], left_w[:, at], f1[:, at]
+            scale = norm_scale(att)
+            unit = att * scale
+            row = gain[pl.ds(h, 1), :]
+            gated = gm * up
+            gg[pl.ds(h, 1), :] = jnp.sum(gated * unit, axis=0, keepdims=True)
+            gup[:, at] = (gm * unit * row).astype(bf16)
+            g = gated * row
+            low = (
+                scale * (g - unit * jnp.mean(g * unit, axis=-1, keepdims=True))
+            ).astype(bf16)
+            ga[:, at] = low
+            held = (queries[:, at].astype(f32) * decay(entry[...], rate[h])).astype(bf16)
+            value[h] = mm_tn(held, low)
+
+        states.spread()
+        load("key_pre", h_key_pre, f2)
+
+    def scores():
+        loaded("keys", "values", "query_pre", "probs", "state_low")
+
+        @pl.loop(0, 8)
+        def _(h):
+            at = head_of(h)
+            low = ga[:, at]
+            grads = (mm_nt(low, values[:, at]) * decay(dist[...], rate[h])).astype(bf16)
+            grad_q = mm(grads, keys[:, at])
+            grad_q = grad_q + mm_nt(low, state_low[h]) * decay(entry[...], rate[h])
+            gqp[:, at] = (grad_q * slope(f4[:, at])).astype(bf16)
+            f1[:, at] = mm_tn(grads, queries[:, at])
+            right_w[:, at] = mm_tn(probs[h], low)
+
+        states.total()
+
+    def hidden_part(name, grad, following, start):
+        loaded(name)
+        term = mm_nt(grad[...], weight(width))
+        f4[...] = term if start else f4[...] + term
+        if following:
+            load(*following)
+
+    def unit_rest():
+        states.back()
+        hidden_part("unit", gup, ("query", w_query, wn), True)
+
+    def last_grads():
+        hidden_part("query", gqp, ("value", w_value, wn), False)
+        states.done()
+        loaded("key_pre")
+
+        @pl.loop(0, 8)
+        def _(h):
+            at = head_of(h)
+            grad = arriving[h].astype(bf16)
+            fall = decay(leaving[...], rate[h])
+            held = (keys[:, at].astype(f32) * fall).astype(bf16)
+            grad_k = f1[:, at] + mm_nt(values[:, at], grad) * fall
+            gkp[:, at] = (grad_k * slope(f2[:, at])).astype(bf16)
+            gvp[:, at] = (right_w[:, at] + mm(held, grad)).astype(bf16)
+
+    def value_rest():
+        hidden_part("value", gvp, ("key", w_key, wn), False)
+
+    def inputs():
+        hidden_part("key", gkp, None, False)
+
+        @pl.loop(0, SPAN // 16)
+        def _(i):
+            at = pl.ds(pl.multiple_of(i * 16, 16), 16)
+            x, g = tokens[at, :].astype(f32), f4[at, :]
+            scale = norm_scale(x)
+            unit = x * scale
+            f3[at, :] = f3[at, :] + scale * (g - unit * jnp.mean(g * unit, axis=-1, keepdims=True))
+
+        load("tokens", f3, tokens_out)
+
+    before = {1: lambda: loaded("product"), 2: lambda: loaded("second"), 6: lambda: loaded("mixed")}
+    before[8] = lambda: loaded("hidden")
+    tasks = {0: [begin], 1: [lambda: gates(0)], 2: [lambda: gates(1)]}
+    tasks[3] = [lambda: second_part("l0", glp, 0, ("l1", w_l1, wl), True)]
+    tasks[4] = [lambda: second_part("l1", glp, 1, ("r0", w_r0, wl), False)]
+    tasks[5] = [
+        lambda: second_part("r0", grp, 0, ("r1", w_r1, wl), False),
+        lambda: second_part("r1", grp, 1, ("output", w_output, wn), False),
+        middle,
+    ]
+    tasks[6] = [spare, attention]
+    tasks[7] = [scores]
+    tasks[8] = [unit_rest]
+    tasks[9] = [last_grads]
+    tasks[10] = [value_rest]
+    tasks[11] = [inputs]
+    load("product", h_product, product)
+    load("down0", w_down.at[pl.ds(0, 2)], wd)
+    load("left0", h_left.at[:, side(0)], left)
+    load("right0", h_right.at[:, side(0)], right)
+    load("middle", h_middle, f2)
+    load("second", h_second, rows)
+    load("l0", w_l0, wl)
+    load("mixed", h_mixed, mixed)
+    load("gain", h_gain, gain)
+    load("query_pre", h_query_pre, f4)
+    load("probs", h_probs, probs)
+    load("state_low", h_state_low, state_low)
+    for step in range(n + 6):
+        if step < n:
+            if step in before:
+                before[step]()
+            if step > 2:
+                made[step - 1].handed()
+            if step > 1:
+                pieces[step][1].first()
+            made[step].round(0)
+        if 0 < step <= n:
+            made[step - 1].round(1)
+        for task in tasks.get(step, []):
+            task()
+        for r in range(2, 7):
+            if 0 <= step - r < n:
+                made[step - r].round(r)
+    for i, one in enumerate(made):
+        if i < 2 or i == n - 1:
+            one.handed()
+        one.finish()
+    states.finish()
+    loaded("result", "tokens")
+
+
+def backward(lengths, order, rate, tokens, cot, saved, weights):
+    f32, bf16 = jnp.float32, jnp.bfloat16
+    size, width = tokens.shape
+    wide = saved[13].shape[1]
+    half = wide // 2
+    rows = width // 32
+    down_rows = wide // 32
+    blocks = [((down_rows, width // 2), bf16)] * 2 + [((rows, half), bf16)] * 4
+    blocks += [((rows, width), bf16), ((8, 128), f32)] + [((rows, width), bf16)] * 4
+    n = len(blocks)
+    square, cube = (size, width), (8, 128, 128)
+    vmem, hbm = pl.BlockSpec(memory_space=pltpu.VMEM), pl.BlockSpec(memory_space=pltpu.HBM)
+    smem = pl.BlockSpec(memory_space=pltpu.SMEM)
+    out = pl.pallas_call(
+        backward_kernel,
+        out_shape=[jax.ShapeDtypeStruct(b, f32) for b, _ in blocks]
+        + [jax.ShapeDtypeStruct(square, bf16), jax.ShapeDtypeStruct(square, f32)],
+        in_specs=[smem] * 3 + [vmem] * 2 + [hbm] * (len(saved) + len(weights)),
+        out_specs=[vmem] * n + [hbm] * 2,
+        scratch_shapes=[pltpu.VMEM((4, 2, 2) + b, t) for b, t in blocks]
+        + [pltpu.VMEM((19,) + b, t) for b, t in blocks]
+        + [
+            pltpu.VMEM((4, 2, 2, rows, half), bf16),
+            pltpu.VMEM((4, 2, 2, 8, 128), f32),
+            pltpu.VMEM((2, 2, 2, 2, down_rows, width), bf16),
+            pltpu.VMEM((half, width), bf16),
+            pltpu.VMEM((4, 2, 2, 2, rows, half), bf16),
+            pltpu.VMEM((size, half), f32),
+            pltpu.VMEM((size, half), f32),
+        ]
+        + [pltpu.VMEM(square, f32)] * 4
+        + [pltpu.VMEM(square, bf16)] * 6
+        + [pltpu.VMEM((size, wide), bf16)] * 2
+        + [pltpu.VMEM((4, 2, 2, 2, rows, size), bf16)] * 2
+        + [pltpu.VMEM((4, 2, 2, 2, down_rows, size), bf16)]
+        + [pltpu.VMEM((8, size, size), bf16), pltpu.VMEM(cube, bf16)]
+        + [pltpu.VMEM((8, 128), f32)] * 2
+        + [pltpu.VMEM((size, size), f32), pltpu.VMEM((size, 128), f32), pltpu.VMEM((size, 128), f32)]
+        + [pltpu.VMEM(cube, f32), pltpu.VMEM(cube, f32), pltpu.VMEM((4, 128, 128), f32)]
+        + [pltpu.VMEM((9, 128, 128), f32), pltpu.VMEM(cube, f32)]
+        + [
+            pltpu.SemaphoreType.DMA((n, Scatter.NSEND + 1)),
+            pltpu.SemaphoreType.DMA((n, Scatter.NRECV)),
+            pltpu.SemaphoreType.DMA((18,)),
+            pltpu.SemaphoreType.DMA((18,)),
+            pltpu.SemaphoreType.DMA((40,)),
+        ],
+        compiler_params=pltpu.CompilerParams(
+            collective_id=3, has_side_effects=True, vmem_limit_bytes=67000000
+        ),
+        name="backward",
+    )(lengths, order, rate, tokens, cot, *saved, *weights)
+    return out[:n], out[n], out[n + 1]
+
 
 def entering(value, axis, combine, identity, reverse):
     length, here = (lax.axis_size(axis), lax.axis_index(axis))
@@ -1144,168 +1368,36 @@
     cotangent,
 ):
     f32 = jnp.float32
-    bf16 = jnp.bfloat16
-    length, width = tokens.shape
     heads = decay_rate.shape[0]
-    head_size = width // heads
-    count = length // SPAN
-    first = lax.axis_index(AXIS) * length
-    places = first + jnp.arange(length, dtype=jnp.int32)
-    segments = segment_of(places, lengths, seq_order)
-    before = segment_of(jnp.reshape(first - 1, (1,)), lengths, seq_order)[0]
-    within, entry, leaving, passing, arrival, through = decay_tables(
-        segments, before, decay_rate, SPAN
-    )
     devices = lax.axis_size(AXIS)
     me = lax.axis_index(AXIS)
     mine = jnp.arange(devices, dtype=jnp.int32)[:, None] == me
-    gain_tile = jnp.where(mine, norm_gain.astype(f32)[None, :], 0.0).reshape(heads, head_size)
-    full, kept = forward(
+    gain_tile = jnp.where(mine, norm_gain.astype(f32)[None, :], 0.0).reshape(heads, -1)
+    full, saved = forward(
         lengths,
         seq_order,
         decay_rate,
         tokens,
+        cotangent,
         gain_tile,
         [w_key, w_value, w_query, w_unit, w_output, w_left, w_right, w_down],
     )
-    full_key, full_value, full_query, full_unit = [f.reshape(-1, width) for f in full[:4]]
-    full_gain = jnp.sum(full[4].reshape(devices, heads, head_size), axis=0).reshape(width)
-    full_output = full[5].reshape(-1, width)
-    full_left = jnp.concatenate([f.reshape(width, -1) for f in full[6:8]], axis=1)
-    full_right = jnp.concatenate([f.reshape(width, -1) for f in full[8:10]], axis=1)
-    full_down = full[10].reshape(-1, width)
-    ends = segment_of((jnp.arange(devices + 1, dtype=jnp.int32)) * length - 1, lengths, seq_order)
-    through_all = jnp.where(
-        (ends[1:] == ends[:-1])[:, None], jnp.exp(-decay_rate * length)[None, :], 0.0
-    )
-    hidden, keys, values, queries, key_pre, query_pre, unit_pre, mixing = kept[:8]
-    attended, state_low, mixed_in, middle, second, left_pre, right_pre, product = kept[8:]
-    block_shape = (count, SPAN, heads, head_size)
-    query_blocks = queries.reshape(block_shape)
-    key_blocks = keys.reshape(block_shape)
-    value_blocks = values.reshape(block_shape)
-    mixing, state_low = mixing[None], state_low[None]
-    inputs = tokens.astype(f32)
-    first_scale = row_scale(inputs)
-    normed = inputs * first_scale
-    keys_held = (key_blocks * leaving[..., None]).astype(bf16)
-    query_held = (query_blocks * entry[..., None]).astype(bf16)
-    attended_heads = attended.reshape(length, heads, head_size)
-    head_scale = row_scale(attended_heads)
-    unit_norm = (attended_heads * head_scale).reshape(length, width)
-    gated = unit_norm * full_gain
-    second_scale = row_scale(middle)
-    second_unit = middle * second_scale
-    result = (middle + jnp.dot(product, full_down, preferred_element_type=f32)).astype(bf16)
-    back_left, back_right, back_down = full_left, full_right, full_down
-    grad_product = jnp.einsum("td,fd->tf", cotangent, back_down, preferred_element_type=f32)
-    grad_left_pre = (grad_product * right_pre).astype(bf16)
-    grad_right_pre = (grad_product * left_pre).astype(bf16)
-    grad_w_down = jnp.einsum("tf,td->fd", product, cotangent, preferred_element_type=f32)
-    grad_w_left = jnp.einsum("td,tf->df", second, grad_left_pre, preferred_element_type=f32)
-    grad_w_right = jnp.einsum("td,tf->df", second, grad_right_pre, preferred_element_type=f32)
-    grad_second = jnp.einsum(
-        "tf,df->td", grad_left_pre, back_left, preferred_element_type=f32
-    ) + jnp.einsum("tf,df->td", grad_right_pre, back_right, preferred_element_type=f32)
-    grad_middle = cotangent.astype(f32) + second_scale * (
-        grad_second - second_unit * jnp.mean(grad_second * second_unit, axis=-1, keepdims=True)
-    )
-    back_query, back_key, back_value, back_unit = full_query, full_key, full_value, full_unit
-    back_output, back_gain = full_output, full_gain
-    grad_branch = grad_middle.astype(bf16)
-    grad_w_output = jnp.einsum(TD_TE, mixed_in, grad_branch, preferred_element_type=f32)
-    grad_mixed = jnp.einsum(TE_DE, grad_branch, back_output, preferred_element_type=f32)
-    grad_gated = grad_mixed * unit_pre
-    grad_unit_pre = (grad_mixed * gated).astype(bf16)
-    grad_gain = jnp.sum(grad_gated * unit_norm, axis=0)
-    grad_norm_heads = (grad_gated * back_gain.astype(f32)).reshape(length, heads, head_size)
-    norm_heads = unit_norm.reshape(length, heads, head_size)
-    grad_att = head_scale * (
-        grad_norm_heads
-        - norm_heads * jnp.mean(grad_norm_heads * norm_heads, axis=-1, keepdims=True)
-    )
-    grad_att_blocks = grad_att.astype(bf16).reshape(block_shape)
-    grad_mixing = jnp.einsum(
-        "nthf,nshf->nhts", grad_att_blocks, value_blocks, preferred_element_type=f32
-    )
-    grad_scores = (grad_mixing * within).astype(bf16)
-    grad_query_blocks = (
-        jnp.einsum("nhts,nshe->nthe", grad_scores, key_blocks, preferred_element_type=f32)
-        + jnp.einsum("nthf,nhef->nthe", grad_att_blocks, state_low, preferred_element_type=f32)
-        * entry[..., None]
-    )
-    grad_key_blocks = jnp.einsum(
-        "nhts,nthe->nshe", grad_scores, query_blocks, preferred_element_type=f32
-    )
-    grad_value_blocks = jnp.einsum(
-        "nhts,nthf->nshf", mixing, grad_att_blocks, preferred_element_type=f32
-    )
-    direct = jnp.einsum("nthe,nthf->nhef", query_held, grad_att_blocks, preferred_element_type=f32)
-    leaving_sum = jnp.sum(arrival[:, :, None, None] * direct, axis=0)
-    later = states(leaving_sum, through_all, True)
-    next_grads = [later]
-    grad_increment = jnp.stack(next_grads[::-1]).astype(bf16)
-    grad_keys_held = jnp.einsum(
-        "nhef,nshf->nshe", grad_increment, value_blocks, preferred_element_type=f32
-    )
-    grad_key_blocks = grad_key_blocks + grad_keys_held * leaving[..., None]
-    grad_value_blocks = grad_value_blocks + jnp.einsum(
-        "nshe,nhef->nshf", keys_held, grad_increment, preferred_element_type=f32
-    )
-    grad_query_pre = (grad_query_blocks.reshape(length, width) * silu_slope(query_pre)).astype(bf16)
-    grad_key_pre = (grad_key_blocks.reshape(length, width) * silu_slope(key_pre)).astype(bf16)
-    grad_value_pre = grad_value_blocks.reshape(length, width).astype(bf16)
-    grad_w_query = jnp.einsum(TD_TE, hidden, grad_query_pre, preferred_element_type=f32)
-    grad_w_key = jnp.einsum(TD_TE, hidden, grad_key_pre, preferred_element_type=f32)
-    grad_w_value = jnp.einsum(TD_TE, hidden, grad_value_pre, preferred_element_type=f32)
-    grad_w_unit = jnp.einsum(TD_TE, hidden, grad_unit_pre, preferred_element_type=f32)
-    def blocks(grad):
-        return grad.astype(bf16).reshape((4, 2, 2, 2, -1) + grad.shape[1:])
-
-    gain_rows = grad_gain.reshape(devices, 1, width // devices)
-    gain_rows = jnp.pad(gain_rows, ((0, 0), (0, 7), (0, 128 - width // devices)))
-    split = w_left.shape[1] // 2
-    grads = scatter_all(
-        [blocks(grad_w_down)]
-        + [blocks(grad_w_left[:, :split]), blocks(grad_w_left[:, split:])]
-        + [blocks(grad_w_right[:, :split]), blocks(grad_w_right[:, split:])]
-        + [blocks(grad_w_output), gain_rows.reshape(4, 2, 2, 2, 8, 128)]
-        + [blocks(grad_w_unit), blocks(grad_w_value), blocks(grad_w_key), blocks(grad_w_query)]
-    )
-    feed_grads = (
-        jnp.concatenate(grads[1:3], axis=1),
-        jnp.concatenate(grads[3:5], axis=1),
-        grads[0],
-    )
-    attention_grads = (
-        grads[10],
-        grads[9],
-        grads[8],
-        grads[7],
-        grads[5],
-        grads[6][0, : width // devices],
-    )
-    grad_hidden = (
-        jnp.einsum(TE_DE, grad_query_pre, back_query, preferred_element_type=f32)
-        + jnp.einsum(TE_DE, grad_key_pre, back_key, preferred_element_type=f32)
-        + jnp.einsum(TE_DE, grad_value_pre, back_value, preferred_element_type=f32)
-        + jnp.einsum(TE_DE, grad_unit_pre, back_unit, preferred_element_type=f32)
-    )
-    grad_inputs = grad_middle + first_scale * (
-        grad_hidden - normed * jnp.mean(grad_hidden * normed, axis=-1, keepdims=True)
-    )
+    grads, result, grad_inputs = backward(
+        lengths, seq_order, decay_rate, tokens, cotangent, saved, full[:4] + full[5:]
+    )
+    own = norm_gain.shape[0]
     return (
         result,
         grad_inputs,
-        attention_grads[0],
-        attention_grads[1],
-        attention_grads[2],
-        attention_grads[3],
-        attention_grads[4],
-        attention_grads[5],
-        feed_grads[0],
-        feed_grads[1],
-        feed_grads[2],
+        grads[9],
+        grads[11],
+        grads[10],
+        grads[8],
+        grads[6],
+        lax.dynamic_slice(grads[7].reshape(-1), (me * own,), (own,)),
+        jnp.concatenate(grads[2:4], axis=1),
+        jnp.concatenate(grads[4:6], axis=1),
+        jnp.concatenate(grads[0:2], axis=1),
     )
 
 

time: 379 us -> 285 us (0.75); the launches traced: 375 us -> 285 us
  matrix products: 42.7 us -> 0 us
  local copies, waits for them, and re-layouts: 34.3 us -> 8.41 us
  other arithmetic: 15.6 us -> 4.54 us
  Pallas kernels: 279 us -> 271 us
    dot_general x25 -> x0, matrix products: 42.7 us -> none  [the longest x1 6.34 us: body_kernels(): jnp.einsum('td,fd->tf', cotangent, back_down, preferred_element_type=f32)]
    pallas_call x2 -> x1, Pallas kernels: 142 us -> 128 us  [backward(): pl.pallas_call(backward_kernel, out_shape=[jax.ShapeDtypeStruct(b, f32) f...]
    unnamed x74 -> x19, local copies, waits for them, and re-layouts: 16.8 us -> 6.14 us
    slice x4 -> x0, local copies, waits for them, and re-layouts: 6.71 us -> none  [the longest x1 3.24 us: body_kernels(): grad_w_right[:, split:]]
    pallas_call x1, Pallas kernels: 137 us -> 143 us  [forward(): pl.pallas_call(forward_kernel, out_shape=[jax.ShapeDtypeStruct((4, 2, 2,...]
    reshape x3 -> x0, local copies, waits for them, and re-layouts: 5.19 us -> none  [the longest x1 2.56 us: body_kernels(): grad_query_blocks.reshape(length, width) * silu_slope(query_pre)]
    convert_element_type x5 -> x0, other arithmetic: 4.66 us -> none  [the longest x1 3.06 us: body_kernels(): (grad_key_blocks.reshape(length, width) * silu_slope(key_pre)).astype(bf16)]
    reduce_sum x9 -> x0, other arithmetic: 4.05 us -> none  [the longest x3 1.71 us: row_scale(): jnp.mean(values * values, axis=-1, keepdims=True) + EPSILON]
where the time goes in v3:
time: 285 us
  Pallas kernels  271 us (95%)
  local copies, waits for them, and re-layouts  8.41 us (3%)
  other arithmetic  4.54 us (2%)
    pallas_call x1, Pallas kernels, forward(): pl.pallas_call(forward_kernel, out_shape=[jax.ShapeDtypeStruct((4, 2, 2,...  143 us
    pallas_call x1, Pallas kernels, backward(): pl.pallas_call(backward_kernel, out_shape=[jax.ShapeDtypeStruct(b, f32) f...  128 us
    unnamed x19, local copies, waits for them, and re-layouts  6.14 us

profile of v3, /device:TPU:0, one launch (start us, length us, event | category | flops | bytes accessed | tf_op | source)
XLA Modules:
  0.0 284.6 jit_solution(8755258844378543656)
XLA Ops:
  0.7 0.7 broadcast_in_dim.30
  1.3 0.1 broadcast_in_dim.31
  1.4 0.1 broadcast_in_dim.28
  1.5 0.1 broadcast_in_dim.29
  1.6 0.6 broadcast_select_fusion.gain_own
  2.2 142.7 %forward.1 = (bf16[4,2,2,2,32,1024]{5,4,3,2,1,0:T(8,128)(2,1)}, bf16[4,2,2,2,32,1024]{5,4,3,2,1,0:T(8,128)(2,1)}, bf16[4,2,2,2,32,1024]{5,4,3,2,1,0:T(8,128)(2,1...) custom-call(s32[4]{0:T(128)} %lengths.3, s32[4]{0:T(128)} %order.3, ...), custom_call_target="tpu_custom_call" | custom-call | tf_op jit(solution)/shard_map/forward/pallas_call | solution.py:722
  144.8 128.3 %backward.1 = (f32[88,512]{1,0:T(8,128)}, f32[88,512]{1,0:T(8,128)}, f32[32,1408]{1,0:T(8,128)}, f32[32,1408]{1,0:T(8,128)}, f32[32,1408]{1,0:T(8,128)}, /*index...) custom-call(s32[4]{0:T(128)} %lengths.3, s32[4]{0:T(128)} %order.3, ...), custom_call_target="tpu_custom_call" | custom-call | tf_op jit(solution)/shard_map/backward/pallas_call | solution.py:1046
  273.2 0.0 copy-start
  273.2 0.0 copy-start.5
  273.2 0.0 copy-start.4
  273.2 1.4 dynamic_slice.3
  274.5 0.0 copy-start.3
  274.5 0.0 copy-start.2
  274.5 1.8 pad_maximum_fusion.2
  276.4 0.0 copy-start.1
  276.4 2.1 pad_maximum_fusion
  278.5 1.9 copy.32
  280.3 0.0 copy-done
  280.4 1.0 copy.33
  281.3 0.0 copy-done.5
  281.3 0.7 copy.34
  282.0 0.0 copy-done.4
  282.0 0.7 copy.35
  282.6 0.0 copy-done.3
  282.6 0.7 copy.36
  283.3 0.0 copy-done.2
  283.3 0.7 copy.37
  284.0 0.0 copy-done.1
  284.0 0.7 copy.38
  (1 shorter events, 0.0 us)
Async XLA Ops:
  273.2 7.2 %copy-start = (f32[256,1024]{1,0:T(8,128)S(1)}, f32[256,1024]{1,0:T(8,128)}, u32[]{:S(2)}) copy-start(f32[256,1024]{1,0:T(8,128)} %get-tuple-element.109) | copy-start | bytes 3145732
  273.2 8.2 %copy-start.5 = (f32[32,1024]{1,0:T(8,128)S(1)}, f32[32,1024]{1,0:T(8,128)}, u32[]{:S(2)}) copy-start(f32[32,1024]{1,0:T(8,128)} %get-tuple-element.110) | copy-start | bytes 393220
  273.2 8.8 %copy-start.4 = (f32[32,1024]{1,0:T(8,128)S(1)}, f32[32,1024]{1,0:T(8,128)}, u32[]{:S(2)}) copy-start(f32[32,1024]{1,0:T(8,128)} %get-tuple-element.111) | copy-start | bytes 393220
  274.5 8.1 %copy-start.3 = (f32[32,1024]{1,0:T(8,128)S(1)}, f32[32,1024]{1,0:T(8,128)}, u32[]{:S(2)}) copy-start(f32[32,1024]{1,0:T(8,128)} %get-tuple-element.112) | copy-start | bytes 393220
  274.5 8.8 %copy-start.2 = (f32[32,1024]{1,0:T(8,128)S(1)}, f32[32,1024]{1,0:T(8,128)}, u32[]{:S(2)}) copy-start(f32[32,1024]{1,0:T(8,128)} %get-tuple-element.113) | copy-start | bytes 393220
  276.4 7.6 %copy-start.1 = (f32[32,1024]{1,0:T(8,128)S(1)}, f32[32,1024]{1,0:T(8,128)}, u32[]{:S(2)}) copy-start(f32[32,1024]{1,0:T(8,128)} %get-tuple-element.114) | copy-start | bytes 393220

commit v4 on v3

--- a/solution.py
+++ b/solution.py
@@ -415,20 +415,34 @@
 
 
 class States:
-    PEERS = 10
-
-    def __init__(self, place, bounds, rate, reverse, value, met, planes, ready, out, send, recv):
-        self.bounds, self.reverse = bounds, reverse
-        self.value, self.met, self.planes, self.ready, self.out = value, met, planes, ready, out
+    def __init__(self, place, bounds, rate, reverse, value, buffers, send, recv):
+        self.bounds, self.reverse, self.rate = bounds, reverse, rate
+        self.value = value
+        self.theirs, self.sums, self.met, self.planes, self.ready, self.entered, self.give, self.out, self.sum = buffers
         self.send, self.recv = send, recv
-        self.z, self.r = place.z, lax.rem(place.me, 8)
-        self.plane = [self.z * 8 + lax.bitwise_xor(self.r, k) for k in range(8)]
-        self.level = [lax.rem(self.z + k, 4) * 8 + self.r for k in range(4)]
-        self.order = range(7, -1, -1) if reverse else range(8)
-        self.step = jnp.exp(jnp.full((1, 128), -SPAN * rate[self.r], jnp.float32))
-
-    def through(self, device):
-        return same_segment(self.bounds, device * SPAN - 1, device * SPAN + SPAN - 1)
+        self.z, self.c, self.c1 = place.z, place.c, place.c1
+        self.me, self.partner = place.me, place.to["p"]
+        self.q = lax.rem(place.me // 2, 4)
+        self.chip = [self.at(self.z, lax.bitwise_xor(self.q, k)) for k in range(4)]
+        self.level = [self.at(lax.rem(self.z + k, 4), self.q) for k in range(4)]
+        self.order = range(3, -1, -1) if reverse else range(4)
+        lead = 1 if reverse else 0
+        self.lead = jnp.where(self.c == lead, 1.0, 0.0).astype(jnp.float32)
+        base = self.me - self.c
+        self.lead_through = self.through(base + lead, 1)
+        self.last_through = self.through(base + 1 - lead, 1)
+        mine = rate[4 * self.c + self.q]
+        self.chip_step = jnp.exp(jnp.full((1, 128), -2 * SPAN * mine, jnp.float32))
+        self.plane_step = jnp.exp(jnp.full((1, 128), -8 * SPAN * mine, jnp.float32))
+
+    def at(self, z, q):
+        return (z * 4 + q) * 2 + self.c
+
+    def through(self, device, count):
+        return same_segment(self.bounds, device * SPAN - 1, (device + count) * SPAN - 1)
+
+    def step(self, k):
+        return jnp.exp(jnp.full((1, 128), -SPAN * self.rate[4 * self.c + k], jnp.float32))
 
     def copy(self, src, dst, k, peer):
         return pltpu.make_async_remote_copy(
@@ -441,36 +455,55 @@
         )
 
     def other(self, k):
-        return lax.bitwise_xor(self.r, k)
+        return lax.bitwise_xor(self.q, k)
+
+    def begin(self, made):
+        for one in made:
+            one.start()
+        return made
+
+    def terms(self, k):
+        mine, theirs = self.value[4 * self.c + k], self.theirs[k]
+        rest = 1.0 - self.lead
+        return self.lead * mine + rest * theirs, rest * mine + self.lead * theirs
 
     def spread(self):
-        self.first = [
-            self.copy(self.value.at[self.other(k)], self.met.at[self.r], k, self.plane[k])
-            for k in range(1, 8)
-        ]
-        for one in self.first:
-            one.start()
-        self.met[self.r] = self.value[self.r]
+        half = self.value.at[pl.ds(4 * self.c1, 4)]
+        self.sent = self.begin([self.copy(half, self.theirs, 0, self.partner)])
+
+    def join(self):
+        self.copy(self.theirs, self.theirs, 0, self.partner).wait_recv()
+        for k in range(4):
+            first, last = self.terms(k)
+            self.sums[k] = (self.last_through * self.step(k) * first + last).astype(jnp.bfloat16)
+        self.sent += self.begin(
+            [
+                self.copy(self.sums.at[self.other(k)], self.met.at[self.q], k, self.chip[k])
+                for k in range(1, 4)
+            ]
+        )
+        self.met[self.q] = self.sums[self.q]
 
     def total(self):
-        for k in range(1, 8):
-            self.copy(self.value.at[0], self.met.at[self.other(k)], k, self.plane[k]).wait_recv()
+        for k in range(1, 4):
+            self.copy(self.sums.at[0], self.met.at[self.other(k)], k, self.chip[k]).wait_recv()
         total = jnp.zeros(self.met.shape[1:], jnp.float32)
         for i in self.order:
-            total = self.through(self.z * 8 + i) * self.step * total + self.met[i]
-        self.planes[self.z] = total
+            through = self.through(self.z * 8 + 2 * i, 2)
+            total = through * self.chip_step * total + self.met[i].astype(jnp.float32)
+        self.planes[self.z] = total.astype(jnp.bfloat16)
         self.second = []
         for k in range(1, 4):
             far = self.z - k if self.reverse else self.z + k
             cond = far >= 0 if self.reverse else far <= 3
             made = self.copy(
-                self.planes.at[self.z], self.planes.at[self.z], 7 + k, far * 8 + self.r
+                self.planes.at[self.z], self.planes.at[self.z], 3 + k, self.at(far, self.q)
             )
             self.second.append((made, cond))
             pl.when(cond)(made.start)
 
     def back(self):
-        self.ready[8] = jnp.zeros(self.met.shape[1:], jnp.float32)
+        self.sum[...] = jnp.zeros(self.sum.shape, jnp.float32)
         for k in range(3, 0, -1):
             far = self.z + k if self.reverse else self.z - k
             cond = far <= 3 if self.reverse else far >= 0
@@ -478,34 +511,55 @@
             @pl.when(cond)
             def _():
                 self.copy(
-                    self.planes.at[self.z], self.planes.at[far], 7 + k, self.plane[0]
+                    self.planes.at[self.z], self.planes.at[far], 3 + k, self.partner
                 ).wait_recv()
-                kept = jnp.ones((1, 128), jnp.float32)
-                for i in range(8):
-                    kept = kept * (self.through(far * 8 + i) * self.step)
-                self.ready[8] = kept * self.ready[8] + self.planes[far]
-
-        total = self.ready[8]
+                kept = self.through(far * 8, 8) * self.plane_step
+                self.sum[...] = kept * self.sum[...] + self.planes[far].astype(jnp.float32)
+
+        total = self.sum[...]
         for i in self.order:
-            self.ready[i] = total
-            total = self.through(self.z * 8 + i) * self.step * total + self.met[i]
-        self.third = [
-            self.copy(self.ready.at[self.other(k)], self.out.at[self.r], 10 + k, self.plane[k])
-            for k in range(1, 8)
-        ]
-        for one in self.third:
-            one.start()
-        self.out[self.r] = self.ready[self.r]
+            self.ready[i] = total.astype(jnp.bfloat16)
+            through = self.through(self.z * 8 + 2 * i, 2)
+            total = through * self.chip_step * total + self.met[i].astype(jnp.float32)
+        self.sent += self.begin(
+            [
+                self.copy(self.ready.at[self.other(k)], self.entered.at[self.q], 6 + k, self.chip[k])
+                for k in range(1, 4)
+            ]
+        )
+        self.entered[self.q] = self.ready[self.q]
+
+    def part(self):
+        for k in range(1, 4):
+            self.copy(self.ready.at[0], self.entered.at[self.other(k)], 6 + k, self.chip[k]).wait_recv()
+        rest = 1.0 - self.lead
+        for k in range(4):
+            first, _ = self.terms(k)
+            entering = self.entered[k].astype(jnp.float32)
+            later = self.lead_through * self.step(k) * entering + first
+            self.out[4 * self.c + k] = (self.lead * entering + rest * later).astype(jnp.bfloat16)
+            self.give[k] = (self.lead * later + rest * entering).astype(jnp.bfloat16)
+        at = pl.ds(4 * self.c, 4)
+        self.sent += self.begin([self.copy(self.give, self.out.at[at], 10, self.partner)])
 
     def done(self):
-        for k in range(1, 8):
-            self.copy(self.ready.at[0], self.out.at[self.other(k)], 10 + k, self.plane[k]).wait_recv()
+        at = pl.ds(4 * self.c1, 4)
+        self.copy(self.give, self.out.at[at], 10, self.partner).wait_recv()
 
     def finish(self):
-        for one in self.first + self.third:
+        for one in self.sent:
             one.wait_send()
         for made, cond in self.second:
             pl.when(cond)(made.wait_send)
+
+
+def state_buffers():
+    cube, low = (4, 128, 128), jnp.bfloat16
+    return (
+        [pltpu.VMEM(cube, jnp.float32)]
+        + [pltpu.VMEM(cube, low)] * 6
+        + [pltpu.VMEM((8, 128, 128), low), pltpu.VMEM((128, 128), jnp.float32)]
+    )
 
 
 def greet_more(place):
@@ -536,7 +590,7 @@
     *refs,
 ):
     f32, bf16 = jnp.float32, jnp.bfloat16
-    n = 11
+    n = 12
     full, refs = refs[:n], refs[n:]
     saved, refs = refs[:SAVED_BACK], refs[SAVED_BACK:]
     kept, refs = refs[:SAVED_BACK], refs[SAVED_BACK:]
@@ -544,18 +598,21 @@
     (attended, state_low, mixed_rows, middle, second_rows, left, right, product) = kept[8:16]
     gain, down_term = kept[16:]
     (hidden, mixed, second, turned) = refs[:4]
-    (dist, entry, leaving, gains, value, met, planes, ready, arriving) = refs[4:13]
-    (narrow, wide, send, recv, state_send, state_recv, load_sem, save_sem) = refs[13:]
+    (dist, entry, leaving, gains, value) = refs[4:9]
+    state_refs, arriving = refs[9:18], refs[16]
+    (narrow, wide, send, recv, state_send, state_recv, load_sem, save_sem) = refs[18:]
     place = Place()
     half = s_left.shape[1] // 2
     own = [s_key, s_value, s_query, s_unit, gain_own, s_output]
     own += [s_left.at[:, pl.ds(0, half)], s_left.at[:, pl.ds(half, half)]]
-    own += [s_right.at[:, pl.ds(0, half)], s_right.at[:, pl.ds(half, half)], s_down]
+    own += [s_right.at[:, pl.ds(0, half)], s_right.at[:, pl.ds(half, half)]]
+    down_cols = s_down.shape[1] // 2
+    own += [s_down.at[:, pl.ds(i * down_cols, down_cols)] for i in (0, 1)]
     greet_more(place)
     made = [Gather(place, own[i], full[i], send, recv, i) for i in range(n)]
     bounds = bounds_of(lengths, order)
     states = States(
-        place, bounds, rate, False, value, met, planes, ready, arriving, state_send, state_recv
+        place, bounds, rate, False, value, state_refs, state_send, state_recv
     )
     slots = {0: narrow.at[0], 1: narrow.at[1], 2: narrow.at[0], 3: narrow.at[1], 4: gains}
     slots.update({5: narrow.at[0], 6: wide.at[0], 7: wide.at[1], 8: wide.at[0], 9: wide.at[1]})
@@ -652,44 +709,44 @@
     def gate(i, side, part):
         side[:, pl.ds(part * half, half)] = mm(second[...], weight(i))
 
-    def multiply():
+    def multiply(j):
         cols = cot.shape[1] // 2
 
-        @pl.loop(0, 2)
-        def _(j):
-            @pl.loop(0, half // 128)
-            def _(i):
-                at = pl.ds(pl.multiple_of(j * half + i * 128, 128), 128)
-                block = (left[:, at] * right[:, at]).astype(bf16).astype(f32)
-                turned[pl.ds(pl.multiple_of(i * 128, 128), 128), :] = block.T
-
-            both = pl.ds(2 * j, 2)
-            block = turned[...].reshape((2,) + product.shape[1:])
-            product[both] = block.astype(bf16)
-            rows = flat_rows(product[both, :, :, place.c1])
-            for m in range(2):
-                term = mm(rows, cot[:, pl.ds(m * cols, cols)])
-                down_term[m, both] = term.reshape((2,) + down_term.shape[2:]).astype(bf16)
-
-        save(13, 14, 15, 17)
-
-    tasks = {0: [start], 7: [key], 8: [increments], 9: [states.total, query], 10: [states.back, unit]}
-    tasks[11] = [states.done, attend]
-    tasks[12] = [output]
+        @pl.loop(0, half // 128)
+        def _(i):
+            at = pl.ds(pl.multiple_of(j * half + i * 128, 128), 128)
+            block = (left[:, at] * right[:, at]).astype(bf16).astype(f32)
+            turned[pl.ds(pl.multiple_of(i * 128, 128), 128), :] = block.T
+
+        both = pl.ds(2 * j, 2)
+        block = turned[...].reshape((2,) + product.shape[1:])
+        product[both] = block.astype(bf16)
+        rows = flat_rows(product[both, :, :, place.c1])
+        for m in range(2):
+            term = mm(rows, cot[:, pl.ds(m * cols, cols)])
+            down_term[m, both] = term.reshape((2,) + down_term.shape[2:]).astype(bf16)
+
+    tasks = {2: [start], 7: [key], 8: [increments], 8.5: [states.join], 9: [query], 9.5: [states.total]}
+    tasks.update({10: [unit], 10.5: [states.back], 11.5: [states.part], 12: [states.done, attend]})
+    tasks[12.5] = [output]
     tasks[13] = [lambda: gate(6, left, 0)]
-    tasks[14] = [lambda: gate(7, left, 1)]
-    tasks[15] = [lambda: gate(8, right, 0)]
-    tasks[16] = [lambda: gate(9, right, 1), multiply]
+    tasks[14] = [lambda: gate(7, left, 1), lambda: save(13)]
+    tasks[15] = [lambda: gate(8, right, 0), lambda: multiply(0)]
+    tasks[16] = [lambda: gate(9, right, 1), lambda: multiply(1), lambda: save(17, 15, 14)]
     loads = {}
     for step in range(n + 6):
+        i = step - 6
         for r in range(6):
             if 0 <= step - r < n:
                 made[step - r].round(r)
-        i = step - 6
-        if i - 1 in loads:
-            loads[i - 1].wait()
-        for task in tasks.get(step, []):
-            task()
+            if r == 0:
+                if i - 1 in loads:
+                    loads[i - 1].wait()
+                for task in tasks.get(step, []):
+                    task()
+            if r == 3:
+                for task in tasks.get(step + 0.5, []):
+                    task()
         if 0 <= i < n:
             made[i].pairs()
         if i in slots:
@@ -708,7 +765,8 @@
     wide = shards[5].shape[1]
     half = wide // 2
     blocks = [(s.shape, s.dtype) for s in shards[:4]] + [(gain_tile.shape, f32)]
-    blocks += [(shards[4].shape, bf16)] + [((32, half), bf16)] * 4 + [(shards[7].shape, bf16)]
+    blocks += [(shards[4].shape, bf16)] + [((32, half), bf16)] * 4
+    blocks += [((shards[7].shape[0], width // 2), bf16)] * 2
     square, cube = (size, width), (8, 128, 128)
     rows, down_rows = shards[4].shape[0], shards[7].shape[0]
     across = ((4, 2, 2, 2, rows, size), bf16)
@@ -730,8 +788,8 @@
         + [pltpu.VMEM((half, size), f32)]
         + [pltpu.VMEM((size, size), f32), pltpu.VMEM((size, 128), f32), pltpu.VMEM((size, 128), f32)]
         + [pltpu.VMEM((4, 2, 2, 2, 8, 128), f32)]
-        + [pltpu.VMEM(cube, f32), pltpu.VMEM(cube, f32), pltpu.VMEM((4, 128, 128), f32)]
-        + [pltpu.VMEM((9, 128, 128), f32), pltpu.VMEM(cube, f32)]
+        + [pltpu.VMEM(cube, f32)]
+        + state_buffers()
         + [
             pltpu.VMEM((2, 4, 2, 2, 2, 32, width), bf16),
             pltpu.VMEM((2, 4, 2, 2, 2, 32, half), bf16),
@@ -756,15 +814,16 @@
     (h_hidden, h_keys, h_values, h_queries, h_key_pre, h_query_pre, h_unit_pre, h_probs) = saved[:8]
     (h_attended, h_state_low, h_mixed, h_middle, h_second, h_left, h_right, h_product) = saved[8:16]
     h_gain, h_down = saved[16:]
-    w_in, refs = refs[:10], refs[10:]
-    (w_key, w_value, w_query, w_unit, w_output, w_l0, w_l1, w_r0, w_r1, w_down) = w_in
+    w_in, refs = refs[:11], refs[11:]
+    (w_key, w_value, w_query, w_unit, w_output, w_l0, w_l1, w_r0, w_r1) = w_in[:9]
+    w_down = w_in[9:]
     out, result_out, tokens_out, refs = refs[:n], refs[n], refs[n + 1], refs[n + 2 :]
     acc, came, refs = refs[:n], refs[n : 2 * n], refs[2 * n :]
     (part, gain_part, wd, down, wl, left, right, f1, f2, f3, f4) = refs[:11]
     (branch, ga, gup, gkp, gvp, result, glp, grp, rows, mixed, product) = refs[11:22]
     (probs, state_low, gain, gg, dist, entry, leaving) = refs[22:29]
-    (value, met, planes, ready, arriving) = refs[29:34]
-    (send, recv, state_send, state_recv, load_sem) = refs[34:]
+    value, state_refs, arriving = refs[29], refs[30:39], refs[37]
+    (send, recv, state_send, state_recv, load_sem) = refs[39:]
     place = Place()
     half = h_left.shape[1] // 2
     width = tokens.shape[1]
@@ -775,7 +834,7 @@
     greet_more(place)
     bounds = bounds_of(lengths, order)
     states = States(
-        place, bounds, rate, True, value, met, planes, ready, arriving, state_send, state_recv
+        place, bounds, rate, True, value, state_refs, state_send, state_recv
     )
     loads = {}
 
@@ -783,6 +842,11 @@
         copy = pltpu.make_async_copy(src, dst, load_sem.at[len(loads)])
         loads[name] = copy
         copy.start()
+
+    def load_down(i):
+        for m in range(2):
+            dst = wd.at[:, :, :, :, :, pl.ds(m * cols, cols)]
+            load("down%d%d" % (i, m), w_down[m].at[pl.ds(2 * i, 2)], dst)
 
     def loaded(*names):
         for name in names:
@@ -844,7 +908,7 @@
         spans_of(place.me * SPAN, bounds, dist, entry, leaving)
 
     def gates(i):
-        loaded("down%d" % i, "left%d" % i, "right%d" % i)
+        loaded("down%d0" % i, "down%d1" % i, "left%d" % i, "right%d" % i)
         pair = 2 * wd.shape[4]
 
         @pl.loop(0, 8)
@@ -858,7 +922,7 @@
         if i == 0:
             loaded("middle")
             f3[...] = f2[...] + mm_tn(product_of(0), down[...])
-            load("down1", w_down.at[pl.ds(2, 2)], wd)
+            load_down(1)
             load("left1", h_left.at[:, side(1)], left)
             load("right1", h_right.at[:, side(1)], right)
         else:
@@ -934,8 +998,6 @@
             f1[:, at] = mm_tn(grads, queries[:, at])
             right_w[:, at] = mm_tn(probs[h], low)
 
-        states.total()
-
     def hidden_part(name, grad, following, start):
         loaded(name)
         term = mm_nt(grad[...], weight(width))
@@ -944,7 +1006,6 @@
             load(*following)
 
     def unit_rest():
-        states.back()
         hidden_part("unit", gup, ("query", w_query, wn), True)
 
     def last_grads():
@@ -989,13 +1050,16 @@
         middle,
     ]
     tasks[6] = [spare, attention]
+    tasks[6.5] = [states.join]
     tasks[7] = [scores]
-    tasks[8] = [unit_rest]
+    tasks[7.5] = [states.total]
+    tasks[8] = [unit_rest, states.back]
+    tasks[8.5] = [states.part]
     tasks[9] = [last_grads]
     tasks[10] = [value_rest]
     tasks[11] = [inputs]
     load("product", h_product, product)
-    load("down0", w_down.at[pl.ds(0, 2)], wd)
+    load_down(0)
     load("left0", h_left.at[:, side(0)], left)
     load("right0", h_right.at[:, side(0)], right)
     load("middle", h_middle, f2)
@@ -1022,6 +1086,9 @@
         for r in range(2, 7):
             if 0 <= step - r < n:
                 made[step - r].round(r)
+            if r == 4:
+                for task in tasks.get(step + 0.5, []):
+                    task()
     for i, one in enumerate(made):
         if i < 2 or i == n - 1:
             one.handed()
@@ -1068,8 +1135,8 @@
         + [pltpu.VMEM((8, size, size), bf16), pltpu.VMEM(cube, bf16)]
         + [pltpu.VMEM((8, 128), f32)] * 2
         + [pltpu.VMEM((size, size), f32), pltpu.VMEM((size, 128), f32), pltpu.VMEM((size, 128), f32)]
-        + [pltpu.VMEM(cube, f32), pltpu.VMEM(cube, f32), pltpu.VMEM((4, 128, 128), f32)]
-        + [pltpu.VMEM((9, 128, 128), f32), pltpu.VMEM(cube, f32)]
+        + [pltpu.VMEM(cube, f32)]
+        + state_buffers()
         + [
             pltpu.SemaphoreType.DMA((n, Scatter.NSEND + 1)),
             pltpu.SemaphoreType.DMA((n, Scatter.NRECV)),
@@ -1083,6 +1150,42 @@
         name="backward",
     )(lengths, order, rate, tokens, cot, *saved, *weights)
     return out[:n], out[n], out[n + 1]
+
+
+def deliver_kernel(result, inputs, *refs):
+    grads, out = refs[:12], refs[12:]
+    out[0][...] = result[...]
+    out[1][...] = inputs[...]
+    for i, k in enumerate((9, 11, 10, 8, 6)):
+        out[2 + i][...] = grads[k][...]
+    me = lax.axis_index(AXIS)
+    row = grads[7][pl.ds(me // 4, 1), :]
+    own = jnp.zeros((1, 32), jnp.float32)
+    for k in range(4):
+        own = own + jnp.where(lax.rem(me, 4) == k, 1.0, 0.0) * row[:, 32 * k : 32 * k + 32]
+    out[7][...] = own
+    for i, k in enumerate((2, 4, 0)):
+        out[8 + i][...] = jnp.concatenate([grads[k][...], grads[k + 1][...]], axis=1)
+
+
+def deliver(result, inputs, grads):
+    f32 = jnp.float32
+    narrow = [grads[k].shape for k in (9, 11, 10, 8, 6)]
+    wide = [(grads[k].shape[0], 2 * grads[k].shape[1]) for k in (2, 4, 0)]
+    shapes = narrow + [(1, 32)] + wide
+    vmem = pl.BlockSpec(memory_space=pltpu.VMEM)
+    out = pl.pallas_call(
+        deliver_kernel,
+        out_shape=[
+            jax.ShapeDtypeStruct(result.shape, result.dtype),
+            jax.ShapeDtypeStruct(inputs.shape, f32),
+        ]
+        + [jax.ShapeDtypeStruct(s, f32) for s in shapes],
+        in_specs=[vmem] * 14,
+        out_specs=[vmem] * 11,
+        name="deliver",
+    )(result, inputs, *grads)
+    return (*out[:7], out[7].reshape(-1), *out[8:])
 
 
 def entering(value, axis, combine, identity, reverse):
@@ -1385,20 +1488,7 @@
     grads, result, grad_inputs = backward(
         lengths, seq_order, decay_rate, tokens, cotangent, saved, full[:4] + full[5:]
     )
-    own = norm_gain.shape[0]
-    return (
-        result,
-        grad_inputs,
-        grads[9],
-        grads[11],
-        grads[10],
-        grads[8],
-        grads[6],
-        lax.dynamic_slice(grads[7].reshape(-1), (me * own,), (own,)),
-        jnp.concatenate(grads[2:4], axis=1),
-        jnp.concatenate(grads[4:6], axis=1),
-        jnp.concatenate(grads[0:2], axis=1),
-    )
+    return deliver(result, grad_inputs, grads)
 
 
 def solution(mesh):

time: 285 us -> 259 us (0.909)
  Pallas kernels: 271 us -> 257 us
  local copies, waits for them, and re-layouts: 8.41 us -> 0.91 us
  other arithmetic: 4.54 us -> 0.61 us
    pallas_call x1, Pallas kernels: 143 us -> 131 us  [forward(): pl.pallas_call(forward_kernel, out_shape=[jax.ShapeDtypeStruct((4, 2, 2,...]
    pallas_call x1, Pallas kernels: 128 us -> 122 us  [backward(): pl.pallas_call(backward_kernel, out_shape=[jax.ShapeDtypeStruct(b, f32) f...]
    unnamed x19 -> x0, local copies, waits for them, and re-layouts: 6.14 us -> none
    concatenate x2 -> x0, other arithmetic: 3.93 us -> none  [the longest x1 2.12 us: body_kernels(): jnp.concatenate(grads[2:4], axis=1)]
    pallas_call x0 -> x1, Pallas kernels: none -> 3.66 us  [deliver(): pl.pallas_call(deliver_kernel, out_shape=[jax.ShapeDtypeStruct(result.sha...]
where the time goes in v4:
time: 259 us
  Pallas kernels  257 us (99%)
    pallas_call x1, Pallas kernels, forward(): pl.pallas_call(forward_kernel, out_shape=[jax.ShapeDtypeStruct((4, 2, 2,...  131 us
    pallas_call x1, Pallas kernels, backward(): pl.pallas_call(backward_kernel, out_shape=[jax.ShapeDtypeStruct(b, f32) f...  122 us

profile of v4, /device:TPU:0, one launch (start us, length us, event | category | flops | bytes accessed | tf_op | source)
XLA Modules:
  0.0 258.9 jit_solution(9422956094667693177)
XLA Ops:
  0.7 0.7 broadcast_in_dim.30
  1.3 0.1 broadcast_in_dim.31
  1.4 0.1 broadcast_in_dim.28
  1.5 0.1 broadcast_in_dim.29
  1.6 0.6 broadcast_select_fusion.gain_own
  2.2 131.3 %forward.1 = (bf16[4,2,2,2,32,1024]{5,4,3,2,1,0:T(8,128)(2,1)}, bf16[4,2,2,2,32,1024]{5,4,3,2,1,0:T(8,128)(2,1)}, bf16[4,2,2,2,32,1024]{5,4,3,2,1,0:T(8,128)(2,1...) custom-call(s32[4]{0:T(128)} %lengths.3, s32[4]{0:T(128)} %order.3, ...), custom_call_target="tpu_custom_call" | custom-call | tf_op jit(solution)/shard_map/forward/pallas_call | solution.py:780
  133.5 121.6 %backward.1 = (f32[88,512]{1,0:T(8,128)}, f32[88,512]{1,0:T(8,128)}, f32[32,1408]{1,0:T(8,128)}, f32[32,1408]{1,0:T(8,128)}, f32[32,1408]{1,0:T(8,128)}, /*index...) custom-call(s32[4]{0:T(128)} %lengths.3, s32[4]{0:T(128)} %order.3, ...), custom_call_target="tpu_custom_call" | custom-call | tf_op jit(solution)/shard_map/backward/pallas_call | solution.py:1113
  255.2 3.7 %deliver.1 = (bf16[256,1024]{1,0:T(8,128)(2,1)}, f32[256,1024]{1,0:T(8,128)}, f32[32,1024]{1,0:T(8,128)}, f32[32,1024]{1,0:T(8,128)}, f32[32,1024]{1,0:T(8,128)}...) custom-call(bf16[256,1024]{1,0:T(8,128)(2,1)} %get-tuple-element.94., ...), custom_call_target="tpu_custom_call" | custom-call | tf_op jit(solution)/shard_map/deliver/pallas_call | solution.py:1177
  (1 shorter events, 0.0 us)

commit v5 on v4

--- a/solution.py
+++ b/solution.py
@@ -135,6 +135,7 @@
             self.go("Co", "K", "Cn", inner)
             self.go("Co", "x", "Xo")
             self.go("Co", "y", "Yo")
+        outer = jnp.logical_not(inner)
         if r == 1:
             self.wait("Cs")
             self.go("Cs", "K", "Cf", inner)
@@ -144,9 +145,9 @@
             self.go("Xo", "y", "D0", even)
             self.wait("Yo")
             self.go("Yo", "x", "D0", odd)
+            self.relay("Cn")
         if r == 2:
-            self.wait("Cn")
-            self.go("Cn", "S", "Cn", inner)
+            pl.when(outer)(lambda: self.wait("Cn"))
             self.go("Cn", "x", "Xn")
             self.go("Cn", "y", "Yn")
             self.wait("Xs")
@@ -155,9 +156,9 @@
             self.go("Ys", "x", "D1", even)
             self.wait("D0")
             self.go("D0", "K", "En", inner)
+            self.relay("Cf")
         if r == 3:
-            self.wait("Cf")
-            self.go("Cf", "S", "Cf", inner)
+            pl.when(outer)(lambda: self.wait("Cf"))
             self.go("Cf", "x", "Xf")
             self.go("Cf", "y", "Yf")
             self.keep.wait()
@@ -166,17 +167,21 @@
             self.go("D1", "K", "Ef", inner)
             self.wait("Xn")
             self.wait("Yn")
+            self.relay("En")
         if r == 4:
-            self.wait("En")
-            self.go("En", "S", "En", inner)
+            pl.when(outer)(lambda: self.wait("En"))
             self.wait("Xf")
             self.pair("X")
             self.wait("Yf")
             self.pair("Y")
+            self.relay("Ef")
         if r == 5:
-            self.wait("Ef")
-            self.go("Ef", "S", "Ef", inner)
+            pl.when(outer)(lambda: self.wait("Ef"))
             self.pair("D")
+
+    def relay(self, name):
+        pl.when(self.p.inner)(lambda: self.wait(name))
+        self.go(name, "S", name, self.p.inner)
 
     def pairs(self):
         for g in self.GROUPS:
@@ -411,7 +416,12 @@
     return value.astype(jnp.float32).reshape(-1, value.shape[-1]).astype(jnp.bfloat16)
 
 
-SAVED_BACK = 18
+SAVED_BACK = 20
+
+
+def parts_of(width, last):
+    cuts = (0, width // 2, width - last, width)
+    return [(a, b - a) for a, b in zip(cuts, cuts[1:])]
 
 
 class States:
@@ -590,24 +600,30 @@
     *refs,
 ):
     f32, bf16 = jnp.float32, jnp.bfloat16
-    n = 12
+    n = 13
     full, refs = refs[:n], refs[n:]
     saved, refs = refs[:SAVED_BACK], refs[SAVED_BACK:]
     kept, refs = refs[:SAVED_BACK], refs[SAVED_BACK:]
     (hidden_rows, keys, values, queries, key_pre, query_pre, unit_pre, probs) = kept[:8]
     (attended, state_low, mixed_rows, middle, second_rows, left, right, product) = kept[8:16]
-    gain, down_term = kept[16:]
-    (hidden, mixed, second, turned) = refs[:4]
+    gain, down_terms = kept[16], kept[17:]
+    (hidden, mixed, second, turned, gain_tile) = refs[:5]
+    refs = refs[1:]
     (dist, entry, leaving, gains, value) = refs[4:9]
     state_refs, arriving = refs[9:18], refs[16]
     (narrow, wide, send, recv, state_send, state_recv, load_sem, save_sem) = refs[18:]
     place = Place()
     half = s_left.shape[1] // 2
-    own = [s_key, s_value, s_query, s_unit, gain_own, s_output]
+    own = [s_key, s_value, s_query, s_unit, gain_tile, s_output]
     own += [s_left.at[:, pl.ds(0, half)], s_left.at[:, pl.ds(half, half)]]
     own += [s_right.at[:, pl.ds(0, half)], s_right.at[:, pl.ds(half, half)]]
-    down_cols = s_down.shape[1] // 2
-    own += [s_down.at[:, pl.ds(i * down_cols, down_cols)] for i in (0, 1)]
+    parts = parts_of(s_down.shape[1], 128)
+    own += [s_down.at[:, pl.ds(a, size)] for a, size in parts]
+    lane = lax.broadcasted_iota(jnp.int32, gain_tile.shape, 1)
+    line = lax.broadcasted_iota(jnp.int32, gain_tile.shape, 0)
+    row = jnp.concatenate([gain_own[...].astype(f32)] * 4, axis=1)
+    here = (lane // 32 == lax.rem(place.me, 4)) & (line == place.me // 4)
+    gain_tile[...] = jnp.where(here, jnp.broadcast_to(row, gain_tile.shape), 0.0)
     greet_more(place)
     made = [Gather(place, own[i], full[i], send, recv, i) for i in range(n)]
     bounds = bounds_of(lengths, order)
@@ -710,8 +726,6 @@
         side[:, pl.ds(part * half, half)] = mm(second[...], weight(i))
 
     def multiply(j):
-        cols = cot.shape[1] // 2
-
         @pl.loop(0, half // 128)
         def _(i):
             at = pl.ds(pl.multiple_of(j * half + i * 128, 128), 128)
@@ -722,9 +736,9 @@
         block = turned[...].reshape((2,) + product.shape[1:])
         product[both] = block.astype(bf16)
         rows = flat_rows(product[both, :, :, place.c1])
-        for m in range(2):
-            term = mm(rows, cot[:, pl.ds(m * cols, cols)])
-            down_term[m, both] = term.reshape((2,) + down_term.shape[2:]).astype(bf16)
+        for (a, size), out in zip(parts, down_terms):
+            term = mm(rows, cot[:, pl.ds(a, size)])
+            out[both] = term.reshape((2,) + out.shape[1:]).astype(bf16)
 
     tasks = {2: [start], 7: [key], 8: [increments], 8.5: [states.join], 9: [query], 9.5: [states.total]}
     tasks.update({10: [unit], 10.5: [states.back], 11.5: [states.part], 12: [states.done, attend]})
@@ -732,12 +746,16 @@
     tasks[13] = [lambda: gate(6, left, 0)]
     tasks[14] = [lambda: gate(7, left, 1), lambda: save(13)]
     tasks[15] = [lambda: gate(8, right, 0), lambda: multiply(0)]
-    tasks[16] = [lambda: gate(9, right, 1), lambda: multiply(1), lambda: save(17, 15, 14)]
+    tasks[16] = [lambda: gate(9, right, 1), lambda: multiply(1), lambda: save(19, 18, 17, 15, 14)]
     loads = {}
     for step in range(n + 6):
         i = step - 6
         for r in range(6):
-            if 0 <= step - r < n:
+            if r == 0:
+                for k in (range(min(n, 1 + 2)) if step == 0 else [step + 2]):
+                    if k < n:
+                        made[k].round(0)
+            elif 0 <= step - r < n:
                 made[step - r].round(r)
             if r == 0:
                 if i - 1 in loads:
@@ -759,21 +777,22 @@
         copy.wait()
 
 
-def forward(lengths, order, rate, tokens, cot, gain_tile, shards):
+def forward(lengths, order, rate, tokens, cot, gain, shards):
     f32, bf16 = jnp.float32, jnp.bfloat16
     size, width = tokens.shape
     wide = shards[5].shape[1]
     half = wide // 2
-    blocks = [(s.shape, s.dtype) for s in shards[:4]] + [(gain_tile.shape, f32)]
+    blocks = [(s.shape, s.dtype) for s in shards[:4]] + [((8, 128), f32)]
     blocks += [(shards[4].shape, bf16)] + [((32, half), bf16)] * 4
-    blocks += [((shards[7].shape[0], width // 2), bf16)] * 2
+    parts = parts_of(width, 128)
+    blocks += [((shards[7].shape[0], p), bf16) for _, p in parts]
     square, cube = (size, width), (8, 128, 128)
     rows, down_rows = shards[4].shape[0], shards[7].shape[0]
     across = ((4, 2, 2, 2, rows, size), bf16)
     kept = [across] + [(square, bf16)] * 3 + [(square, f32)] * 3 + [((8, size, size), bf16)]
     kept += [(square, f32), (cube, bf16), across, (square, f32), across]
     kept += [((size, wide), f32)] * 2 + [((4, 2, 2, 2, down_rows, size), bf16), ((8, 128), f32)]
-    kept += [((2, 4, 2, 2, down_rows, width // 2), bf16)]
+    kept += [((4, 2, 2, down_rows, p), bf16) for _, p in parts]
     vmem, hbm = pl.BlockSpec(memory_space=pltpu.VMEM), pl.BlockSpec(memory_space=pltpu.HBM)
     smem = pl.BlockSpec(memory_space=pltpu.SMEM)
     n = len(blocks)
@@ -785,7 +804,7 @@
         out_specs=[hbm] * (n + len(kept)),
         scratch_shapes=[pltpu.VMEM(s, t) for s, t in kept]
         + [pltpu.VMEM(square, bf16)] * 3
-        + [pltpu.VMEM((half, size), f32)]
+        + [pltpu.VMEM((half, size), f32), pltpu.VMEM((8, 128), f32)]
         + [pltpu.VMEM((size, size), f32), pltpu.VMEM((size, 128), f32), pltpu.VMEM((size, 128), f32)]
         + [pltpu.VMEM((4, 2, 2, 2, 8, 128), f32)]
         + [pltpu.VMEM(cube, f32)]
@@ -804,17 +823,17 @@
             collective_id=0, has_side_effects=True, vmem_limit_bytes=VMEM_LIMIT
         ),
         name="forward",
-    )(lengths, order, rate, tokens, cot, gain_tile, *shards)
+    )(lengths, order, rate, tokens, cot, gain, *shards)
     return out[:n], out[n:]
 
 def backward_kernel(lengths, order, rate, tokens, cot, *refs):
     f32, bf16 = jnp.float32, jnp.bfloat16
-    n = 12
+    n = 14
     saved, refs = refs[:SAVED_BACK], refs[SAVED_BACK:]
     (h_hidden, h_keys, h_values, h_queries, h_key_pre, h_query_pre, h_unit_pre, h_probs) = saved[:8]
     (h_attended, h_state_low, h_mixed, h_middle, h_second, h_left, h_right, h_product) = saved[8:16]
-    h_gain, h_down = saved[16:]
-    w_in, refs = refs[:11], refs[11:]
+    h_gain, h_down = saved[16], saved[17:]
+    w_in, refs = refs[:12], refs[12:]
     (w_key, w_value, w_query, w_unit, w_output, w_l0, w_l1, w_r0, w_r1) = w_in[:9]
     w_down = w_in[9:]
     out, result_out, tokens_out, refs = refs[:n], refs[n], refs[n + 1], refs[n + 2 :]
@@ -844,8 +863,8 @@
         copy.start()
 
     def load_down(i):
-        for m in range(2):
-            dst = wd.at[:, :, :, :, :, pl.ds(m * cols, cols)]
+        for m, (a, size) in enumerate(parts):
+            dst = wd.at[:, :, :, :, :, pl.ds(a, size)]
             load("down%d%d" % (i, m), w_down[m].at[pl.ds(2 * i, 2)], dst)
 
     def loaded(*names):
@@ -893,12 +912,19 @@
 
     wide = part.at[:, :, :, :, pl.ds(0, half)]
     narrow = part.at[:, :, :, :, pl.ds(0, width)]
-    cols = width // 2
-    pieces = [(h_down.at[m], Piece(product, 88, cot.at[:, pl.ds(m * cols, cols)], cols)) for m in (0, 1)]
+    parts = parts_of(width, 128)
+    pieces = []
+    for m in (2, 1, 0):
+        a, size = parts[m]
+        pieces.append((h_down[m], Piece(product, 88, cot.at[:, pl.ds(a, size)], size)))
     pieces += [(wide, Piece(rows, 32, glp.at[:, side(i)], half)) for i in (0, 1)]
     pieces += [(wide, Piece(rows, 32, grp.at[:, side(i)], half)) for i in (0, 1)]
     pieces += [(narrow, Piece(mixed, 32, branch, width)), (gain_part, Gain())]
-    pieces += [(narrow, Piece(rows, 32, g, width)) for g in (gup, gqp, gvp, gkp)]
+    pieces += [(narrow, Piece(rows, 32, g, width)) for g in (gup, gqp, gvp)]
+    last = width // 4
+    for a, size in ((0, width - last), (width - last, last)):
+        view = part.at[:, :, :, :, pl.ds(0, size)]
+        pieces.append((view, Piece(rows, 32, gkp.at[:, pl.ds(a, size)], size)))
     made = [
         Scatter(place, pieces[i][0], acc[i], pieces[i][1], came[i], out[i], send, recv, i)
         for i in range(n)
@@ -908,7 +934,7 @@
         spans_of(place.me * SPAN, bounds, dist, entry, leaving)
 
     def gates(i):
-        loaded("down%d0" % i, "down%d1" % i, "left%d" % i, "right%d" % i)
+        loaded("down%d0" % i, "down%d1" % i, "down%d2" % i, "left%d" % i, "right%d" % i)
         pair = 2 * wd.shape[4]
 
         @pl.loop(0, 8)
@@ -1039,25 +1065,25 @@
 
         load("tokens", f3, tokens_out)
 
-    before = {1: lambda: loaded("product"), 2: lambda: loaded("second"), 6: lambda: loaded("mixed")}
-    before[8] = lambda: loaded("hidden")
-    tasks = {0: [begin], 1: [lambda: gates(0)], 2: [lambda: gates(1)]}
-    tasks[3] = [lambda: second_part("l0", glp, 0, ("l1", w_l1, wl), True)]
-    tasks[4] = [lambda: second_part("l1", glp, 1, ("r0", w_r0, wl), False)]
-    tasks[5] = [
+    before = {1: lambda: loaded("product"), 3: lambda: loaded("second"), 7: lambda: loaded("mixed")}
+    before[9] = lambda: loaded("hidden")
+    tasks = {0: [begin], 2: [lambda: gates(0)], 3: [lambda: gates(1)]}
+    tasks[4] = [lambda: second_part("l0", glp, 0, ("l1", w_l1, wl), True)]
+    tasks[5] = [lambda: second_part("l1", glp, 1, ("r0", w_r0, wl), False)]
+    tasks[6] = [
         lambda: second_part("r0", grp, 0, ("r1", w_r1, wl), False),
         lambda: second_part("r1", grp, 1, ("output", w_output, wn), False),
         middle,
     ]
-    tasks[6] = [spare, attention]
-    tasks[6.5] = [states.join]
-    tasks[7] = [scores]
-    tasks[7.5] = [states.total]
-    tasks[8] = [unit_rest, states.back]
-    tasks[8.5] = [states.part]
-    tasks[9] = [last_grads]
-    tasks[10] = [value_rest]
-    tasks[11] = [inputs]
+    tasks[7] = [spare, attention]
+    tasks[7.5] = [states.join]
+    tasks[8] = [scores]
+    tasks[8.5] = [states.total]
+    tasks[9] = [unit_rest, states.back]
+    tasks[9.5] = [states.part]
+    tasks[10] = [last_grads]
+    tasks[11] = [value_rest]
+    tasks[12] = [inputs]
     load("product", h_product, product)
     load_down(0)
     load("left0", h_left.at[:, side(0)], left)
@@ -1071,13 +1097,15 @@
     load("probs", h_probs, probs)
     load("state_low", h_state_low, state_low)
     for step in range(n + 6):
-        if step < n:
-            if step in before:
-                before[step]()
-            if step > 2:
+        if step == 0:
+            for i in range(3):
+                made[i].round(0)
+        if step in before:
+            before[step]()
+        if 2 < step < n:
+            if step > 3:
                 made[step - 1].handed()
-            if step > 1:
-                pieces[step][1].first()
+            pieces[step][1].first()
             made[step].round(0)
         if 0 < step <= n:
             made[step - 1].round(1)
@@ -1090,7 +1118,7 @@
                 for task in tasks.get(step + 0.5, []):
                     task()
     for i, one in enumerate(made):
-        if i < 2 or i == n - 1:
+        if i < 3 or i == n - 1:
             one.handed()
         one.finish()
     states.finish()
@@ -1104,8 +1132,10 @@
     half = wide // 2
     rows = width // 32
     down_rows = wide // 32
-    blocks = [((down_rows, width // 2), bf16)] * 2 + [((rows, half), bf16)] * 4
-    blocks += [((rows, width), bf16), ((8, 128), f32)] + [((rows, width), bf16)] * 4
+    parts, last = parts_of(width, 128), width // 4
+    blocks = [((down_rows, parts[m][1]), bf16) for m in (2, 1, 0)] + [((rows, half), bf16)] * 4
+    blocks += [((rows, width), bf16), ((8, 128), f32)] + [((rows, width), bf16)] * 3
+    blocks += [((rows, width - last), bf16), ((rows, last), bf16)]
     n = len(blocks)
     square, cube = (size, width), (8, 128, 128)
     vmem, hbm = pl.BlockSpec(memory_space=pltpu.VMEM), pl.BlockSpec(memory_space=pltpu.HBM)
@@ -1152,27 +1182,33 @@
     return out[:n], out[n], out[n + 1]
 
 
+RESULTS = ((10,), (12, 13), (11,), (9,), (7,), (8,), (3, 4), (5, 6), (2, 1, 0))
+
+
 def deliver_kernel(result, inputs, *refs):
-    grads, out = refs[:12], refs[12:]
+    grads, out = refs[:14], refs[14:]
     out[0][...] = result[...]
     out[1][...] = inputs[...]
-    for i, k in enumerate((9, 11, 10, 8, 6)):
-        out[2 + i][...] = grads[k][...]
-    me = lax.axis_index(AXIS)
-    row = grads[7][pl.ds(me // 4, 1), :]
-    own = jnp.zeros((1, 32), jnp.float32)
-    for k in range(4):
-        own = own + jnp.where(lax.rem(me, 4) == k, 1.0, 0.0) * row[:, 32 * k : 32 * k + 32]
-    out[7][...] = own
-    for i, k in enumerate((2, 4, 0)):
-        out[8 + i][...] = jnp.concatenate([grads[k][...], grads[k + 1][...]], axis=1)
+    for dst, found in zip(out[2:], RESULTS):
+        if found == (8,):
+            me = lax.axis_index(AXIS)
+            row = grads[8][pl.ds(me // 4, 1), :]
+            own = jnp.zeros((1, 32), jnp.float32)
+            for k in range(4):
+                own = own + jnp.where(lax.rem(me, 4) == k, 1.0, 0.0) * row[:, 32 * k : 32 * k + 32]
+            dst[...] = own
+        else:
+            at = 0
+            for k in found:
+                size = grads[k].shape[1]
+                dst[:, pl.ds(at, size)] = grads[k][...]
+                at += size
 
 
 def deliver(result, inputs, grads):
     f32 = jnp.float32
-    narrow = [grads[k].shape for k in (9, 11, 10, 8, 6)]
-    wide = [(grads[k].shape[0], 2 * grads[k].shape[1]) for k in (2, 4, 0)]
-    shapes = narrow + [(1, 32)] + wide
+    shapes = [(grads[k[0]].shape[0], sum(grads[i].shape[1] for i in k)) for k in RESULTS]
+    shapes[5] = (1, 32)
     vmem = pl.BlockSpec(memory_space=pltpu.VMEM)
     out = pl.pallas_call(
         deliver_kernel,
@@ -1181,7 +1217,7 @@
             jax.ShapeDtypeStruct(inputs.shape, f32),
         ]
         + [jax.ShapeDtypeStruct(s, f32) for s in shapes],
-        in_specs=[vmem] * 14,
+        in_specs=[vmem] * 16,
         out_specs=[vmem] * 11,
         name="deliver",
     )(result, inputs, *grads)
@@ -1470,19 +1506,13 @@
     w_down,
     cotangent,
 ):
-    f32 = jnp.float32
-    heads = decay_rate.shape[0]
-    devices = lax.axis_size(AXIS)
-    me = lax.axis_index(AXIS)
-    mine = jnp.arange(devices, dtype=jnp.int32)[:, None] == me
-    gain_tile = jnp.where(mine, norm_gain.astype(f32)[None, :], 0.0).reshape(heads, -1)
     full, saved = forward(
         lengths,
         seq_order,
         decay_rate,
         tokens,
         cotangent,
-        gain_tile,
+        norm_gain.reshape(1, -1),
         [w_key, w_value, w_query, w_unit, w_output, w_left, w_right, w_down],
     )
     grads, result, grad_inputs = backward(

time: 259 us -> 252 us (0.973)
  Pallas kernels: 257 us -> 251 us
    pallas_call x1, Pallas kernels: 131 us -> 125 us  [forward(): pl.pallas_call(forward_kernel, out_shape=[jax.ShapeDtypeStruct((4, 2, 2,...]
where the time goes in v5:
time: 252 us
  Pallas kernels  251 us (100%)
    pallas_call x1, Pallas kernels, forward(): pl.pallas_call(forward_kernel, out_shape=[jax.ShapeDtypeStruct((4, 2, 2,...  125 us
    pallas_call x1, Pallas kernels, backward(): pl.pallas_call(backward_kernel, out_shape=[jax.ShapeDtypeStruct(b, f32) f...  123 us

profile of v5, /device:TPU:0, one launch (start us, length us, event | category | flops | bytes accessed | tf_op | source)
XLA Modules:
  0.0 251.6 jit_solution(17776106779032232162)
XLA Ops:
  0.6 124.5 %forward.1 = (bf16[4,2,2,2,32,1024]{5,4,3,2,1,0:T(8,128)(2,1)}, bf16[4,2,2,2,32,1024]{5,4,3,2,1,0:T(8,128)(2,1)}, bf16[4,2,2,2,32,1024]{5,4,3,2,1,0:T(8,128)(2,1...) custom-call(s32[4]{0:T(128)} %lengths.3, s32[4]{0:T(128)} %order.3, ...), custom_call_target="tpu_custom_call" | custom-call | tf_op jit(solution)/shard_map/forward/pallas_call | solution.py:799
  125.2 122.7 %backward.1 = (f32[88,128]{1,0:T(8,128)}, f32[88,384]{1,0:T(8,128)}, f32[88,512]{1,0:T(8,128)}, f32[32,1408]{1,0:T(8,128)}, f32[32,1408]{1,0:T(8,128)}, /*index=...) custom-call(s32[4]{0:T(128)} %lengths.3, s32[4]{0:T(128)} %order.3, ...), custom_call_target="tpu_custom_call" | custom-call | tf_op jit(solution)/shard_map/backward/pallas_call | solution.py:1143
  247.8 3.7 %deliver.1 = (bf16[256,1024]{1,0:T(8,128)(2,1)}, f32[256,1024]{1,0:T(8,128)}, f32[32,1024]{1,0:T(8,128)}, f32[32,1024]{1,0:T(8,128)}, f32[32,1024]{1,0:T(8,128)}...) custom-call(bf16[256,1024]{1,0:T(8,128)(2,1)} %get-tuple-element.102, ...), custom_call_target="tpu_custom_call" | custom-call | tf_op jit(solution)/shard_map/deliver/pallas_call | solution.py:1213

commit v6 on v5

--- a/solution.py
+++ b/solution.py
@@ -259,6 +259,10 @@
         outer = jnp.logical_not(inner)
         ze, zo, near, far = self.ze, self.zo, p.near, p.far
         if r == 0:
+            if self.term is None:
+                self.given = pltpu.make_async_copy(self.part, self.acc, self.send.at[self.index, self.NSEND])
+                self.given.start()
+                return
             self.given = pltpu.make_async_remote_copy(
                 src_ref=self.part,
                 dst_ref=self.acc,
@@ -269,8 +273,11 @@
             )
             self.given.start()
         if r == 1:
-            arrived(self.acc, self.send.at[self.index, 0], self.recv.at[self.index, 19], p)
-            self.term.second(self.acc)
+            if self.term is None:
+                self.given.wait()
+            else:
+                arrived(self.acc, self.send.at[self.index, 0], self.recv.at[self.index, 19], p)
+                self.term.second(self.acc)
             self.go(self.D(far), "S", "Ef", outer)
             self.go(self.D(near), "S", "En", outer)
             self.go(self.X(far), "x", far)
@@ -417,6 +424,8 @@
 
 
 SAVED_BACK = 20
+FIRST = 1
+ORDER = (FIRST, 2, 0)
 
 
 def parts_of(width, last):
@@ -582,23 +591,8 @@
     pl.semaphore_wait(barrier, len(peers))
 
 
-def forward_kernel(
-    lengths,
-    order,
-    rate,
-    tokens,
-    cot,
-    gain_own,
-    s_key,
-    s_value,
-    s_query,
-    s_unit,
-    s_output,
-    s_left,
-    s_right,
-    s_down,
-    *refs,
-):
+def forward_kernel(lengths, order, rate, gain_own, *refs):
+    inputs, refs = refs[:10], refs[10:]
     f32, bf16 = jnp.float32, jnp.bfloat16
     n = 13
     full, refs = refs[:n], refs[n:]
@@ -607,8 +601,17 @@
     (hidden_rows, keys, values, queries, key_pre, query_pre, unit_pre, probs) = kept[:8]
     (attended, state_low, mixed_rows, middle, second_rows, left, right, product) = kept[8:16]
     gain, down_terms = kept[16], kept[17:]
+    held, refs = refs[:10], refs[10:]
+    (s_key, s_value, s_query, s_unit, s_output, tokens, s_left, s_right, s_down, cot) = held
+    (in_sem, first_send, first_recv, down_first), refs = refs[:4], refs[4:]
     (hidden, mixed, second, turned, gain_tile) = refs[:5]
     refs = refs[1:]
+    fetched = [
+        pltpu.make_async_copy(src, dst, in_sem.at[i])
+        for i, (src, dst) in enumerate(zip(inputs, held))
+    ]
+    for copy in fetched:
+        copy.start()
     (dist, entry, leaving, gains, value) = refs[4:9]
     state_refs, arriving = refs[9:18], refs[16]
     (narrow, wide, send, recv, state_send, state_recv, load_sem, save_sem) = refs[18:]
@@ -651,6 +654,8 @@
             rows[i // 2, i % 2] = block.reshape((2, 2) + rows.shape[4:]).astype(bf16)
 
     def start():
+        fetched[5].wait()
+        fetched[9].wait()
         x = tokens[...].astype(f32)
         hidden[...] = (x * norm_scale(x)).astype(bf16)
         spans_of(place.me * SPAN, bounds, dist, entry, leaving)
@@ -736,9 +741,30 @@
         block = turned[...].reshape((2,) + product.shape[1:])
         product[both] = block.astype(bf16)
         rows = flat_rows(product[both, :, :, place.c1])
-        for (a, size), out in zip(parts, down_terms):
+        for m, (a, size) in enumerate(parts):
+            out = down_first if m == FIRST else down_terms[m]
             term = mm(rows, cot[:, pl.ds(a, size)])
             out[both] = term.reshape((2,) + out.shape[1:]).astype(bf16)
+        exchange(j).start()
+
+    def exchange(j):
+        both = pl.ds(2 * j, 2)
+        return pltpu.make_async_remote_copy(
+            src_ref=down_first.at[both],
+            dst_ref=down_terms[FIRST].at[both],
+            send_sem=first_send.at[j],
+            recv_sem=first_recv.at[j],
+            device_id=place.to["p"],
+            device_id_type=LOGICAL,
+        )
+
+    def joined(j):
+        exchange(j).wait_recv()
+        both, out = pl.ds(2 * j, 2), down_terms[FIRST]
+        a, size = parts[FIRST]
+        rows = flat_rows(product[both, :, :, place.c])
+        term = mm(rows, cot[:, pl.ds(a, size)]).reshape((2,) + out.shape[1:])
+        out[both] = (out[both].astype(f32) + term).astype(bf16)
 
     tasks = {2: [start], 7: [key], 8: [increments], 8.5: [states.join], 9: [query], 9.5: [states.total]}
     tasks.update({10: [unit], 10.5: [states.back], 11.5: [states.part], 12: [states.done, attend]})
@@ -746,13 +772,18 @@
     tasks[13] = [lambda: gate(6, left, 0)]
     tasks[14] = [lambda: gate(7, left, 1), lambda: save(13)]
     tasks[15] = [lambda: gate(8, right, 0), lambda: multiply(0)]
-    tasks[16] = [lambda: gate(9, right, 1), lambda: multiply(1), lambda: save(19, 18, 17, 15, 14)]
+    tasks[16] = [lambda: gate(9, right, 1), lambda: multiply(1), lambda: save(19, 17, 15, 14)]
+    tasks[16] += [lambda: joined(0)]
+    tasks[18] = [lambda: joined(1), lambda: save(18)]
+    needs = {0: 0, 1: 1, 2: 2, 3: 3, 5: 4, 6: 6, 8: 7, 10: 8}
     loads = {}
     for step in range(n + 6):
         i = step - 6
         for r in range(6):
             if r == 0:
-                for k in (range(min(n, 1 + 2)) if step == 0 else [step + 2]):
+                for k in range(3) if step == 0 else [step + 2]:
+                    if k in needs:
+                        fetched[needs[k]].wait()
                     if k < n:
                         made[k].round(0)
             elif 0 <= step - r < n:
@@ -773,6 +804,8 @@
     for one in made:
         one.finish()
     states.finish()
+    for j in range(2):
+        exchange(j).wait_send()
     for copy in saves:
         copy.wait()
 
@@ -796,13 +829,18 @@
     vmem, hbm = pl.BlockSpec(memory_space=pltpu.VMEM), pl.BlockSpec(memory_space=pltpu.HBM)
     smem = pl.BlockSpec(memory_space=pltpu.SMEM)
     n = len(blocks)
+    inputs = [*shards[:5], tokens, *shards[5:], cot]
     out = pl.pallas_call(
         forward_kernel,
         out_shape=[jax.ShapeDtypeStruct((4, 2, 2, 2) + s, t) for s, t in blocks]
         + [jax.ShapeDtypeStruct(s, t) for s, t in kept],
-        in_specs=[smem] * 3 + [vmem] * 11,
+        in_specs=[smem] * 3 + [vmem] + [hbm] * 10,
         out_specs=[hbm] * (n + len(kept)),
         scratch_shapes=[pltpu.VMEM(s, t) for s, t in kept]
+        + [pltpu.VMEM(s.shape, s.dtype) for s in inputs]
+        + [pltpu.SemaphoreType.DMA((10,))]
+        + [pltpu.SemaphoreType.DMA((2,))] * 2
+        + [pltpu.VMEM((4, 2, 2, down_rows, parts[FIRST][1]), bf16)]
         + [pltpu.VMEM(square, bf16)] * 3
         + [pltpu.VMEM((half, size), f32), pltpu.VMEM((8, 128), f32)]
         + [pltpu.VMEM((size, size), f32), pltpu.VMEM((size, 128), f32), pltpu.VMEM((size, 128), f32)]
@@ -823,10 +861,10 @@
             collective_id=0, has_side_effects=True, vmem_limit_bytes=VMEM_LIMIT
         ),
         name="forward",
-    )(lengths, order, rate, tokens, cot, gain, *shards)
+    )(lengths, order, rate, gain, *inputs)
     return out[:n], out[n:]
 
-def backward_kernel(lengths, order, rate, tokens, cot, *refs):
+def backward_kernel(lengths, order, rate, h_tokens, h_cot, *refs):
     f32, bf16 = jnp.float32, jnp.bfloat16
     n = 14
     saved, refs = refs[:SAVED_BACK], refs[SAVED_BACK:]
@@ -836,13 +874,14 @@
     w_in, refs = refs[:12], refs[12:]
     (w_key, w_value, w_query, w_unit, w_output, w_l0, w_l1, w_r0, w_r1) = w_in[:9]
     w_down = w_in[9:]
-    out, result_out, tokens_out, refs = refs[:n], refs[n], refs[n + 1], refs[n + 2 :]
+    sums, result_out, tokens_out, refs = refs[:n], refs[n], refs[n + 1], refs[n + 2 :]
+    out, tokens, cot, refs = refs[:n], refs[n], refs[n + 1], refs[n + 2 :]
     acc, came, refs = refs[:n], refs[n : 2 * n], refs[2 * n :]
     (part, gain_part, wd, down, wl, left, right, f1, f2, f3, f4) = refs[:11]
     (branch, ga, gup, gkp, gvp, result, glp, grp, rows, mixed, product) = refs[11:22]
     (probs, state_low, gain, gg, dist, entry, leaving) = refs[22:29]
     value, state_refs, arriving = refs[29], refs[30:39], refs[37]
-    (send, recv, state_send, state_recv, load_sem) = refs[39:]
+    (send, recv, state_send, state_recv, load_sem, out_sem) = refs[39:]
     place = Place()
     half = h_left.shape[1] // 2
     width = tokens.shape[1]
@@ -914,9 +953,10 @@
     narrow = part.at[:, :, :, :, pl.ds(0, width)]
     parts = parts_of(width, 128)
     pieces = []
-    for m in (2, 1, 0):
+    for m in ORDER:
         a, size = parts[m]
-        pieces.append((h_down[m], Piece(product, 88, cot.at[:, pl.ds(a, size)], size)))
+        piece = None if m == FIRST else Piece(product, 88, cot.at[:, pl.ds(a, size)], size)
+        pieces.append((h_down[m], piece))
     pieces += [(wide, Piece(rows, 32, glp.at[:, side(i)], half)) for i in (0, 1)]
     pieces += [(wide, Piece(rows, 32, grp.at[:, side(i)], half)) for i in (0, 1)]
     pieces += [(narrow, Piece(mixed, 32, branch, width)), (gain_part, Gain())]
@@ -1054,6 +1094,7 @@
 
     def inputs():
         hidden_part("key", gkp, None, False)
+        loaded("input")
 
         @pl.loop(0, SPAN // 16)
         def _(i):
@@ -1065,7 +1106,7 @@
 
         load("tokens", f3, tokens_out)
 
-    before = {1: lambda: loaded("product"), 3: lambda: loaded("second"), 7: lambda: loaded("mixed")}
+    before = {2: lambda: loaded("product", "cot"), 3: lambda: loaded("second"), 7: lambda: loaded("mixed")}
     before[9] = lambda: loaded("hidden")
     tasks = {0: [begin], 2: [lambda: gates(0)], 3: [lambda: gates(1)]}
     tasks[4] = [lambda: second_part("l0", glp, 0, ("l1", w_l1, wl), True)]
@@ -1084,7 +1125,10 @@
     tasks[10] = [last_grads]
     tasks[11] = [value_rest]
     tasks[12] = [inputs]
+    for i in range(3):
+        made[i].round(0)
     load("product", h_product, product)
+    load("cot", h_cot, cot)
     load_down(0)
     load("left0", h_left.at[:, side(0)], left)
     load("right0", h_right.at[:, side(0)], right)
@@ -1096,10 +1140,11 @@
     load("query_pre", h_query_pre, f4)
     load("probs", h_probs, probs)
     load("state_low", h_state_low, state_low)
+    load("input", h_tokens, tokens)
+    def given(i):
+        return pltpu.make_async_copy(out[i], sums[i], out_sem.at[i])
+
     for step in range(n + 6):
-        if step == 0:
-            for i in range(3):
-                made[i].round(0)
         if step in before:
             before[step]()
         if 2 < step < n:
@@ -1114,12 +1159,15 @@
         for r in range(2, 7):
             if 0 <= step - r < n:
                 made[step - r].round(r)
+                if r == 6:
+                    given(step - r).start()
             if r == 4:
                 for task in tasks.get(step + 0.5, []):
                     task()
     for i, one in enumerate(made):
-        if i < 3 or i == n - 1:
+        if i in (1, 2, n - 1):
             one.handed()
+        given(i).wait()
         one.finish()
     states.finish()
     loaded("result", "tokens")
@@ -1133,20 +1181,22 @@
     rows = width // 32
     down_rows = wide // 32
     parts, last = parts_of(width, 128), width // 4
-    blocks = [((down_rows, parts[m][1]), bf16) for m in (2, 1, 0)] + [((rows, half), bf16)] * 4
+    blocks = [((down_rows, parts[m][1]), bf16) for m in ORDER] + [((rows, half), bf16)] * 4
     blocks += [((rows, width), bf16), ((8, 128), f32)] + [((rows, width), bf16)] * 3
     blocks += [((rows, width - last), bf16), ((rows, last), bf16)]
     n = len(blocks)
     square, cube = (size, width), (8, 128, 128)
-    vmem, hbm = pl.BlockSpec(memory_space=pltpu.VMEM), pl.BlockSpec(memory_space=pltpu.HBM)
+    hbm = pl.BlockSpec(memory_space=pltpu.HBM)
     smem = pl.BlockSpec(memory_space=pltpu.SMEM)
     out = pl.pallas_call(
         backward_kernel,
         out_shape=[jax.ShapeDtypeStruct(b, f32) for b, _ in blocks]
         + [jax.ShapeDtypeStruct(square, bf16), jax.ShapeDtypeStruct(square, f32)],
-        in_specs=[smem] * 3 + [vmem] * 2 + [hbm] * (len(saved) + len(weights)),
-        out_specs=[vmem] * n + [hbm] * 2,
-        scratch_shapes=[pltpu.VMEM((4, 2, 2) + b, t) for b, t in blocks]
+        in_specs=[smem] * 3 + [hbm] * (2 + len(saved) + len(weights)),
+        out_specs=[hbm] * (n + 2),
+        scratch_shapes=[pltpu.VMEM(b, f32) for b, _ in blocks]
+        + [pltpu.VMEM(square, bf16)] * 2
+        + [pltpu.VMEM((4, 2, 2) + b, t) for b, t in blocks]
         + [pltpu.VMEM((19,) + b, t) for b, t in blocks]
         + [
             pltpu.VMEM((4, 2, 2, rows, half), bf16),
@@ -1172,7 +1222,8 @@
             pltpu.SemaphoreType.DMA((n, Scatter.NRECV)),
             pltpu.SemaphoreType.DMA((18,)),
             pltpu.SemaphoreType.DMA((18,)),
-            pltpu.SemaphoreType.DMA((40,)),
+            pltpu.SemaphoreType.DMA((48,)),
+            pltpu.SemaphoreType.DMA((n,)),
         ],
         compiler_params=pltpu.CompilerParams(
             collective_id=3, has_side_effects=True, vmem_limit_bytes=67000000
@@ -1182,43 +1233,62 @@
     return out[:n], out[n], out[n + 1]
 
 
-RESULTS = ((10,), (12, 13), (11,), (9,), (7,), (8,), (3, 4), (5, 6), (2, 1, 0))
-
-
-def deliver_kernel(result, inputs, *refs):
-    grads, out = refs[:14], refs[14:]
-    out[0][...] = result[...]
-    out[1][...] = inputs[...]
-    for dst, found in zip(out[2:], RESULTS):
-        if found == (8,):
+RESULTS = ((10,), (12, 13), (11,), (9,), (7,), (8,), (3, 4), (5, 6), (2, 0, 1))
+
+
+def deliver_kernel(*refs):
+    given, out, held, gain, own = refs[:16], refs[16:27], refs[27:38], refs[38], refs[39]
+    in_sem, out_sem = refs[40:]
+    sources = [(0,), (1,)] + [tuple(k + 2 for k in found) for found in RESULTS]
+    copies = []
+    for dst, found in zip(held, sources):
+        at, mine = 0, []
+        for k in found:
+            size = given[k].shape[1]
+            place = gain if k == 10 else dst.at[:, pl.ds(at, size)]
+            mine.append(pltpu.make_async_copy(given[k], place, in_sem.at[k]))
+            at += size
+        for copy in mine:
+            copy.start()
+        copies.append(mine)
+    made = []
+    for i, mine in enumerate(copies):
+        for copy in mine:
+            copy.wait()
+        src = held[i]
+        if i == 7:
             me = lax.axis_index(AXIS)
-            row = grads[8][pl.ds(me // 4, 1), :]
-            own = jnp.zeros((1, 32), jnp.float32)
+            row = gain[pl.ds(me // 4, 1), :]
+            found = jnp.zeros((1, 32), jnp.float32)
             for k in range(4):
-                own = own + jnp.where(lax.rem(me, 4) == k, 1.0, 0.0) * row[:, 32 * k : 32 * k + 32]
-            dst[...] = own
-        else:
-            at = 0
-            for k in found:
-                size = grads[k].shape[1]
-                dst[:, pl.ds(at, size)] = grads[k][...]
-                at += size
+                found = found + jnp.where(lax.rem(me, 4) == k, 1.0, 0.0) * row[:, 32 * k : 32 * k + 32]
+            own[...] = found
+            src = own
+        copy = pltpu.make_async_copy(src, out[i], out_sem.at[i])
+        copy.start()
+        made.append(copy)
+    for copy in made:
+        copy.wait()
 
 
 def deliver(result, inputs, grads):
     f32 = jnp.float32
     shapes = [(grads[k[0]].shape[0], sum(grads[i].shape[1] for i in k)) for k in RESULTS]
     shapes[5] = (1, 32)
-    vmem = pl.BlockSpec(memory_space=pltpu.VMEM)
+    shapes = [(result.shape, result.dtype), (inputs.shape, f32)] + [(s, f32) for s in shapes]
+    hbm = pl.BlockSpec(memory_space=pltpu.HBM)
     out = pl.pallas_call(
         deliver_kernel,
-        out_shape=[
-            jax.ShapeDtypeStruct(result.shape, result.dtype),
-            jax.ShapeDtypeStruct(inputs.shape, f32),
-        ]
-        + [jax.ShapeDtypeStruct(s, f32) for s in shapes],
-        in_specs=[vmem] * 16,
-        out_specs=[vmem] * 11,
+        out_shape=[jax.ShapeDtypeStruct(s, t) for s, t in shapes],
+        in_specs=[hbm] * 16,
+        out_specs=[hbm] * 11,
+        scratch_shapes=[pltpu.VMEM(s, t) for s, t in shapes]
+        + [
+            pltpu.VMEM((8, 128), f32),
+            pltpu.VMEM((1, 32), f32),
+            pltpu.SemaphoreType.DMA((16,)),
+            pltpu.SemaphoreType.DMA((11,)),
+        ],
         name="deliver",
     )(result, inputs, *grads)
     return (*out[:7], out[7].reshape(-1), *out[8:])

time: 252 us -> 249 us (0.988)
  Pallas kernels: 251 us -> 248 us
where the time goes in v6:
time: 249 us; the launch traced here: 248 us
  Pallas kernels  248 us (100%)
    pallas_call x1, Pallas kernels, forward(): pl.pallas_call(forward_kernel, out_shape=[jax.ShapeDtypeStruct((4, 2, 2,...  124 us
    pallas_call x1, Pallas kernels, backward(): pl.pallas_call(backward_kernel, out_shape=[jax.ShapeDtypeStruct(b, f32) f...  120 us

profile of v6, /device:TPU:0, one launch (start us, length us, event | category | flops | bytes accessed | tf_op | source)
XLA Modules:
  0.0 248.5 jit_solution(1793371634467393869)
XLA Ops:
  0.6 124.2 %forward.1 = (bf16[4,2,2,2,32,1024]{5,4,3,2,1,0:T(8,128)(2,1)}, bf16[4,2,2,2,32,1024]{5,4,3,2,1,0:T(8,128)(2,1)}, bf16[4,2,2,2,32,1024]{5,4,3,2,1,0:T(8,128)(2,1...) custom-call(s32[4]{0:T(128)} %lengths.3, s32[4]{0:T(128)} %order.3, ...), custom_call_target="tpu_custom_call" | custom-call | tf_op jit(solution)/shard_map/forward/pallas_call | solution.py:833
  124.9 120.2 %backward.1 = (f32[88,384]{1,0:T(8,128)}, f32[88,128]{1,0:T(8,128)}, f32[88,512]{1,0:T(8,128)}, f32[32,1408]{1,0:T(8,128)}, f32[32,1408]{1,0:T(8,128)}, /*index=...) custom-call(s32[4]{0:T(128)} %lengths.3, s32[4]{0:T(128)} %order.3, ...), custom_call_target="tpu_custom_call" | custom-call | tf_op jit(solution)/shard_map/backward/pallas_call | solution.py:1191
  245.1 3.2 %deliver.1 = (bf16[256,1024]{1,0:T(8,128)(2,1)}, f32[256,1024]{1,0:T(8,128)}, f32[32,1024]{1,0:T(8,128)}, f32[32,1024]{1,0:T(8,128)}, f32[32,1024]{1,0:T(8,128)}...) custom-call(bf16[256,1024]{1,0:T(8,128)(2,1)} %get-tuple-element.102, ...), custom_call_target="tpu_custom_call" | custom-call | tf_op jit(solution)/shard_map/deliver/pallas_call | solution.py:1280

commit v7 on v6

--- a/solution.py
+++ b/solution.py
@@ -423,6 +423,14 @@
     return value.astype(jnp.float32).reshape(-1, value.shape[-1]).astype(jnp.bfloat16)
 
 
+GATHERED = (2, 2, 2, 2)
+
+
+def gathered(width):
+    sizes = [width * part // 8 for part in GATHERED]
+    return [(sum(sizes[:i]), size) for i, size in enumerate(sizes)]
+
+
 SAVED_BACK = 20
 FIRST = 1
 ORDER = (FIRST, 2, 0)
@@ -581,20 +589,26 @@
     )
 
 
-def greet_more(place):
-    barrier = pltpu.get_barrier_semaphore()
+def greeted(place):
     r = lax.rem(place.me, 8)
     peers = [place.z * 8 + lax.bitwise_xor(r, k) for k in range(1, 8)]
-    peers += [lax.rem(place.z + k, 4) * 8 + r for k in range(1, 4)]
-    for peer in peers:
+    return peers + [lax.rem(place.z + k, 4) * 8 + r for k in range(1, 4)]
+
+
+def greet(place):
+    barrier = pltpu.get_barrier_semaphore()
+    for peer in greeted(place):
         pl.semaphore_signal(barrier, inc=1, device_id=peer, device_id_type=LOGICAL)
-    pl.semaphore_wait(barrier, len(peers))
+
+
+def met_all(place):
+    pl.semaphore_wait(pltpu.get_barrier_semaphore(), len(greeted(place)))
 
 
 def forward_kernel(lengths, order, rate, gain_own, *refs):
     inputs, refs = refs[:10], refs[10:]
     f32, bf16 = jnp.float32, jnp.bfloat16
-    n = 13
+    n = 10 + len(GATHERED)
     full, refs = refs[:n], refs[n:]
     saved, refs = refs[:SAVED_BACK], refs[SAVED_BACK:]
     kept, refs = refs[:SAVED_BACK], refs[SAVED_BACK:]
@@ -606,6 +620,8 @@
     (in_sem, first_send, first_recv, down_first), refs = refs[:4], refs[4:]
     (hidden, mixed, second, turned, gain_tile) = refs[:5]
     refs = refs[1:]
+    place = Place()
+    greet(place)
     fetched = [
         pltpu.make_async_copy(src, dst, in_sem.at[i])
         for i, (src, dst) in enumerate(zip(inputs, held))
@@ -615,19 +631,18 @@
     (dist, entry, leaving, gains, value) = refs[4:9]
     state_refs, arriving = refs[9:18], refs[16]
     (narrow, wide, send, recv, state_send, state_recv, load_sem, save_sem) = refs[18:]
-    place = Place()
     half = s_left.shape[1] // 2
     own = [s_key, s_value, s_query, s_unit, gain_tile, s_output]
     own += [s_left.at[:, pl.ds(0, half)], s_left.at[:, pl.ds(half, half)]]
     own += [s_right.at[:, pl.ds(0, half)], s_right.at[:, pl.ds(half, half)]]
     parts = parts_of(s_down.shape[1], 128)
-    own += [s_down.at[:, pl.ds(a, size)] for a, size in parts]
+    own += [s_down.at[:, pl.ds(a, size)] for a, size in gathered(s_down.shape[1])]
     lane = lax.broadcasted_iota(jnp.int32, gain_tile.shape, 1)
     line = lax.broadcasted_iota(jnp.int32, gain_tile.shape, 0)
     row = jnp.concatenate([gain_own[...].astype(f32)] * 4, axis=1)
     here = (lane // 32 == lax.rem(place.me, 4)) & (line == place.me // 4)
     gain_tile[...] = jnp.where(here, jnp.broadcast_to(row, gain_tile.shape), 0.0)
-    greet_more(place)
+    met_all(place)
     made = [Gather(place, own[i], full[i], send, recv, i) for i in range(n)]
     bounds = bounds_of(lengths, order)
     states = States(
@@ -818,7 +833,7 @@
     blocks = [(s.shape, s.dtype) for s in shards[:4]] + [((8, 128), f32)]
     blocks += [(shards[4].shape, bf16)] + [((32, half), bf16)] * 4
     parts = parts_of(width, 128)
-    blocks += [((shards[7].shape[0], p), bf16) for _, p in parts]
+    blocks += [((shards[7].shape[0], p), bf16) for _, p in gathered(width)]
     square, cube = (size, width), (8, 128, 128)
     rows, down_rows = shards[4].shape[0], shards[7].shape[0]
     across = ((4, 2, 2, 2, rows, size), bf16)
@@ -871,7 +886,7 @@
     (h_hidden, h_keys, h_values, h_queries, h_key_pre, h_query_pre, h_unit_pre, h_probs) = saved[:8]
     (h_attended, h_state_low, h_mixed, h_middle, h_second, h_left, h_right, h_product) = saved[8:16]
     h_gain, h_down = saved[16], saved[17:]
-    w_in, refs = refs[:12], refs[12:]
+    w_in, refs = refs[: 9 + len(GATHERED)], refs[9 + len(GATHERED) :]
     (w_key, w_value, w_query, w_unit, w_output, w_l0, w_l1, w_r0, w_r1) = w_in[:9]
     w_down = w_in[9:]
     sums, result_out, tokens_out, refs = refs[:n], refs[n], refs[n + 1], refs[n + 2 :]
@@ -889,7 +904,7 @@
     queries, keys = glp.at[:, pl.ds(0, width)], glp.at[:, pl.ds(width, width)]
     values, gqp = grp.at[:, pl.ds(0, width)], grp.at[:, pl.ds(width, width)]
     wn = wl.at[:, :, :, :, :, pl.ds(0, width)]
-    greet_more(place)
+    greet(place)
     bounds = bounds_of(lengths, order)
     states = States(
         place, bounds, rate, True, value, state_refs, state_send, state_recv
@@ -902,7 +917,7 @@
         copy.start()
 
     def load_down(i):
-        for m, (a, size) in enumerate(parts):
+        for m, (a, size) in enumerate(gathered(width)):
             dst = wd.at[:, :, :, :, :, pl.ds(a, size)]
             load("down%d%d" % (i, m), w_down[m].at[pl.ds(2 * i, 2)], dst)
 
@@ -974,7 +989,8 @@
         spans_of(place.me * SPAN, bounds, dist, entry, leaving)
 
     def gates(i):
-        loaded("down%d0" % i, "down%d1" % i, "down%d2" % i, "left%d" % i, "right%d" % i)
+        loaded(*["down%d%d" % (i, m) for m in range(len(GATHERED))])
+        loaded("left%d" % i, "right%d" % i)
         pair = 2 * wd.shape[4]
 
         @pl.loop(0, 8)
@@ -1108,7 +1124,7 @@
 
     before = {2: lambda: loaded("product", "cot"), 3: lambda: loaded("second"), 7: lambda: loaded("mixed")}
     before[9] = lambda: loaded("hidden")
-    tasks = {0: [begin], 2: [lambda: gates(0)], 3: [lambda: gates(1)]}
+    tasks = {0: [lambda: rest()], 2: [lambda: gates(0)], 3: [lambda: gates(1)]}
     tasks[4] = [lambda: second_part("l0", glp, 0, ("l1", w_l1, wl), True)]
     tasks[5] = [lambda: second_part("l1", glp, 1, ("r0", w_r0, wl), False)]
     tasks[6] = [
@@ -1125,22 +1141,29 @@
     tasks[10] = [last_grads]
     tasks[11] = [value_rest]
     tasks[12] = [inputs]
-    for i in range(3):
-        made[i].round(0)
+    made[0].round(0)
     load("product", h_product, product)
     load("cot", h_cot, cot)
     load_down(0)
     load("left0", h_left.at[:, side(0)], left)
     load("right0", h_right.at[:, side(0)], right)
-    load("middle", h_middle, f2)
-    load("second", h_second, rows)
-    load("l0", w_l0, wl)
-    load("mixed", h_mixed, mixed)
-    load("gain", h_gain, gain)
-    load("query_pre", h_query_pre, f4)
-    load("probs", h_probs, probs)
-    load("state_low", h_state_low, state_low)
-    load("input", h_tokens, tokens)
+    met_all(place)
+    made[1].round(0)
+    made[2].round(0)
+    made[0].round(1)
+
+    def rest():
+        load("middle", h_middle, f2)
+        load("second", h_second, rows)
+        load("l0", w_l0, wl)
+        load("mixed", h_mixed, mixed)
+        load("gain", h_gain, gain)
+        load("query_pre", h_query_pre, f4)
+        load("probs", h_probs, probs)
+        load("state_low", h_state_low, state_low)
+        load("input", h_tokens, tokens)
+        begin()
+
     def given(i):
         return pltpu.make_async_copy(out[i], sums[i], out_sem.at[i])
 
@@ -1152,7 +1175,7 @@
                 made[step - 1].handed()
             pieces[step][1].first()
             made[step].round(0)
-        if 0 < step <= n:
+        if 1 < step <= n:
             made[step - 1].round(1)
         for task in tasks.get(step, []):
             task()
@@ -1222,7 +1245,7 @@
             pltpu.SemaphoreType.DMA((n, Scatter.NRECV)),
             pltpu.SemaphoreType.DMA((18,)),
             pltpu.SemaphoreType.DMA((18,)),
-            pltpu.SemaphoreType.DMA((48,)),
+            pltpu.SemaphoreType.DMA((60,)),
             pltpu.SemaphoreType.DMA((n,)),
         ],
         compiler_params=pltpu.CompilerParams(

time: 249 us -> 248 us (level)
  no operation moved by 1% of the time
where the time goes in v7:
time: 248 us
  Pallas kernels  247 us (100%)
    pallas_call x1, Pallas kernels, forward(): pl.pallas_call(forward_kernel, out_shape=[jax.ShapeDtypeStruct((4, 2, 2,...  124 us
    pallas_call x1, Pallas kernels, backward(): pl.pallas_call(backward_kernel, out_shape=[jax.ShapeDtypeStruct(b, f32) f...  120 us

profile of v7, /device:TPU:0, one launch (start us, length us, event | category | flops | bytes accessed | tf_op | source)
XLA Modules:
  0.0 247.7 jit_solution(919468178318772718)
XLA Ops:
  0.6 124.0 %forward.1 = (bf16[4,2,2,2,32,1024]{5,4,3,2,1,0:T(8,128)(2,1)}, bf16[4,2,2,2,32,1024]{5,4,3,2,1,0:T(8,128)(2,1)}, bf16[4,2,2,2,32,1024]{5,4,3,2,1,0:T(8,128)(2,1...) custom-call(s32[4]{0:T(128)} %lengths.3, s32[4]{0:T(128)} %order.3, ...), custom_call_target="tpu_custom_call" | custom-call | tf_op jit(solution)/shard_map/forward/pallas_call | solution.py:848
  124.6 119.7 %backward.1 = (f32[88,384]{1,0:T(8,128)}, f32[88,128]{1,0:T(8,128)}, f32[88,512]{1,0:T(8,128)}, f32[32,1408]{1,0:T(8,128)}, f32[32,1408]{1,0:T(8,128)}, /*index=...) custom-call(s32[4]{0:T(128)} %lengths.3, s32[4]{0:T(128)} %order.3, ...), custom_call_target="tpu_custom_call" | custom-call | tf_op jit(solution)/shard_map/backward/pallas_call | solution.py:1214
  244.3 3.2 %deliver.1 = (bf16[256,1024]{1,0:T(8,128)(2,1)}, f32[256,1024]{1,0:T(8,128)}, f32[32,1024]{1,0:T(8,128)}, f32[32,1024]{1,0:T(8,128)}, f32[32,1024]{1,0:T(8,128)}...) custom-call(bf16[256,1024]{1,0:T(8,128)(2,1)} %get-tuple-element.104, ...), custom_call_target="tpu_custom_call" | custom-call | tf_op jit(solution)/shard_map/deliver/pallas_call | solution.py:1303
